TPU v7x, 128 devices: a whole 4x4x4 slice. The times are simulated.
128 devices in a mesh: pt: 8 (over z, core), comp: 16 (over x, y).
Axes of the slice: x: 4, y: 4, z: 4, core: 2. Of those that a mesh axis runs over, the one named last changes fastest.
Arguments:
- spectrum: float32 [512, 131072], P(None, ('pt', 'comp')), may hold values from 0.1 to 2
- wind: float32 [131072], P(('pt', 'comp')), may hold values from 0.5 to 4
- growth: float32 [512], replicated, may hold values from 0.05 to 0.5
- whitecap: float32 [512], replicated, may hold values from 0.1 to 1
- courant: float32 [16], replicated, may hold values from 0.2 to 0.7
- substeps: int32 [512], replicated, may hold values from 1 to 8, as said below
- limiter: int32 [131072], P(('pt', 'comp')), may hold values 0 or 1
- deck: int32 [131072], replicated, may hold values from 0 to 131071, as said below
- wet: int32 [256, 512], replicated, may hold values 0 or 1
Outputs:
- spectrum_out: float32 [512, 131072], P(None, ('pt', 'comp'))
- height: float32 [131072], P(('pt', 'comp'))
Inputs may be any that keep to these rules, and one draw needn't show every extreme that they name: Every component has 1 to 8 substeps, and some component has exactly 8. Each grid cell appears at exactly one deck slot. The deck is dealt in aligned runs of 128 slots: slots k * 128 .. k * 128 + 127 hold 128 consecutive cells, in order, starting at a multiple of 128.
All inputs are finite; a program needn't handle non-finite values. No bound on the sum of `limiter` on one device may be relied on, other than what follows from the above.
Results may differ from a plain program's by a relative error of at most 0.0003.
Values sent between devices are 32-bit elements; how exact they have to be, the bound alone decides.
A program may use at most 64 MiB of HBM per device.

v0:
```python
import math

import jax
import jax.numpy as jnp
from jax import lax
from jax.sharding import PartitionSpec as P

DIRS = 32
MAXSUB = 8
RUN = 128


rate_limit = 0.5
time_step = 0.5


def sources(spectrum, wind, growth, whitecap, limiter):
    mean_energy = jnp.mean(spectrum, axis=0)
    rate = (
        wind[None, :] * growth[:, None]
        - whitecap[:, None] * (mean_energy / (1.0 + mean_energy))[None, :]
    )
    rate = jnp.where(limiter[None, :] == 1, rate_limit * jnp.tanh(rate / rate_limit), rate)
    return spectrum * jnp.exp(time_step * rate)


def substep(field_grid, cross, along, wetness):
    sea = field_grid * wetness[None, :, :]
    east = jnp.roll(sea, 1, axis=2)
    west = jnp.roll(sea, -1, axis=2)
    up_column = jnp.where(along[:, None, None] > 0, east, west)
    zero_row = jnp.zeros_like(sea[:, :1, :])
    south = jnp.concatenate([zero_row, sea[:, :-1, :]], axis=1)
    north = jnp.concatenate([sea[:, 1:, :], zero_row], axis=1)
    up_row = jnp.where(cross[:, None, None] > 0, south, north)
    moved = (
        field_grid
        - jnp.abs(cross)[:, None, None] * (field_grid - up_row)
        - jnp.abs(along)[:, None, None] * (field_grid - up_column)
    )
    return jnp.where(wetness[None, :, :] > 0, moved, field_grid)


def on_device(spectrum, wind, growth, whitecap, courant, substeps, limiter, deck, wet):
    forced = sources(spectrum, wind, growth, whitecap, limiter)
    pt_count = lax.axis_size("pt")
    comp_count = lax.axis_size("comp")
    group_size = pt_count * comp_count
    total_comps = forced.shape[0]
    point_count = forced.shape[1]
    per_device = total_comps // group_size
    all_points = deck.shape[0]
    rows_grid = wet.shape[0]
    cols_grid = wet.shape[1]
    run_count = all_points // RUN
    positions = jnp.arange(total_comps, dtype=jnp.int32)
    received = lax.all_to_all(
        forced.reshape(per_device, group_size, point_count),
        ("pt", "comp"),
        split_axis=1,
        concat_axis=1,
        tiled=True,
    )
    fields = received.reshape(per_device, run_count, RUN)
    own_rank = lax.axis_index("pt") * comp_count + lax.axis_index("comp")
    comps = positions[jnp.arange(per_device, dtype=jnp.int32) * group_size + own_rank]
    angle = 2.0 * math.pi / DIRS * ((comps % DIRS).astype(jnp.float32) + 0.5)
    speed = courant[comps // DIRS]
    cross = speed * jnp.sin(angle)
    along = speed * jnp.cos(angle)
    counts = substeps[comps]
    wetness = wet.astype(jnp.float32)
    slot_runs = deck.reshape(run_count, RUN)[:, 0] // RUN
    run_ids = jnp.arange(run_count, dtype=jnp.int32)
    matches = slot_runs[None, :] == run_ids[:, None]
    cell_runs = jnp.sum(jnp.where(matches, run_ids[None, :], 0), axis=1)
    field_grid = jnp.take(fields, cell_runs, axis=1).reshape(per_device, rows_grid, cols_grid)
    for step in range(MAXSUB):
        field_grid = jnp.where(
            step < counts[:, None, None], substep(field_grid, cross, along, wetness), field_grid
        )
    slots = jnp.take(field_grid.reshape(per_device, run_count, RUN), slot_runs, axis=1).reshape(
        per_device, all_points
    )
    back = lax.all_to_all(
        slots.reshape(per_device, group_size, point_count),
        ("pt", "comp"),
        split_axis=1,
        concat_axis=1,
        tiled=True,
    )
    arrived = back.reshape(total_comps, point_count)
    height = 4.0 * jnp.sqrt(jnp.mean(arrived, axis=0) + 1e-06)
    return (arrived, height)


def solution(mesh):
    in_specs = (
        P(None, ("pt", "comp")),
        P(("pt", "comp")),
        P(),
        P(),
        P(),
        P(),
        P(("pt", "comp")),
        P(),
        P(),
    )
    out_specs = (P(None, ("pt", "comp")), P(("pt", "comp")))
    return jax.shard_map(
        on_device, mesh=mesh, in_specs=in_specs, out_specs=out_specs, check_vma=False
    )
```

profile of v0, /device:TPU:1, one launch (start us, length us, event | category | flops | bytes accessed | tf_op | source)
XLA Modules:
  0.0 139.6 jit_solution(12242542745949455757)
XLA Ops:
  0.6 0.0 copy-start
  0.6 0.0 copy-start.4
  0.7 0.0 copy-start.8
  0.7 0.8 broadcast_compare_fusion.1
  1.5 1.7 %reduce_sum.27 = f32[1024]{0:T(1024)S(1)} reduce(f32[512,1024]{1,0:T(8,128)} %param.11, f32[]{:T(128)} %constant.49.clone.1), dimensions={0}, to_apply=%region_0.0 | reduce | flops 523264 | bytes 2101252 | tf_op jit(solution)/shard_map/reduce_sum | solution.py:18
  3.3 0.8 exponential_multiply_fusion
  4.2 2.7 %copy.29 = f32[4,128,1024]{2,0,1:T(4,128)} copy(f32[4,128,1024]{2,1,0:T(8,128)S(1)} %bitcast.28) | data formatting | bytes 4194304 | tf_op jit(solution)/shard_map/reshape | solution.py:58
  6.8 11.5 %all-to-all-start = ((f32[4,128,1024]{2,0,1:T(4,128)}), f32[4,128,1024]{2,0,1:T(4,128)S(1)}, u32[]{:S(2)}, u32[]{:S(2)}) async-start(f32[4,128,1024]{2,0,1:T(4,128)} %copy.29), calls=%async_computation | async-start | bytes 4194304 | tf_op jit(solution)/shard_map/all_to_all | solution.py:57
  18.4 0.0 copy-start.2
  18.4 0.6 gather_fusion
  19.1 0.0 copy-done.6
  19.1 0.2 slice_reduce_fusion
  19.4 0.6 gather_fusion.2
  20.0 0.6 gather_fusion.1
  20.7 0.5 select_reduce_fusion
  21.2 0.1 broadcast_compare_fusion.3
  21.4 0.1 broadcast_compare_fusion
  21.5 26.6 %all-to-all-done = f32[4,128,1024]{2,0,1:T(4,128)S(1)} async-done(((f32[4,128,1024]{2,0,1:T(4,128)}), f32[4,128,1024]{2,0,1:T(4,128)S(1)}, u32[]{:S(2)}, u32[]{:S(2)}) %all-to-all-start) | async-done | bytes 2097184 | tf_op jit(solution)/shard_map/all_to_all | solution.py:57
  48.1 1.3 copy-done.3
  49.4 5.1 %gather_fusion.3 = f32[1024,4,128]{2,1,0:T(4,128)S(1)} fusion(f32[4,1024,128]{2,0,1:T(4,128)} %bitcast.26, s32[1024]{0:T(1024)S(1)} %fusion.26), kind=kCustom, calls=%fused_computation.clone | custom fusion | bytes 4198400 | tf_op jit(solution)/shard_map/jit(_take)/gather | solution.py:77
  54.6 3.7 %select_bitcast_fusion = f32[4,1024,128]{2,0,1:T(4,128)S(1)} fusion(f32[1024,4,128]{2,1,0:T(4,128)S(1)} %gather_fusion.3, pred[1024]{0:T(1024)(128)(4,1)S(1)} %compare_and_fusion.1), kind=kLoop, calls=%fused_computation.47 | loop fusion | flops 524288 | bytes 4195328 | tf_op jit(solution)/shard_map/jit(_take)/select_n | solution.py:77
  58.3 1.5 %copy.32 = f32[4,1024,128]{2,1,0:T(8,128)} copy(f32[4,1024,128]{2,0,1:T(4,128)S(1)} %select_bitcast_fusion) | data formatting | bytes 4194304 | tf_op jit(solution)/shard_map/jit(_take)/select_n | solution.py:77
  59.8 1.7 %reshape.230 = f32[4,256,512]{2,1,0:T(8,128)S(1)} reshape(f32[4,1024,128]{2,1,0:T(8,128)} %copy.32) | data formatting | bytes 4194304 | tf_op jit(solution)/shard_map/reshape | solution.py:77
  61.5 0.3 broadcast_multiply_fusion.7
  61.8 0.2 fusion.60
  62.0 0.8 fusion.61
  62.8 0.5 fusion.59
  63.3 1.8 %broadcast_multiply_fusion.6 = (f32[4,256,512]{2,1,0:T(8,128)S(1)}, f32[4,256,512]{2,1,0:T(8,128)S(1)}) fusion(f32[256,512]{1,0:T(8,128)S(1)} %convert_element_type.19, f32[4,256,512]{2,1,0:T(8,128)S(1)} %reshape.230, f32[4,256,1]{2,1,0:T(8,128)S(1)} %get-tuple-element.66, f32[4,256,511]{2,1,0:T(8,128)S(1)} %get-tuple-element.68, ...), kind=kLoop, calls=%fused_computation.56 | loop fusion | flops 6815744 | bytes 15319084 | tf_op jit(solution)/shard_map/mul | solution.py:28
  65.1 0.2 fusion.57
  65.3 0.7 fusion.58
  66.1 0.5 fusion.56
  66.5 1.8 %broadcast_multiply_fusion.5 = (f32[4,256,512]{2,1,0:T(8,128)S(1)}, f32[4,256,512]{2,1,0:T(8,128)S(1)}) fusion(f32[256,512]{1,0:T(8,128)S(1)} %convert_element_type.19, f32[4,256,512]{2,1,0:T(8,128)S(1)} %get-tuple-element.18, f32[4,256,1]{2,1,0:T(8,128)S(1)} %get-tuple-element.60, f32[4,256,511]{2,1,0:T(8,128)S(1)} %get-tuple-element.62, ...), kind=kLoop, calls=%fused_computation.55 | loop fusion | flops 6815744 | bytes 15319084 | tf_op jit(solution)/shard_map/mul | solution.py:28
  68.3 0.2 fusion.54
  68.5 0.7 fusion.55
  69.3 0.5 fusion.53
  69.8 1.8 %broadcast_multiply_fusion.4 = (f32[4,256,512]{2,1,0:T(8,128)S(1)}, f32[4,256,512]{2,1,0:T(8,128)S(1)}) fusion(f32[256,512]{1,0:T(8,128)S(1)} %convert_element_type.19, f32[4,256,512]{2,1,0:T(8,128)S(1)} %get-tuple-element.16, f32[4,256,1]{2,1,0:T(8,128)S(1)} %get-tuple-element.54, f32[4,256,511]{2,1,0:T(8,128)S(1)} %get-tuple-element.56, ...), kind=kLoop, calls=%fused_computation.54 | loop fusion | flops 6815744 | bytes 15319084 | tf_op jit(solution)/shard_map/mul | solution.py:28
  71.6 0.2 fusion.51
  71.8 0.7 fusion.52
  72.5 0.5 fusion.50
  73.0 2.0 %broadcast_multiply_fusion.3 = (f32[4,256,512]{2,1,0:T(8,128)S(1)}, f32[4,256,512]{2,1,0:T(8,128)S(1)}) fusion(f32[256,512]{1,0:T(8,128)S(1)} %convert_element_type.19, f32[4,256,512]{2,1,0:T(8,128)S(1)} %get-tuple-element.14, f32[4,256,1]{2,1,0:T(8,128)S(1)} %get-tuple-element.48, f32[4,256,511]{2,1,0:T(8,128)S(1)} %get-tuple-element.50, ...), kind=kLoop, calls=%fused_computation.53 | loop fusion | flops 6815744 | bytes 15319084 | tf_op jit(solution)/shard_map/mul | solution.py:28
  75.0 0.2 fusion.48
  75.2 0.7 fusion.49
  76.0 0.5 fusion.47
  76.5 1.8 %broadcast_multiply_fusion.2 = (f32[4,256,512]{2,1,0:T(8,128)S(1)}, f32[4,256,512]{2,1,0:T(8,128)S(1)}) fusion(f32[256,512]{1,0:T(8,128)S(1)} %convert_element_type.19, f32[4,256,512]{2,1,0:T(8,128)S(1)} %get-tuple-element.12, f32[4,256,1]{2,1,0:T(8,128)S(1)} %get-tuple-element.42, f32[4,256,511]{2,1,0:T(8,128)S(1)} %get-tuple-element.44, ...), kind=kLoop, calls=%fused_computation.52 | loop fusion | flops 6815744 | bytes 15319084 | tf_op jit(solution)/shard_map/mul | solution.py:28
  78.3 0.2 fusion.45
  78.5 0.7 fusion.46
  79.2 0.5 fusion.44
  79.7 1.8 %broadcast_multiply_fusion.1 = (f32[4,256,512]{2,1,0:T(8,128)S(1)}, f32[4,256,512]{2,1,0:T(8,128)S(1)}) fusion(f32[256,512]{1,0:T(8,128)S(1)} %convert_element_type.19, f32[4,256,512]{2,1,0:T(8,128)S(1)} %get-tuple-element.10, f32[4,256,1]{2,1,0:T(8,128)S(1)} %get-tuple-element.36, f32[4,256,511]{2,1,0:T(8,128)S(1)} %get-tuple-element.38, ...), kind=kLoop, calls=%fused_computation.51 | loop fusion | flops 6815744 | bytes 15319084 | tf_op jit(solution)/shard_map/mul | solution.py:28
  81.5 0.2 fusion.42
  81.7 0.7 fusion.43
  82.5 0.5 fusion.41
  82.9 1.8 %broadcast_multiply_fusion = (f32[4,256,512]{2,1,0:T(8,128)S(1)}, f32[4,256,512]{2,1,0:T(8,128)S(1)}) fusion(f32[256,512]{1,0:T(8,128)S(1)} %convert_element_type.19, f32[4,256,512]{2,1,0:T(8,128)S(1)} %get-tuple-element.8, f32[4,256,1]{2,1,0:T(8,128)S(1)} %get-tuple-element.30, f32[4,256,511]{2,1,0:T(8,128)S(1)} %get-tuple-element.32, ...), kind=kLoop, calls=%fused_computation.50 | loop fusion | flops 6815744 | bytes 15319084 | tf_op jit(solution)/shard_map/mul | solution.py:28
  84.7 0.2 fusion.40
  84.9 0.8 fusion.39
  85.7 0.5 fusion.38
  86.2 2.7 %select_select_fusion = f32[4,256,512]{2,1,0:T(8,128)} fusion(f32[4,256,512]{2,1,0:T(8,128)S(1)} %get-tuple-element.6, f32[4,256,511]{2,1,0:T(8,128)S(1)} %get-tuple-element.24, f32[4,256,1]{2,1,0:T(8,128)S(1)} %get-tuple-element.26, f32[4,256,1]{2,1,0:T(8,128)S(1)} %get-tuple-element.25, f32[4,256,511]{2,1,0:T(8,128)S(1)} %get-tuple-element.23, ...), kind=kLoop, calls=%fused_computation.7 | loop fusion | flops 6291456 | bytes 12697644 | tf_op jit(solution)/shard_map/jit(_where)/select_n | solution.py:79
  88.9 1.6 %reshape.231 = f32[4,1024,128]{2,1,0:T(8,128)S(1)} reshape(f32[4,256,512]{2,1,0:T(8,128)} %select_select_fusion) | data formatting | bytes 4194304 | tf_op jit(solution)/shard_map/reshape | solution.py:82
  90.5 2.7 %copy.33 = f32[4,1024,128]{2,0,1:T(4,128)} copy(f32[4,1024,128]{2,1,0:T(8,128)S(1)} %reshape.231) | data formatting | bytes 4194304 | tf_op jit(solution)/shard_map/reshape | solution.py:82
  93.2 5.1 %gather_fusion.4 = f32[1024,4,128]{2,1,0:T(4,128)S(1)} fusion(f32[4,1024,128]{2,0,1:T(4,128)} %copy.33, s32[1024]{0:T(1024)S(1)} %fusion.27), kind=kCustom, calls=%fused_computation.1.clone | custom fusion | bytes 4198400 | tf_op jit(solution)/shard_map/jit(_take)/gather | solution.py:82
  98.3 3.7 %broadcast_select_fusion = f32[1024,4,128]{2,1,0:T(4,128)S(1)} fusion(f32[1024,4,128]{2,1,0:T(4,128)S(1)} %gather_fusion.4, pred[1024]{0:T(1024)(128)(4,1)S(1)} %get-tuple-element.3), kind=kLoop, calls=%fused_computation.49 | loop fusion | flops 524288 | bytes 4195328 | tf_op jit(solution)/shard_map/jit(_take)/select_n | solution.py:82
  102.0 34.1 %all_to_all.10 = f32[4,128,1024]{2,0,1:T(4,128)S(1)} all-to-all(f32[4,128,1024]{2,0,1:T(4,128)S(1)} %bitcast.27), channel_id=1, replica_groups=mesh['pt'=8,'comp'=16] {'pt','comp'}, dimensions={1} | all-to-all | bytes 4194304 | tf_op jit(solution)/shard_map/all_to_all | solution.py:85
  136.1 0.4 reduce_sum.29
  136.5 0.6 sqrt_multiply_fusion
  137.1 2.5 %copy.36 = f32[4,128,1024]{2,1,0:T(8,128)} copy(f32[4,128,1024]{2,0,1:T(4,128)S(1)} %all_to_all.10) | data formatting | bytes 4194304 | tf_op jit(solution)/shard_map/all_to_all | solution.py:85
  (28 shorter events, 0.2 us)
Async XLA Ops:
  0.6 19.4 %copy-start = (s32[512]{0:T(512)S(1)}, s32[512]{0:T(512)}, u32[]{:S(2)}) copy-start(s32[512]{0:T(512)} %param.16) | copy-start | bytes 6148
  0.6 2.6 %copy-start.4 = (f32[512,1024]{1,0:T(8,128)S(1)}, f32[512,1024]{1,0:T(8,128)}, u32[]{:S(2)}) copy-start(f32[512,1024]{1,0:T(8,128)} %param.11) | copy-start | bytes 6291460
  0.7 2.6 %copy-start.8 = (f32[512]{0:T(512)S(1)}, f32[512]{0:T(512)}, u32[]{:S(2)}) copy-start(f32[512]{0:T(512)} %param.14) | copy-start | bytes 6148
  0.7 2.6 %copy-start.9 = (f32[512]{0:T(512)S(1)}, f32[512]{0:T(512)}, u32[]{:S(2)}) copy-start(f32[512]{0:T(512)} %param.13) | copy-start | bytes 6148
  0.7 2.6 %copy-start.7 = (f32[1024]{0:T(1024)S(1)}, f32[1024]{0:T(1024)}, u32[]{:S(2)}) copy-start(f32[1024]{0:T(1024)} %param.12) | copy-start | bytes 12292
  6.8 12.2 %copy-start.6 = (s32[131072]{0:T(1024)S(1)}, s32[131072]{0:T(1024)}, u32[]{:S(2)}) copy-start(s32[131072]{0:T(1024)} %param.18) | copy-start | bytes 1572868
  6.8 12.5 %copy-start.5 = (s32[256,512]{1,0:T(8,128)S(1)}, s32[256,512]{1,0:T(8,128)}, u32[]{:S(2)}) copy-start(s32[256,512]{1,0:T(8,128)} %param.19) | copy-start | bytes 1572868
  6.8 41.3 %all-to-all-start = ((f32[4,128,1024]{2,0,1:T(4,128)}), f32[4,128,1024]{2,0,1:T(4,128)S(1)}, u32[]{:S(2)}, u32[]{:S(2)}) async-start(f32[4,128,1024]{2,0,1:T(4,128)} %copy.29), calls=%async_computation | async-start | bytes 4194304 | tf_op jit(solution)/shard_map/all_to_all | solution.py:57
  18.4 1.0 copy-start.2
  48.1 1.3 copy-start.3
  136.5 3.1 %copy-start.1 = (s32[512]{0:T(512)S(1)}, s32[512]{0:T(512)}, u32[]{:S(2)}) copy-start(s32[512]{0:T(512)} %param.16) | copy-start | bytes 6148
where the time goes:
time: 140 us
  local copies, waits for them, and re-layouts  37.9 us (27%)
  blocking collectives  34.1 us (24%)
  other arithmetic  28.4 us (20%)
  waiting for transfers between devices  26.6 us (19%)
  starting transfers between devices  11.5 us (8%)
    all_to_all x1, blocking collectives, on_device(): lax.all_to_all(slots.reshape(per_device, group_size, point_count), ('pt',...  34.1 us
    all_to_all x1, waiting for transfers between devices, on_device(): lax.all_to_all(forced.reshape(per_device, group_size, point_count), ('pt'...  26.6 us
    mul x8, other arithmetic, substep(): sea = field_grid * wetness[None, :, :]  13 us
    all_to_all x1, starting transfers between devices, on_device(): lax.all_to_all(forced.reshape(per_device, group_size, point_count), ('pt'...  11.5 us
    slice x14, local copies, waits for them, and re-layouts, substep(): east = jnp.roll(sea, 1, axis=2)  6.66 us
    gather x1, local copies, waits for them, and re-layouts, on_device(): jnp.take(fields, cell_runs, axis=1)  5.13 us
    gather x1, local copies, waits for them, and re-layouts, on_device(): jnp.take(field_grid.reshape(per_device, run_count, RUN), slot_runs, axis=1)  5.13 us
    reshape x2, local copies, waits for them, and re-layouts, on_device(): field_grid.reshape(per_device, run_count, RUN)  4.29 us
  transfers between devices with their start and end apart: 1, of which 1 were waited for; matrix products, arithmetic and copies ran while one was open for 2% of the time, Pallas kernels for 0%

commit v1 on v0

v1 whole, which is shorter than its diff:
```python
import functools
import math

import jax
import jax.numpy as jnp
from jax import lax
from jax.experimental import pallas as pl
from jax.experimental.pallas import tpu as pltpu
from jax.sharding import PartitionSpec as P

DIRS = 32
MAXSUB = 8
RUN = 128
SUB = 8


rate_limit = 0.5
time_step = 0.5


def sources(spectrum, wind, growth, whitecap, limiter):
    mean_energy = jnp.mean(spectrum, axis=0)
    rate = (
        wind[None, :] * growth[:, None]
        - whitecap[:, None] * (mean_energy / (1.0 + mean_energy))[None, :]
    )
    rate = jnp.where(limiter[None, :] == 1, rate_limit * jnp.tanh(rate / rate_limit), rate)
    return spectrum * jnp.exp(time_step * rate)


def propagate_kernel(inv_ref, ax_ref, ay_ref, var_ref, cnt_ref, recv_ref, wet_ref, out_ref, buf_ref):
    comps = recv_ref.shape[0]
    slabs = wet_ref.shape[0]
    cols = wet_ref.shape[2]
    quarters = cols // RUN

    def copy_runs(c, to_grid, slot):
        def body(j, carry):
            for k in range(SUB):
                for q in range(quarters):
                    s = inv_ref[(k * slabs + j) * quarters + q]
                    lanes = slice(q * RUN, (q + 1) * RUN)
                    if to_grid:
                        buf_ref[slot, j, k:k + 1, lanes] = recv_ref[c, pl.ds(s, 1), :]
                    else:
                        out_ref[c, pl.ds(s, 1), :] = buf_ref[slot, j, k:k + 1, lanes]
            return carry

        lax.fori_loop(0, slabs, body, 0)

    def substep(src, dst, south, east, axc, ayc):
        sub_id = lax.broadcasted_iota(jnp.int32, (SUB, cols), 0)
        if south:
            edge = buf_ref[src, slabs - 1] * wet_ref[slabs - 1]
            init = jnp.where(sub_id == 0, 0.0, pltpu.roll(edge, 1, 0))
        else:
            edge = buf_ref[src, 0] * wet_ref[0]
            init = jnp.where(sub_id == SUB - 1, 0.0, pltpu.roll(edge, SUB - 1, 0))

        def body(i, up_row):
            j = i if south else slabs - 1 - i
            f = buf_ref[src, j]
            w = wet_ref[j]
            sea = f * w
            up_col = pltpu.roll(sea, 1 if east else cols - 1, 1)
            moved = f - axc * (f - up_row) - ayc * (f - up_col)
            buf_ref[dst, j] = jnp.where(w > 0, moved, f)
            return sea

        lax.fori_loop(0, slabs, body, init, unroll=2)

    def variant(south, east, c):
        axc = ax_ref[c]
        ayc = ay_ref[c]
        cnt = cnt_ref[c]
        for n in range(MAXSUB):
            @pl.when(n < cnt)
            def _():
                substep(n % 2, (n + 1) % 2, south, east, axc, ayc)

    def comp_body(c, carry):
        copy_runs(c, True, 0)
        v = var_ref[c]
        for vi, (south, east) in enumerate(((False, False), (False, True), (True, False), (True, True))):
            @pl.when(v == vi)
            def _():
                variant(south, east, c)
        fin = cnt_ref[c] % 2
        copy_runs_dyn(c, fin)
        return carry

    def copy_runs_dyn(c, slot):
        def body(j, carry):
            for k in range(SUB):
                for q in range(quarters):
                    s = inv_ref[(k * slabs + j) * quarters + q]
                    out_ref[c, pl.ds(s, 1), :] = buf_ref[slot, j, k:k + 1, q * RUN:(q + 1) * RUN]
            return carry

        lax.fori_loop(0, slabs, body, 0)

    lax.fori_loop(0, comps, comp_body, 0)


def propagate(inv, ax, ay, var, cnt, recv, wet_t):
    comps, nruns, _ = recv.shape
    slabs, _, cols = wet_t.shape
    smem = pl.BlockSpec(memory_space=pltpu.SMEM)
    vmem = pl.BlockSpec(memory_space=pltpu.VMEM)
    return pl.pallas_call(
        propagate_kernel,
        out_shape=jax.ShapeDtypeStruct(recv.shape, recv.dtype),
        in_specs=[smem] * 5 + [vmem] * 2,
        out_specs=vmem,
        scratch_shapes=[pltpu.VMEM((2, slabs, SUB, cols), jnp.float32)],
    )(inv, ax, ay, var, cnt, recv, wet_t)


def on_device(spectrum, wind, growth, whitecap, courant, substeps, limiter, deck, wet):
    forced = sources(spectrum, wind, growth, whitecap, limiter)
    pt_count = lax.axis_size("pt")
    comp_count = lax.axis_size("comp")
    group_size = pt_count * comp_count
    total_comps = forced.shape[0]
    point_count = forced.shape[1]
    per_device = total_comps // group_size
    all_points = deck.shape[0]
    rows_grid = wet.shape[0]
    cols_grid = wet.shape[1]
    run_count = all_points // RUN
    received = lax.all_to_all(
        forced.reshape(per_device, group_size, point_count),
        ("pt", "comp"),
        split_axis=1,
        concat_axis=1,
        tiled=True,
    )
    fields = received.reshape(per_device, run_count, RUN)
    own_rank = lax.axis_index("pt") * comp_count + lax.axis_index("comp")
    comps = jnp.arange(per_device, dtype=jnp.int32) * group_size + own_rank
    angle = 2.0 * math.pi / DIRS * ((comps % DIRS).astype(jnp.float32) + 0.5)
    speed = courant[comps // DIRS]
    cross = speed * jnp.sin(angle)
    along = speed * jnp.cos(angle)
    counts = substeps[comps]
    var = (cross > 0).astype(jnp.int32) * 2 + (along > 0).astype(jnp.int32)
    slabs = rows_grid // SUB
    wet_t = wet.astype(jnp.float32).reshape(SUB, slabs, cols_grid).transpose(1, 0, 2)
    slot_runs = deck.reshape(run_count, RUN)[:, 0] // RUN
    inv = jnp.zeros((run_count,), jnp.int32).at[slot_runs].set(jnp.arange(run_count, dtype=jnp.int32))
    slots = propagate(inv, jnp.abs(cross), jnp.abs(along), var, counts, fields, wet_t)
    back = lax.all_to_all(
        slots.reshape(per_device, group_size, point_count),
        ("pt", "comp"),
        split_axis=1,
        concat_axis=1,
        tiled=True,
    )
    arrived = back.reshape(total_comps, point_count)
    height = 4.0 * jnp.sqrt(jnp.mean(arrived, axis=0) + 1e-06)
    return (arrived, height)


def solution(mesh):
    in_specs = (
        P(None, ("pt", "comp")),
        P(("pt", "comp")),
        P(),
        P(),
        P(),
        P(),
        P(("pt", "comp")),
        P(),
        P(),
    )
    out_specs = (P(None, ("pt", "comp")), P(("pt", "comp")))
    return jax.shard_map(
        on_device, mesh=mesh, in_specs=in_specs, out_specs=out_specs, check_vma=False
    )
```

time: 140 us -> 173 us (1.24)
  Pallas kernels: 0 us -> 42.8 us
  blocking collectives: 34.1 us -> 70.2 us
  other arithmetic: 28.4 us -> 5.51 us
  local copies, waits for them, and re-layouts: 37.9 us -> 21.7 us
  waiting for transfers between devices: 26.6 us -> 20 us
    pallas_call x0 -> x1, Pallas kernels: none -> 42.8 us  [propagate(): pl.pallas_call(propagate_kernel, out_shape=jax.ShapeDtypeStruct(recv.shap...]
    all_to_all x1, blocking collectives: 34.1 us -> 70.2 us  [on_device(): lax.all_to_all(slots.reshape(per_device, group_size, point_count), ('pt',...]
    mul x8 -> x0, other arithmetic: 13 us -> none  [substep(): sea = field_grid * wetness[None, :, :]]
    slice x25 -> x0, local copies, waits for them, and re-layouts: 11.7 us -> none  [the longest x14 6.66 us: substep(): east = jnp.roll(sea, 1, axis=2)]
    gather x3 -> x0, local copies, waits for them, and re-layouts: 10.9 us -> none  [the longest x1 5.13 us: on_device(): jnp.take(fields, cell_runs, axis=1)]
    select_n x4 -> x1, other arithmetic: 10.1 us -> 0.44 us  [on_device(): jnp.zeros((run_count,), jnp.int32).at[slot_runs]]
    all_to_all x1, waiting for transfers between devices: 26.6 us -> 20 us  [on_device(): lax.all_to_all(forced.reshape(per_device, group_size, point_count), ('pt'...]
    scatter x0 -> x1, local copies, waits for them, and re-layouts: none -> 4.88 us  [on_device(): jnp.zeros((run_count,), jnp.int32).at[slot_runs]]
  transfers between devices with their start and end apart: 1 -> 1, of which waited for: 1 -> 1; matrix products, arithmetic and copies ran while one was open for 2% -> 6% of each run, Pallas kernels for 0% -> 0%
where the time goes in v1:
time: 173 us
  blocking collectives  70.2 us (41%)
  Pallas kernels  42.8 us (25%)
  local copies, waits for them, and re-layouts  21.7 us (13%)
  waiting for transfers between devices  20 us (12%)
  starting transfers between devices  11.5 us (7%)
  other arithmetic  5.51 us (3%)
    all_to_all x1, blocking collectives, on_device(): lax.all_to_all(slots.reshape(per_device, group_size, point_count), ('pt',...  70.2 us
    pallas_call x1, Pallas kernels, propagate(): pl.pallas_call(propagate_kernel, out_shape=jax.ShapeDtypeStruct(recv.shap...  42.8 us
    all_to_all x1, waiting for transfers between devices, on_device(): lax.all_to_all(forced.reshape(per_device, group_size, point_count), ('pt'...  20 us
    all_to_all x1, starting transfers between devices, on_device(): lax.all_to_all(forced.reshape(per_device, group_size, point_count), ('pt'...  11.5 us
    scatter x1, local copies, waits for them, and re-layouts, on_device(): jnp.zeros((run_count,), jnp.int32).at[slot_runs]  4.88 us
  transfers between devices with their start and end apart: 1, of which 1 were waited for; matrix products, arithmetic and copies ran while one was open for 6% of the time, Pallas kernels for 0%

profile of v1, /device:TPU:1, one launch (start us, length us, event | category | flops | bytes accessed | tf_op | source)
XLA Modules:
  0.0 172.6 jit_solution(4946189597239287210)
XLA Ops:
  0.6 0.0 copy-start
  0.6 0.0 copy-start.2
  0.7 0.0 copy-start.5
  0.7 0.0 copy-start.6
  0.7 0.0 copy-start.8
  0.7 0.0 copy-start.7
  0.7 1.9 %reduce_sum.18 = f32[1024]{0:T(1024)S(1)} reduce(f32[512,1024]{1,0:T(8,128)} %param.9, f32[]{:T(128)} %constant.77.clone.1), dimensions={0}, to_apply=%region_1.2 | reduce | flops 523264 | bytes 2101252 | tf_op jit(solution)/shard_map/reduce_sum | solution.py:22
  2.6 0.0 copy-done.5
  2.6 0.3 copy-done.2
  2.9 0.0 copy-done.6
  2.9 0.0 copy-done.8
  2.9 0.0 copy-done.7
  2.9 0.8 exponential_multiply_fusion
  3.7 2.7 %copy.16 = f32[4,128,1024]{2,0,1:T(4,128)} copy(f32[4,128,1024]{2,1,0:T(8,128)S(1)} %bitcast.11) | data formatting | bytes 4194304 | tf_op jit(solution)/shard_map/reshape | solution.py:132
  6.4 0.0 copy-start.3
  6.4 11.5 %all-to-all-start = ((f32[4,128,1024]{2,0,1:T(4,128)}), f32[4,128,1024]{2,0,1:T(4,128)S(1)}, u32[]{:S(2)}, u32[]{:S(2)}) async-start(f32[4,128,1024]{2,0,1:T(4,128)} %copy.16), calls=%async_computation | async-start | bytes 4194304 | tf_op jit(solution)/shard_map/all_to_all | solution.py:131
  17.9 0.0 copy-start.1
  17.9 0.0 copy-start.4
  18.0 0.0 copy-done.3
  18.0 1.1 copy.22
  19.1 0.0 copy-done.1
  19.1 0.6 gather_fusion
  19.8 0.0 copy-done
  19.8 1.2 gather_fusion.1
  21.0 0.0 copy-done.4
  21.0 0.4 fusion.1
  21.5 4.9 %scatter_custom_fusion.inv_ref = s32[1024]{0:T(1024)} fusion(s32[1024]{0:T(1024)S(1)} %fusion.1, s32[1024]{0:T(1024)S(1)} %iota.10, s32[]{:T(128)} %constant.61.clone.1), kind=kCustom, calls=%fused_computation.22 | custom fusion | bytes 4100 | tf_op jit(solution)/shard_map/scatter | solution.py:150
  26.3 0.6 fusion.9.var_ref
  27.0 0.7 fusion.13
  27.6 20.0 %all-to-all-done = f32[4,128,1024]{2,0,1:T(4,128)S(1)} async-done(((f32[4,128,1024]{2,0,1:T(4,128)}), f32[4,128,1024]{2,0,1:T(4,128)S(1)}, u32[]{:S(2)}, u32[]{:S(2)}) %all-to-all-start) | async-done | bytes 2097184 | tf_op jit(solution)/shard_map/all_to_all | solution.py:131
  47.7 2.5 %copy.17 = f32[4,128,1024]{2,1,0:T(8,128)} copy(f32[4,128,1024]{2,0,1:T(4,128)S(1)} %all-to-all-done) | data formatting | bytes 4194304 | tf_op jit(solution)/shard_map/all_to_all | solution.py:131
  50.2 2.7 %reshape.105.recv_ref = f32[4,1024,128]{2,1,0:T(8,128)} reshape(f32[4,128,1024]{2,1,0:T(8,128)} %copy.17) | data formatting | bytes 4194304 | tf_op jit(solution)/shard_map/reshape | solution.py:138
  52.9 42.8 %shard_map.104 = f32[4,1024,128]{2,1,0:T(8,128)} custom-call(s32[1024]{0:T(1024)} %scatter_custom_fusion.inv_ref, f32[4]{0:T(128)} %get-tuple-element.3.ax_ref, f32[4]{0:T(128)} %get-tuple-element.2.ay_ref, s32[4]{0:T(128)} %fusion.9.var_ref, s32[4]{0:T(128)} %gather_fusion.1, f32[4,1024,128]{2,1,0:T(8,128)} %reshape.105.recv_ref, f32[32,8,512]{2,1,0:T(8,128)} %bitcast.12), custom_call_target="tpu_custom_call" | custom-call | tf_op jit(solution)/shard_map/pallas_call | solution.py:110
  95.8 1.7 reshape.107
  97.5 1.4 copy.19
  98.9 70.2 %all_to_all.10 = f32[4,128,1024]{2,0,1:T(4,128)S(1)} all-to-all(f32[4,128,1024]{2,0,1:T(4,128)S(1)} %copy.19), channel_id=1, replica_groups=mesh['pt'=8,'comp'=16] {'pt','comp'}, dimensions={1} | all-to-all | bytes 4194304 | tf_op jit(solution)/shard_map/all_to_all | solution.py:152
  169.1 0.4 reduce_sum.19
  169.4 0.6 sqrt_multiply_fusion
  170.1 2.5 %copy.20 = f32[4,128,1024]{2,1,0:T(8,128)} copy(f32[4,128,1024]{2,0,1:T(4,128)S(1)} %all_to_all.10) | data formatting | bytes 4194304 | tf_op jit(solution)/shard_map/all_to_all | solution.py:152
  (7 shorter events, 0.1 us)
Async XLA Ops:
  0.6 19.2 %copy-start = (s32[512]{0:T(512)S(1)}, s32[512]{0:T(512)}, u32[]{:S(2)}) copy-start(s32[512]{0:T(512)} %param.14) | copy-start | bytes 6148
  0.6 2.2 %copy-start.2 = (f32[512,1024]{1,0:T(8,128)S(1)}, f32[512,1024]{1,0:T(8,128)}, u32[]{:S(2)}) copy-start(f32[512,1024]{1,0:T(8,128)} %param.9) | copy-start | bytes 6291460
  0.7 1.9 %copy-start.5 = (s32[1024]{0:T(1024)S(1)}, s32[1024]{0:T(1024)}, u32[]{:S(2)}) copy-start(s32[1024]{0:T(1024)} %param.15) | copy-start | bytes 12292
  0.7 2.2 %copy-start.6 = (f32[1024]{0:T(1024)S(1)}, f32[1024]{0:T(1024)}, u32[]{:S(2)}) copy-start(f32[1024]{0:T(1024)} %param.10) | copy-start | bytes 12292
  0.7 2.2 %copy-start.8 = (f32[512]{0:T(512)S(1)}, f32[512]{0:T(512)}, u32[]{:S(2)}) copy-start(f32[512]{0:T(512)} %param.11) | copy-start | bytes 6148
  0.7 2.2 %copy-start.7 = (f32[512]{0:T(512)S(1)}, f32[512]{0:T(512)}, u32[]{:S(2)}) copy-start(f32[512]{0:T(512)} %param.12) | copy-start | bytes 6148
  6.4 11.5 %copy-start.3 = (s32[256,512]{1,0:T(8,128)S(1)}, s32[256,512]{1,0:T(8,128)}, u32[]{:S(2)}) copy-start(s32[256,512]{1,0:T(8,128)} %param.17) | copy-start | bytes 1572868
  6.4 41.3 %all-to-all-start = ((f32[4,128,1024]{2,0,1:T(4,128)}), f32[4,128,1024]{2,0,1:T(4,128)S(1)}, u32[]{:S(2)}, u32[]{:S(2)}) async-start(f32[4,128,1024]{2,0,1:T(4,128)} %copy.16), calls=%async_computation | async-start | bytes 4194304 | tf_op jit(solution)/shard_map/all_to_all | solution.py:131
  17.9 1.2 copy-start.1
  17.9 3.1 %copy-start.4 = (s32[131072]{0:T(1024)S(1)}, s32[131072]{0:T(1024)}, u32[]{:S(2)}) copy-start(s32[131072]{0:T(1024)} %param.16) | copy-start | bytes 1572868

commit v2 on v1

--- a/solution.py
+++ b/solution.py
@@ -67,7 +67,7 @@
             buf_ref[dst, j] = jnp.where(w > 0, moved, f)
             return sea
 
-        lax.fori_loop(0, slabs, body, init, unroll=2)
+        lax.fori_loop(0, slabs, body, init, unroll=True)
 
     def variant(south, east, c):
         axc = ax_ref[c]

time: 173 us -> 113 us (0.65)
  blocking collectives: 70.2 us -> 36.7 us
  Pallas kernels: 42.8 us -> 16.6 us
    all_to_all x1, blocking collectives: 70.2 us -> 36.7 us  [on_device(): lax.all_to_all(slots.reshape(per_device, group_size, point_count), ('pt',...]
    pallas_call x1, Pallas kernels: 42.8 us -> 16.6 us  [propagate(): pl.pallas_call(propagate_kernel, out_shape=jax.ShapeDtypeStruct(recv.shap...]
  transfers between devices with their start and end apart: 1 -> 1, of which waited for: 1 -> 1; matrix products, arithmetic and copies ran while one was open for 6% -> 9% of each run, Pallas kernels for 0% -> 0%
where the time goes in v2:
time: 113 us
  blocking collectives  36.7 us (32%)
  local copies, waits for them, and re-layouts  21.7 us (19%)
  waiting for transfers between devices  20 us (18%)
  Pallas kernels  16.6 us (15%)
  starting transfers between devices  11.5 us (10%)
  other arithmetic  5.51 us (5%)
    all_to_all x1, blocking collectives, on_device(): lax.all_to_all(slots.reshape(per_device, group_size, point_count), ('pt',...  36.7 us
    all_to_all x1, waiting for transfers between devices, on_device(): lax.all_to_all(forced.reshape(per_device, group_size, point_count), ('pt'...  20 us
    pallas_call x1, Pallas kernels, propagate(): pl.pallas_call(propagate_kernel, out_shape=jax.ShapeDtypeStruct(recv.shap...  16.6 us
    all_to_all x1, starting transfers between devices, on_device(): lax.all_to_all(forced.reshape(per_device, group_size, point_count), ('pt'...  11.5 us
    scatter x1, local copies, waits for them, and re-layouts, on_device(): jnp.zeros((run_count,), jnp.int32).at[slot_runs]  4.88 us
    reshape x2, local copies, waits for them, and re-layouts, on_device(): slots.reshape(per_device, group_size, point_count)  3.07 us
    reshape x1, local copies, waits for them, and re-layouts, on_device(): fields = received.reshape(per_device, run_count, RUN)  2.72 us
    reshape x1, local copies, waits for them, and re-layouts, on_device(): forced.reshape(per_device, group_size, point_count)  2.67 us
  transfers between devices with their start and end apart: 1, of which 1 were waited for; matrix products, arithmetic and copies ran while one was open for 9% of the time, Pallas kernels for 0%

profile of v2, /device:TPU:1, one launch (start us, length us, event | category | flops | bytes accessed | tf_op | source)
XLA Modules:
  0.0 112.8 jit_solution(13016357868764066040)
XLA Ops:
  0.6 0.0 copy-start
  0.6 0.0 copy-start.2
  0.7 0.0 copy-start.5
  0.7 0.0 copy-start.6
  0.7 0.0 copy-start.8
  0.7 0.0 copy-start.7
  0.7 1.9 %reduce_sum.18 = f32[1024]{0:T(1024)S(1)} reduce(f32[512,1024]{1,0:T(8,128)} %param.9, f32[]{:T(128)} %constant.77.clone.1), dimensions={0}, to_apply=%region_1.2 | reduce | flops 523264 | bytes 2101252 | tf_op jit(solution)/shard_map/reduce_sum | solution.py:22
  2.6 0.0 copy-done.5
  2.6 0.3 copy-done.2
  2.9 0.0 copy-done.6
  2.9 0.0 copy-done.8
  2.9 0.0 copy-done.7
  2.9 0.8 exponential_multiply_fusion
  3.7 2.7 %copy.16 = f32[4,128,1024]{2,0,1:T(4,128)} copy(f32[4,128,1024]{2,1,0:T(8,128)S(1)} %bitcast.11) | data formatting | bytes 4194304 | tf_op jit(solution)/shard_map/reshape | solution.py:132
  6.4 0.0 copy-start.3
  6.4 11.5 %all-to-all-start = ((f32[4,128,1024]{2,0,1:T(4,128)}), f32[4,128,1024]{2,0,1:T(4,128)S(1)}, u32[]{:S(2)}, u32[]{:S(2)}) async-start(f32[4,128,1024]{2,0,1:T(4,128)} %copy.16), calls=%async_computation | async-start | bytes 4194304 | tf_op jit(solution)/shard_map/all_to_all | solution.py:131
  17.9 0.0 copy-start.1
  17.9 0.0 copy-start.4
  18.0 0.0 copy-done.3
  18.0 1.1 copy.22
  19.1 0.0 copy-done.1
  19.1 0.6 gather_fusion
  19.8 0.0 copy-done
  19.8 1.2 %gather_fusion.1 = s32[4]{0:T(128)} fusion(s32[512]{0:T(512)S(1)} %copy-done, s32[1024]{0:T(1024)S(1)} %pad_clamp_fusion), kind=kCustom, calls=%fused_computation.1 | custom fusion | bytes 48 | tf_op jit(solution)/shard_map/gather | solution.py:145
  21.0 0.0 copy-done.4
  21.0 0.4 fusion.1
  21.5 4.9 %scatter_custom_fusion.inv_ref = s32[1024]{0:T(1024)} fusion(s32[1024]{0:T(1024)S(1)} %fusion.1, s32[1024]{0:T(1024)S(1)} %iota.10, s32[]{:T(128)} %constant.61.clone.1), kind=kCustom, calls=%fused_computation.22 | custom fusion | bytes 4100 | tf_op jit(solution)/shard_map/scatter | solution.py:150
  26.3 0.6 fusion.9.var_ref
  27.0 0.7 fusion.13
  27.6 20.0 %all-to-all-done = f32[4,128,1024]{2,0,1:T(4,128)S(1)} async-done(((f32[4,128,1024]{2,0,1:T(4,128)}), f32[4,128,1024]{2,0,1:T(4,128)S(1)}, u32[]{:S(2)}, u32[]{:S(2)}) %all-to-all-start) | async-done | bytes 2097184 | tf_op jit(solution)/shard_map/all_to_all | solution.py:131
  47.7 2.5 %copy.17 = f32[4,128,1024]{2,1,0:T(8,128)} copy(f32[4,128,1024]{2,0,1:T(4,128)S(1)} %all-to-all-done) | data formatting | bytes 4194304 | tf_op jit(solution)/shard_map/all_to_all | solution.py:131
  50.2 2.7 %reshape.105.recv_ref = f32[4,1024,128]{2,1,0:T(8,128)} reshape(f32[4,128,1024]{2,1,0:T(8,128)} %copy.17) | data formatting | bytes 4194304 | tf_op jit(solution)/shard_map/reshape | solution.py:138
  52.9 16.6 %shard_map.104 = f32[4,1024,128]{2,1,0:T(8,128)} custom-call(s32[1024]{0:T(1024)} %scatter_custom_fusion.inv_ref, f32[4]{0:T(128)} %get-tuple-element.3.ax_ref, f32[4]{0:T(128)} %get-tuple-element.2.ay_ref, s32[4]{0:T(128)} %fusion.9.var_ref, s32[4]{0:T(128)} %gather_fusion.1, f32[4,1024,128]{2,1,0:T(8,128)} %reshape.105.recv_ref, f32[32,8,512]{2,1,0:T(8,128)} %bitcast.12), custom_call_target="tpu_custom_call" | custom-call | tf_op jit(solution)/shard_map/pallas_call | solution.py:110
  69.5 1.7 %reshape.107 = f32[4,128,1024]{2,1,0:T(8,128)S(1)} reshape(f32[4,1024,128]{2,1,0:T(8,128)} %shard_map.104) | data formatting | bytes 4194304 | tf_op jit(solution)/shard_map/reshape | solution.py:153
  71.3 1.4 %copy.19 = f32[4,128,1024]{2,0,1:T(4,128)S(1)} copy(f32[4,128,1024]{2,1,0:T(8,128)S(1)} %reshape.107) | data formatting | bytes 4194304 | tf_op jit(solution)/shard_map/reshape | solution.py:153
  72.6 36.7 %all_to_all.10 = f32[4,128,1024]{2,0,1:T(4,128)S(1)} all-to-all(f32[4,128,1024]{2,0,1:T(4,128)S(1)} %copy.19), channel_id=1, replica_groups=mesh['pt'=8,'comp'=16] {'pt','comp'}, dimensions={1} | all-to-all | bytes 4194304 | tf_op jit(solution)/shard_map/all_to_all | solution.py:152
  109.3 0.4 reduce_sum.19
  109.7 0.6 sqrt_multiply_fusion
  110.3 2.5 %copy.20 = f32[4,128,1024]{2,1,0:T(8,128)} copy(f32[4,128,1024]{2,0,1:T(4,128)S(1)} %all_to_all.10) | data formatting | bytes 4194304 | tf_op jit(solution)/shard_map/all_to_all | solution.py:152
  (7 shorter events, 0.1 us)
Async XLA Ops:
  0.6 19.2 %copy-start = (s32[512]{0:T(512)S(1)}, s32[512]{0:T(512)}, u32[]{:S(2)}) copy-start(s32[512]{0:T(512)} %param.14) | copy-start | bytes 6148
  0.6 2.2 %copy-start.2 = (f32[512,1024]{1,0:T(8,128)S(1)}, f32[512,1024]{1,0:T(8,128)}, u32[]{:S(2)}) copy-start(f32[512,1024]{1,0:T(8,128)} %param.9) | copy-start | bytes 6291460
  0.7 1.9 %copy-start.5 = (s32[1024]{0:T(1024)S(1)}, s32[1024]{0:T(1024)}, u32[]{:S(2)}) copy-start(s32[1024]{0:T(1024)} %param.15) | copy-start | bytes 12292
  0.7 2.2 %copy-start.6 = (f32[1024]{0:T(1024)S(1)}, f32[1024]{0:T(1024)}, u32[]{:S(2)}) copy-start(f32[1024]{0:T(1024)} %param.10) | copy-start | bytes 12292
  0.7 2.2 %copy-start.8 = (f32[512]{0:T(512)S(1)}, f32[512]{0:T(512)}, u32[]{:S(2)}) copy-start(f32[512]{0:T(512)} %param.11) | copy-start | bytes 6148
  0.7 2.2 %copy-start.7 = (f32[512]{0:T(512)S(1)}, f32[512]{0:T(512)}, u32[]{:S(2)}) copy-start(f32[512]{0:T(512)} %param.12) | copy-start | bytes 6148
  6.4 11.5 %copy-start.3 = (s32[256,512]{1,0:T(8,128)S(1)}, s32[256,512]{1,0:T(8,128)}, u32[]{:S(2)}) copy-start(s32[256,512]{1,0:T(8,128)} %param.17) | copy-start | bytes 1572868
  6.4 41.3 %all-to-all-start = ((f32[4,128,1024]{2,0,1:T(4,128)}), f32[4,128,1024]{2,0,1:T(4,128)S(1)}, u32[]{:S(2)}, u32[]{:S(2)}) async-start(f32[4,128,1024]{2,0,1:T(4,128)} %copy.16), calls=%async_computation | async-start | bytes 4194304 | tf_op jit(solution)/shard_map/all_to_all | solution.py:131
  17.9 1.2 %copy-start.1 = (f32[16]{0:T(128)S(1)}, f32[16]{0:T(128)}, u32[]{:S(2)}) copy-start(f32[16]{0:T(128)} %param.13) | copy-start | bytes 196
  17.9 3.1 %copy-start.4 = (s32[131072]{0:T(1024)S(1)}, s32[131072]{0:T(1024)}, u32[]{:S(2)}) copy-start(s32[131072]{0:T(1024)} %param.16) | copy-start | bytes 1572868

commit v3 on v2

v3 whole, which is shorter than its diff:
```python
import functools
import math

import jax
import jax.numpy as jnp
from jax import lax
from jax.experimental import pallas as pl
from jax.experimental.pallas import tpu as pltpu
from jax.sharding import PartitionSpec as P

DIRS = 32
MAXSUB = 8
RUN = 128
SUB = 8


rate_limit = 0.5
time_step = 0.5


def sources(spectrum, wind, growth, whitecap, limiter):
    mean_energy = jnp.mean(spectrum, axis=0)
    rate = (
        wind[None, :] * growth[:, None]
        - whitecap[:, None] * (mean_energy / (1.0 + mean_energy))[None, :]
    )
    rate = jnp.where(limiter[None, :] == 1, rate_limit * jnp.tanh(rate / rate_limit), rate)
    return spectrum * jnp.exp(time_step * rate)


def propagate_kernel(inv_ref, ax_ref, ay_ref, var_ref, cnt_ref, recv_ref, wet_ref, out_ref, buf_ref):
    comps = recv_ref.shape[1]
    runs_per_dev = recv_ref.shape[2] // RUN
    slabs = wet_ref.shape[0]
    cols = wet_ref.shape[2]
    quarters = cols // RUN

    def copy_runs(c, to_grid):
        slot = 0 if to_grid else cnt_ref[c] % 2

        def body(j, carry):
            for k in range(SUB):
                for q in range(quarters):
                    s = inv_ref[(k * slabs + j) * quarters + q]
                    src = s // runs_per_dev
                    off = pl.multiple_of((s % runs_per_dev) * RUN, RUN)
                    lanes = slice(q * RUN, (q + 1) * RUN)
                    if to_grid:
                        buf_ref[c, slot, j, k:k + 1, lanes] = recv_ref[src, c:c + 1, pl.ds(off, RUN)]
                    else:
                        out_ref[src, c:c + 1, pl.ds(off, RUN)] = buf_ref[c, slot, j, k:k + 1, lanes]
            return carry

        lax.fori_loop(0, slabs, body, 0)

    def substep(c, src, dst, south, east, axc, ayc):
        sub_id = lax.broadcasted_iota(jnp.int32, (SUB, cols), 0)
        if south:
            edge = buf_ref[c, src, slabs - 1] * wet_ref[slabs - 1]
            init = jnp.where(sub_id == 0, 0.0, pltpu.roll(edge, 1, 0))
        else:
            edge = buf_ref[c, src, 0] * wet_ref[0]
            init = jnp.where(sub_id == SUB - 1, 0.0, pltpu.roll(edge, SUB - 1, 0))

        def body(i, up_row):
            j = i if south else slabs - 1 - i
            f = buf_ref[c, src, j]
            w = wet_ref[j]
            sea = f * w
            up_col = pltpu.roll(sea, 1 if east else cols - 1, 1)
            moved = f - axc * (f - up_row) - ayc * (f - up_col)
            buf_ref[c, dst, j] = jnp.where(w > 0, moved, f)
            return sea

        lax.fori_loop(0, slabs, body, init, unroll=True)

    def variant(south, east, c):
        axc = ax_ref[c]
        ayc = ay_ref[c]
        cnt = cnt_ref[c]
        for n in range(MAXSUB):
            @pl.when(n < cnt)
            def _():
                substep(c, n % 2, (n + 1) % 2, south, east, axc, ayc)

    def comp_body(c, carry):
        v = var_ref[c]
        for vi, (south, east) in enumerate(((False, False), (False, True), (True, False), (True, True))):
            @pl.when(v == vi)
            def _():
                variant(south, east, c)
        return carry

    for c in range(comps):
        copy_runs(c, True)
    lax.fori_loop(0, comps, comp_body, 0)
    for c in range(comps):
        copy_runs(c, False)


def propagate(inv, ax, ay, var, cnt, recv, wet_t):
    slabs, _, cols = wet_t.shape
    smem = pl.BlockSpec(memory_space=pltpu.SMEM)
    vmem = pl.BlockSpec(memory_space=pltpu.VMEM)
    return pl.pallas_call(
        propagate_kernel,
        out_shape=jax.ShapeDtypeStruct(recv.shape, recv.dtype),
        in_specs=[smem] * 5 + [vmem] * 2,
        out_specs=vmem,
        scratch_shapes=[pltpu.VMEM((recv.shape[1], 2, slabs, SUB, cols), jnp.float32)],
    )(inv, ax, ay, var, cnt, recv, wet_t)


def on_device(spectrum, wind, growth, whitecap, courant, substeps, limiter, deck, wet):
    forced = sources(spectrum, wind, growth, whitecap, limiter)
    pt_count = lax.axis_size("pt")
    comp_count = lax.axis_size("comp")
    group_size = pt_count * comp_count
    total_comps = forced.shape[0]
    point_count = forced.shape[1]
    per_device = total_comps // group_size
    all_points = deck.shape[0]
    rows_grid = wet.shape[0]
    cols_grid = wet.shape[1]
    run_count = all_points // RUN
    fields = lax.all_to_all(
        forced.reshape(group_size, per_device, point_count),
        ("pt", "comp"),
        split_axis=0,
        concat_axis=0,
        tiled=True,
    )
    own_rank = lax.axis_index("pt") * comp_count + lax.axis_index("comp")
    comps = own_rank * per_device + jnp.arange(per_device, dtype=jnp.int32)
    angle = 2.0 * math.pi / DIRS * ((comps % DIRS).astype(jnp.float32) + 0.5)
    speed = courant[comps // DIRS]
    cross = speed * jnp.sin(angle)
    along = speed * jnp.cos(angle)
    counts = substeps[comps]
    var = (cross > 0).astype(jnp.int32) * 2 + (along > 0).astype(jnp.int32)
    slabs = rows_grid // SUB
    wet_t = wet.astype(jnp.float32).reshape(SUB, slabs, cols_grid).transpose(1, 0, 2)
    slot_runs = deck.reshape(run_count, RUN)[:, 0] // RUN
    run_ids = jnp.arange(run_count, dtype=jnp.int32)
    inv = jnp.sum(jnp.where(slot_runs[None, :] == run_ids[:, None], run_ids[None, :], 0), axis=1)
    slots = propagate(inv, jnp.abs(cross), jnp.abs(along), var, counts, fields, wet_t)
    back = lax.all_to_all(slots, ("pt", "comp"), split_axis=0, concat_axis=0, tiled=True)
    arrived = back.reshape(total_comps, point_count)
    height = 4.0 * jnp.sqrt(jnp.mean(arrived, axis=0) + 1e-06)
    return (arrived, height)


def solution(mesh):
    in_specs = (
        P(None, ("pt", "comp")),
        P(("pt", "comp")),
        P(),
        P(),
        P(),
        P(),
        P(("pt", "comp")),
        P(),
        P(),
    )
    out_specs = (P(None, ("pt", "comp")), P(("pt", "comp")))
    return jax.shard_map(
        on_device, mesh=mesh, in_specs=in_specs, out_specs=out_specs, check_vma=False
    )
```

time: 113 us -> 160 us (1.42)
  Pallas kernels: 16.6 us -> 71.9 us
  local copies, waits for them, and re-layouts: 21.7 us -> 9.35 us
  waiting for transfers between devices: 20 us -> 24.1 us
  blocking collectives: 36.7 us -> 34.1 us
  other arithmetic: 5.51 us -> 7.5 us
    pallas_call x1, Pallas kernels: 16.6 us -> 71.9 us  [propagate(): pl.pallas_call(propagate_kernel, out_shape=jax.ShapeDtypeStruct(recv.shap...]
    all_to_all x2 -> x0, local copies, waits for them, and re-layouts: 5.07 us -> none  [the longest x1 2.54 us: on_device(): lax.all_to_all(forced.reshape(per_device, group_size, point_count), ('pt'...]
    scatter x1 -> x0, local copies, waits for them, and re-layouts: 4.88 us -> none  [on_device(): jnp.zeros((run_count,), jnp.int32).at[slot_runs]]
    all_to_all x1, waiting for transfers between devices: 20 us -> 24.1 us  [on_device(): lax.all_to_all(forced.reshape(group_size, per_device, point_count), ('pt'...]
    reshape x4 -> x2, local copies, waits for them, and re-layouts: 8.46 us -> 4.56 us  [the longest x1 2.87 us: on_device(): forced.reshape(group_size, per_device, point_count)]
    all_to_all x1, blocking collectives: 36.7 us -> 34.1 us  [on_device(): lax.all_to_all(slots, ('pt', 'comp'), split_axis=0, concat_axis=0, tiled=...]
  transfers between devices with their start and end apart: 1 -> 1, of which waited for: 1 -> 1; matrix products, arithmetic and copies ran while one was open for 9% -> 4% of each run, Pallas kernels for 0% -> 0%
where the time goes in v3:
time: 160 us; the launch traced here: 159 us
  Pallas kernels  71.9 us (45%)
  blocking collectives  34.1 us (21%)
  waiting for transfers between devices  24.1 us (15%)
  starting transfers between devices  11.5 us (7%)
  local copies, waits for them, and re-layouts  9.35 us (6%)
  other arithmetic  7.5 us (5%)
    pallas_call x1, Pallas kernels, propagate(): pl.pallas_call(propagate_kernel, out_shape=jax.ShapeDtypeStruct(recv.shap...  71.9 us
    all_to_all x1, blocking collectives, on_device(): lax.all_to_all(slots, ('pt', 'comp'), split_axis=0, concat_axis=0, tiled=...  34.1 us
    all_to_all x1, waiting for transfers between devices, on_device(): lax.all_to_all(forced.reshape(group_size, per_device, point_count), ('pt'...  24.1 us
    all_to_all x1, starting transfers between devices, on_device(): lax.all_to_all(forced.reshape(group_size, per_device, point_count), ('pt'...  11.5 us
  transfers between devices with their start and end apart: 1, of which 1 were waited for; matrix products, arithmetic and copies ran while one was open for 4% of the time, Pallas kernels for 0%

profile of v3, /device:TPU:1, one launch (start us, length us, event | category | flops | bytes accessed | tf_op | source)
XLA Modules:
  0.0 159.2 jit_solution(3013039916073242846)
XLA Ops:
  0.6 0.0 copy-start
  0.6 0.0 copy-start.3
  0.7 0.0 copy-start.6
  0.7 0.0 copy-start.7
  0.7 0.0 copy-start.9
  0.7 0.0 copy-start.8
  0.7 1.9 %reduce_sum.28 = f32[1024]{0:T(1024)S(1)} reduce(f32[512,1024]{1,0:T(8,128)} %param.9, f32[]{:T(128)} %constant.75.clone.1), dimensions={0}, to_apply=%region_1.2 | reduce | flops 523264 | bytes 2101252 | tf_op jit(solution)/shard_map/reduce_sum | solution.py:22
  2.6 0.0 copy-done.6
  2.6 0.3 copy-done.3
  2.9 0.0 copy-done.7
  2.9 0.0 copy-done.9
  2.9 0.0 copy-done.8
  2.9 2.2 %exponential_multiply_fusion = f32[512,1024]{1,0:T(8,128)} fusion(f32[512,1024]{1,0:T(8,128)S(1)} %copy-done.3, f32[1024]{0:T(1024)S(1)} %add_divide_fusion, f32[512]{0:T(512)S(1)} %copy-done.8, f32[512]{0:T(512)S(1)} %copy-done.9, f32[1024]{0:T(1024)S(1)} %copy-done.7, pred[1024]{0:T(1024)(128)(4,1)S(1)} %broadcast_compare_fusion), kind=kLoop, calls=%fused_computation.4 | loop fusion | flops 4194304 | bytes 4207616 | tf_op jit(solution)/shard_map/mul | solution.py:28
  5.1 2.9 %reshape.123 = f32[128,4,1024]{2,1,0:T(4,128)} reshape(f32[512,1024]{1,0:T(8,128)} %exponential_multiply_fusion) | data formatting | bytes 4194304 | tf_op jit(solution)/shard_map/reshape | solution.py:127
  7.9 0.0 copy-start.4
  7.9 11.5 %all-to-all-start = ((f32[128,4,1024]{2,1,0:T(4,128)}), f32[128,4,1024]{2,1,0:T(4,128)S(1)}, u32[]{:S(2)}, u32[]{:S(2)}) async-start(f32[128,4,1024]{2,1,0:T(4,128)} %reshape.123), calls=%async_computation | async-start | bytes 4194304 | tf_op jit(solution)/shard_map/all_to_all | solution.py:126
  19.4 0.0 copy-start.1
  19.4 0.0 copy-start.5
  19.5 0.0 copy-done.4
  19.5 1.1 copy.15
  20.6 0.0 copy-done.1
  20.7 0.6 gather_fusion
  21.3 0.0 copy-done
  21.3 1.2 gather_fusion.1
  22.5 0.0 copy-done.5
  22.5 0.2 slice_reduce_fusion
  22.7 1.1 select_reduce_fusion.inv_ref
  23.8 0.6 fusion.6.var_ref
  24.5 0.7 fusion.10
  25.1 24.1 %all-to-all-done.recv_ref = f32[128,4,1024]{2,1,0:T(4,128)S(1)} async-done(((f32[128,4,1024]{2,1,0:T(4,128)}), f32[128,4,1024]{2,1,0:T(4,128)S(1)}, u32[]{:S(2)}, u32[]{:S(2)}) %all-to-all-start) | async-done | bytes 2097184 | tf_op jit(solution)/shard_map/all_to_all | solution.py:126
  49.2 0.0 copy-start.2
  49.2 1.3 copy-done.2
  50.5 71.9 %shard_map.104 = f32[128,4,1024]{2,1,0:T(4,128)} custom-call(s32[1024]{0:T(1024)} %select_reduce_fusion.inv_ref, f32[4]{0:T(128)} %get-tuple-element.3.ax_ref, f32[4]{0:T(128)} %get-tuple-element.2.ay_ref, s32[4]{0:T(128)} %fusion.6.var_ref, s32[4]{0:T(128)} %gather_fusion.1, f32[128,4,1024]{2,1,0:T(4,128)} %copy-done.2, f32[32,8,512]{2,1,0:T(8,128)} %bitcast.9), custom_call_target="tpu_custom_call" | custom-call | tf_op jit(solution)/shard_map/pallas_call | solution.py:105
  122.4 34.1 %all_to_all.10 = f32[128,4,1024]{2,1,0:T(4,128)S(1)} all-to-all(f32[128,4,1024]{2,1,0:T(4,128)} %shard_map.104), channel_id=1, replica_groups=mesh['pt'=8,'comp'=16] {'pt','comp'}, dimensions={0} | all-to-all | bytes 4194304 | tf_op jit(solution)/shard_map/all_to_all | solution.py:147
  156.5 0.4 reduce_sum.29
  156.9 0.6 sqrt_multiply_fusion
  157.5 1.7 %reshape.125 = f32[512,1024]{1,0:T(8,128)} reshape(f32[128,4,1024]{2,1,0:T(4,128)S(1)} %all_to_all.10) | data formatting | bytes 4194304 | tf_op jit(solution)/shard_map/reshape | solution.py:148
  (7 shorter events, 0.1 us)
Async XLA Ops:
  0.6 20.7 %copy-start = (s32[512]{0:T(512)S(1)}, s32[512]{0:T(512)}, u32[]{:S(2)}) copy-start(s32[512]{0:T(512)} %param.14) | copy-start | bytes 6148
  0.6 2.2 %copy-start.3 = (f32[512,1024]{1,0:T(8,128)S(1)}, f32[512,1024]{1,0:T(8,128)}, u32[]{:S(2)}) copy-start(f32[512,1024]{1,0:T(8,128)} %param.9) | copy-start | bytes 6291460
  0.7 1.9 %copy-start.6 = (s32[1024]{0:T(1024)S(1)}, s32[1024]{0:T(1024)}, u32[]{:S(2)}) copy-start(s32[1024]{0:T(1024)} %param.15) | copy-start | bytes 12292
  0.7 2.2 %copy-start.7 = (f32[1024]{0:T(1024)S(1)}, f32[1024]{0:T(1024)}, u32[]{:S(2)}) copy-start(f32[1024]{0:T(1024)} %param.10) | copy-start | bytes 12292
  0.7 2.2 %copy-start.9 = (f32[512]{0:T(512)S(1)}, f32[512]{0:T(512)}, u32[]{:S(2)}) copy-start(f32[512]{0:T(512)} %param.11) | copy-start | bytes 6148
  0.7 2.2 %copy-start.8 = (f32[512]{0:T(512)S(1)}, f32[512]{0:T(512)}, u32[]{:S(2)}) copy-start(f32[512]{0:T(512)} %param.12) | copy-start | bytes 6148
  7.9 11.5 %copy-start.4 = (s32[256,512]{1,0:T(8,128)S(1)}, s32[256,512]{1,0:T(8,128)}, u32[]{:S(2)}) copy-start(s32[256,512]{1,0:T(8,128)} %param.17) | copy-start | bytes 1572868
  7.9 41.3 %all-to-all-start = ((f32[128,4,1024]{2,1,0:T(4,128)}), f32[128,4,1024]{2,1,0:T(4,128)S(1)}, u32[]{:S(2)}, u32[]{:S(2)}) async-start(f32[128,4,1024]{2,1,0:T(4,128)} %reshape.123), calls=%async_computation | async-start | bytes 4194304 | tf_op jit(solution)/shard_map/all_to_all | solution.py:126
  19.4 1.2 copy-start.1
  19.4 3.1 %copy-start.5 = (s32[131072]{0:T(1024)S(1)}, s32[131072]{0:T(1024)}, u32[]{:S(2)}) copy-start(s32[131072]{0:T(1024)} %param.16) | copy-start | bytes 1572868
  49.2 1.3 copy-start.2

commit v4 on v3

--- a/solution.py
+++ b/solution.py
@@ -29,8 +29,8 @@
 
 
 def propagate_kernel(inv_ref, ax_ref, ay_ref, var_ref, cnt_ref, recv_ref, wet_ref, out_ref, buf_ref):
-    comps = recv_ref.shape[1]
-    runs_per_dev = recv_ref.shape[2] // RUN
+    comps = recv_ref.shape[2]
+    runs_per_dev = recv_ref.shape[1]
     slabs = wet_ref.shape[0]
     cols = wet_ref.shape[2]
     quarters = cols // RUN
@@ -43,12 +43,12 @@
                 for q in range(quarters):
                     s = inv_ref[(k * slabs + j) * quarters + q]
                     src = s // runs_per_dev
-                    off = pl.multiple_of((s % runs_per_dev) * RUN, RUN)
+                    m = s % runs_per_dev
                     lanes = slice(q * RUN, (q + 1) * RUN)
                     if to_grid:
-                        buf_ref[c, slot, j, k:k + 1, lanes] = recv_ref[src, c:c + 1, pl.ds(off, RUN)]
+                        buf_ref[c, slot, j, k:k + 1, lanes] = recv_ref[src, m, c:c + 1, :]
                     else:
-                        out_ref[src, c:c + 1, pl.ds(off, RUN)] = buf_ref[c, slot, j, k:k + 1, lanes]
+                        out_ref[src, m, c:c + 1, :] = buf_ref[c, slot, j, k:k + 1, lanes]
             return carry
 
         lax.fori_loop(0, slabs, body, 0)
@@ -107,7 +107,7 @@
         out_shape=jax.ShapeDtypeStruct(recv.shape, recv.dtype),
         in_specs=[smem] * 5 + [vmem] * 2,
         out_specs=vmem,
-        scratch_shapes=[pltpu.VMEM((recv.shape[1], 2, slabs, SUB, cols), jnp.float32)],
+        scratch_shapes=[pltpu.VMEM((recv.shape[2], 2, slabs, SUB, cols), jnp.float32)],
     )(inv, ax, ay, var, cnt, recv, wet_t)
 
 
@@ -123,8 +123,9 @@
     rows_grid = wet.shape[0]
     cols_grid = wet.shape[1]
     run_count = all_points // RUN
+    runs_per_dev = point_count // RUN
     fields = lax.all_to_all(
-        forced.reshape(group_size, per_device, point_count),
+        forced.reshape(group_size, per_device, runs_per_dev, RUN).transpose(0, 2, 1, 3),
         ("pt", "comp"),
         split_axis=0,
         concat_axis=0,
@@ -145,7 +146,7 @@
     inv = jnp.sum(jnp.where(slot_runs[None, :] == run_ids[:, None], run_ids[None, :], 0), axis=1)
     slots = propagate(inv, jnp.abs(cross), jnp.abs(along), var, counts, fields, wet_t)
     back = lax.all_to_all(slots, ("pt", "comp"), split_axis=0, concat_axis=0, tiled=True)
-    arrived = back.reshape(total_comps, point_count)
+    arrived = back.transpose(0, 2, 1, 3).reshape(total_comps, point_count)
     height = 4.0 * jnp.sqrt(jnp.mean(arrived, axis=0) + 1e-06)
     return (arrived, height)
 

time: 160 us -> 153 us (0.956)
  Pallas kernels: 71.9 us -> 66 us
    pallas_call x1, Pallas kernels: 71.9 us -> 66 us  [propagate(): pl.pallas_call(propagate_kernel, out_shape=jax.ShapeDtypeStruct(recv.shap...]
    reshape x2 -> x1, local copies, waits for them, and re-layouts: 4.56 us -> 1.86 us  [on_device(): forced.reshape(group_size, per_device, runs_per_dev, RUN)]
    mul x1 -> x0, other arithmetic: 2.17 us -> none  [sources(): return spectrum * jnp.exp(time_step * rate)]
    unnamed x20, local copies, waits for them, and re-layouts: 1.64 us -> 3.61 us
where the time goes in v4:
time: 153 us
  Pallas kernels  66 us (43%)
  blocking collectives  35 us (23%)
  waiting for transfers between devices  24.1 us (16%)
  starting transfers between devices  11.5 us (8%)
  local copies, waits for them, and re-layouts  8.81 us (6%)
  other arithmetic  6.76 us (4%)
    pallas_call x1, Pallas kernels, propagate(): pl.pallas_call(propagate_kernel, out_shape=jax.ShapeDtypeStruct(recv.shap...  66 us
    all_to_all x1, blocking collectives, on_device(): lax.all_to_all(slots, ('pt', 'comp'), split_axis=0, concat_axis=0, tiled=...  35 us
    all_to_all x1, waiting for transfers between devices, on_device(): lax.all_to_all(forced.reshape(group_size, per_device, runs_per_dev, RUN)....  24.1 us
    all_to_all x1, starting transfers between devices, on_device(): lax.all_to_all(forced.reshape(group_size, per_device, runs_per_dev, RUN)....  11.5 us
    unnamed x20, local copies, waits for them, and re-layouts  3.61 us
  transfers between devices with their start and end apart: 1, of which 1 were waited for; matrix products, arithmetic and copies ran while one was open for 4% of the time, Pallas kernels for 0%

profile of v4, /device:TPU:1, one launch (start us, length us, event | category | flops | bytes accessed | tf_op | source)
XLA Modules:
  0.0 153.0 jit_solution(10526367579019269021)
XLA Ops:
  0.6 0.0 copy-start
  0.6 0.0 copy-start.3
  0.7 0.0 copy-start.7
  0.7 0.0 copy-start.8
  0.7 0.0 copy-start.6
  0.7 0.8 broadcast_compare_fusion
  1.5 1.7 %reduce_sum.28 = f32[1024]{0:T(1024)S(1)} reduce(f32[512,1024]{1,0:T(8,128)} %param.9, f32[]{:T(128)} %constant.75.clone.1), dimensions={0}, to_apply=%region_1.2 | reduce | flops 523264 | bytes 2101252 | tf_op jit(solution)/shard_map/reduce_sum | solution.py:22
  3.3 0.0 copy-done.3
  3.3 0.0 copy-done.7
  3.3 0.0 copy-done.8
  3.3 0.0 copy-done.6
  3.3 0.8 multiply_bitcast_fusion
  4.2 0.5 copy.20
  4.6 1.9 %copy.26 = f32[128,4,8,128]{3,1,2,0:T(4,128)} copy(f32[128,4,8,128]{3,2,1,0:T(8,128)S(1)} %bitcast.27) | data formatting | bytes 4194304 | tf_op jit(solution)/shard_map/reshape | solution.py:128
  6.5 0.0 copy-start.4
  6.5 11.5 %all-to-all-start = ((f32[128,8,4,128]{3,2,1,0:T(4,128)}), f32[128,8,4,128]{3,2,1,0:T(4,128)S(1)}, u32[]{:S(2)}, u32[]{:S(2)}) async-start(f32[128,8,4,128]{3,2,1,0:T(4,128)} %bitcast.26), calls=%async_computation | async-start | bytes 4194304 | tf_op jit(solution)/shard_map/all_to_all | solution.py:127
  18.0 0.0 copy-start.1
  18.0 0.0 copy-start.5
  18.0 0.0 copy-done.4
  18.1 1.1 copy.27
  19.2 0.0 copy-done
  19.2 1.2 gather_fusion.1
  20.5 0.0 copy-done.1
  20.5 0.6 gather_fusion
  21.1 0.0 copy-done.5
  21.1 0.2 slice_reduce_fusion
  21.3 1.1 select_reduce_fusion.inv_ref
  22.4 0.6 fusion.6.var_ref
  23.1 0.6 fusion.10
  23.7 24.1 %all-to-all-done.recv_ref = f32[128,8,4,128]{3,2,1,0:T(4,128)S(1)} async-done(((f32[128,8,4,128]{3,2,1,0:T(4,128)}), f32[128,8,4,128]{3,2,1,0:T(4,128)S(1)}, u32[]{:S(2)}, u32[]{:S(2)}) %all-to-all-start) | async-done | bytes 2097184 | tf_op jit(solution)/shard_map/all_to_all | solution.py:127
  47.8 0.0 copy-start.2
  47.8 1.3 copy-done.2
  49.1 66.0 %shard_map.104 = f32[128,8,4,128]{3,2,1,0:T(4,128)} custom-call(s32[1024]{0:T(1024)} %select_reduce_fusion.inv_ref, f32[4]{0:T(128)} %get-tuple-element.3.ax_ref, f32[4]{0:T(128)} %get-tuple-element.2.ay_ref, s32[4]{0:T(128)} %fusion.6.var_ref, s32[4]{0:T(128)} %gather_fusion.1, f32[128,8,4,128]{3,2,1,0:T(4,128)} %copy-done.2, f32[32,8,512]{2,1,0:T(8,128)} %bitcast.29), custom_call_target="tpu_custom_call" | custom-call | tf_op jit(solution)/shard_map/pallas_call | solution.py:105
  115.1 35.0 %all_to_all.10 = f32[128,8,4,128]{3,2,1,0:T(4,128)S(1)} all-to-all(f32[128,8,4,128]{3,2,1,0:T(4,128)} %shard_map.104), channel_id=1, replica_groups=mesh['pt'=8,'comp'=16] {'pt','comp'}, dimensions={0} | all-to-all | bytes 4194304 | tf_op jit(solution)/shard_map/all_to_all | solution.py:148
  150.1 0.3 bitcast_reduce_fusion
  150.4 0.6 multiply_bitcast_fusion.1
  151.0 0.2 copy.19
  151.2 1.8 %copy.25 = f32[64,8,8,128]{3,1,2,0:T(8,128)} copy(f32[64,8,8,128]{3,2,1,0:T(8,128)S(1)} %bitcast.28) | data formatting | bytes 4194304
  (6 shorter events, 0.1 us)
Async XLA Ops:
  0.6 18.6 %copy-start = (s32[512]{0:T(512)S(1)}, s32[512]{0:T(512)}, u32[]{:S(2)}) copy-start(s32[512]{0:T(512)} %param.14) | copy-start | bytes 6148
  0.6 2.6 %copy-start.3 = (f32[512,1024]{1,0:T(8,128)S(1)}, f32[512,1024]{1,0:T(8,128)}, u32[]{:S(2)}) copy-start(f32[512,1024]{1,0:T(8,128)} %param.9) | copy-start | bytes 6291460
  0.7 2.6 %copy-start.7 = (f32[512]{0:T(512)S(1)}, f32[512]{0:T(512)}, u32[]{:S(2)}) copy-start(f32[512]{0:T(512)} %param.12) | copy-start | bytes 6148
  0.7 2.6 %copy-start.8 = (f32[512]{0:T(512)S(1)}, f32[512]{0:T(512)}, u32[]{:S(2)}) copy-start(f32[512]{0:T(512)} %param.11) | copy-start | bytes 6148
  0.7 2.6 %copy-start.6 = (f32[1024]{0:T(1024)S(1)}, f32[1024]{0:T(1024)}, u32[]{:S(2)}) copy-start(f32[1024]{0:T(1024)} %param.10) | copy-start | bytes 12292
  6.5 11.5 %copy-start.4 = (s32[256,512]{1,0:T(8,128)S(1)}, s32[256,512]{1,0:T(8,128)}, u32[]{:S(2)}) copy-start(s32[256,512]{1,0:T(8,128)} %param.17) | copy-start | bytes 1572868
  6.5 41.3 %all-to-all-start = ((f32[128,8,4,128]{3,2,1,0:T(4,128)}), f32[128,8,4,128]{3,2,1,0:T(4,128)S(1)}, u32[]{:S(2)}, u32[]{:S(2)}) async-start(f32[128,8,4,128]{3,2,1,0:T(4,128)} %bitcast.26), calls=%async_computation | async-start | bytes 4194304 | tf_op jit(solution)/shard_map/all_to_all | solution.py:127
  18.0 2.5 %copy-start.1 = (f32[16]{0:T(128)S(1)}, f32[16]{0:T(128)}, u32[]{:S(2)}) copy-start(f32[16]{0:T(128)} %param.13) | copy-start | bytes 196
  18.0 3.1 %copy-start.5 = (s32[131072]{0:T(1024)S(1)}, s32[131072]{0:T(1024)}, u32[]{:S(2)}) copy-start(s32[131072]{0:T(1024)} %param.16) | copy-start | bytes 1572868
  47.8 1.3 copy-start.2

commit v5 on v4

--- a/solution.py
+++ b/solution.py
@@ -37,6 +37,7 @@
 
     def copy_runs(c, to_grid):
         slot = 0 if to_grid else cnt_ref[c] % 2
+        buf_c = buf_ref
 
         def body(j, carry):
             for k in range(SUB):
@@ -46,9 +47,9 @@
                     m = s % runs_per_dev
                     lanes = slice(q * RUN, (q + 1) * RUN)
                     if to_grid:
-                        buf_ref[c, slot, j, k:k + 1, lanes] = recv_ref[src, m, c:c + 1, :]
+                        buf_c[slot, j, k:k + 1, lanes] = recv_ref[src, m, c:c + 1, :]
                     else:
-                        out_ref[src, m, c:c + 1, :] = buf_ref[c, slot, j, k:k + 1, lanes]
+                        out_ref[src, m, c:c + 1, :] = buf_c[slot, j, k:k + 1, lanes]
             return carry
 
         lax.fori_loop(0, slabs, body, 0)
@@ -56,20 +57,20 @@
     def substep(c, src, dst, south, east, axc, ayc):
         sub_id = lax.broadcasted_iota(jnp.int32, (SUB, cols), 0)
         if south:
-            edge = buf_ref[c, src, slabs - 1] * wet_ref[slabs - 1]
+            edge = buf_ref[src, slabs - 1] * wet_ref[slabs - 1]
             init = jnp.where(sub_id == 0, 0.0, pltpu.roll(edge, 1, 0))
         else:
-            edge = buf_ref[c, src, 0] * wet_ref[0]
+            edge = buf_ref[src, 0] * wet_ref[0]
             init = jnp.where(sub_id == SUB - 1, 0.0, pltpu.roll(edge, SUB - 1, 0))
 
         def body(i, up_row):
             j = i if south else slabs - 1 - i
-            f = buf_ref[c, src, j]
+            f = buf_ref[src, j]
             w = wet_ref[j]
             sea = f * w
             up_col = pltpu.roll(sea, 1 if east else cols - 1, 1)
             moved = f - axc * (f - up_row) - ayc * (f - up_col)
-            buf_ref[c, dst, j] = jnp.where(w > 0, moved, f)
+            buf_ref[dst, j] = jnp.where(w > 0, moved, f)
             return sea
 
         lax.fori_loop(0, slabs, body, init, unroll=True)
@@ -84,18 +85,22 @@
                 substep(c, n % 2, (n + 1) % 2, south, east, axc, ayc)
 
     def comp_body(c, carry):
+        for cc in range(comps):
+            @pl.when(c == cc)
+            def _():
+                copy_runs(cc, True)
         v = var_ref[c]
         for vi, (south, east) in enumerate(((False, False), (False, True), (True, False), (True, True))):
             @pl.when(v == vi)
             def _():
                 variant(south, east, c)
+        for cc in range(comps):
+            @pl.when(c == cc)
+            def _():
+                copy_runs(cc, False)
         return carry
 
-    for c in range(comps):
-        copy_runs(c, True)
     lax.fori_loop(0, comps, comp_body, 0)
-    for c in range(comps):
-        copy_runs(c, False)
 
 
 def propagate(inv, ax, ay, var, cnt, recv, wet_t):
@@ -107,7 +112,7 @@
         out_shape=jax.ShapeDtypeStruct(recv.shape, recv.dtype),
         in_specs=[smem] * 5 + [vmem] * 2,
         out_specs=vmem,
-        scratch_shapes=[pltpu.VMEM((recv.shape[2], 2, slabs, SUB, cols), jnp.float32)],
+        scratch_shapes=[pltpu.VMEM((2, slabs, SUB, cols), jnp.float32)],
     )(inv, ax, ay, var, cnt, recv, wet_t)
 
 

time: 153 us -> 152 us (level)
  no operation moved by 1% of the time
where the time goes in v5:
time: 152 us
  Pallas kernels  64.8 us (43%)
  blocking collectives  35.4 us (23%)
  waiting for transfers between devices  24.1 us (16%)
  starting transfers between devices  11.5 us (8%)
  local copies, waits for them, and re-layouts  8.81 us (6%)
  other arithmetic  6.76 us (4%)
    pallas_call x1, Pallas kernels, propagate(): pl.pallas_call(propagate_kernel, out_shape=jax.ShapeDtypeStruct(recv.shap...  64.8 us
    all_to_all x1, blocking collectives, on_device(): lax.all_to_all(slots, ('pt', 'comp'), split_axis=0, concat_axis=0, tiled=...  35.4 us
    all_to_all x1, waiting for transfers between devices, on_device(): lax.all_to_all(forced.reshape(group_size, per_device, runs_per_dev, RUN)....  24.1 us
    all_to_all x1, starting transfers between devices, on_device(): lax.all_to_all(forced.reshape(group_size, per_device, runs_per_dev, RUN)....  11.5 us
    unnamed x20, local copies, waits for them, and re-layouts  3.61 us
  transfers between devices with their start and end apart: 1, of which 1 were waited for; matrix products, arithmetic and copies ran while one was open for 4% of the time, Pallas kernels for 0%

profile of v5, /device:TPU:1, one launch (start us, length us, event | category | flops | bytes accessed | tf_op | source)
XLA Modules:
  0.0 152.1 jit_solution(11143981525381708531)
XLA Ops:
  0.6 0.0 copy-start
  0.6 0.0 copy-start.3
  0.7 0.0 copy-start.7
  0.7 0.0 copy-start.8
  0.7 0.0 copy-start.6
  0.7 0.8 broadcast_compare_fusion
  1.5 1.7 %reduce_sum.28 = f32[1024]{0:T(1024)S(1)} reduce(f32[512,1024]{1,0:T(8,128)} %param.9, f32[]{:T(128)} %constant.75.clone.1), dimensions={0}, to_apply=%region_1.2 | reduce | flops 523264 | bytes 2101252 | tf_op jit(solution)/shard_map/reduce_sum | solution.py:22
  3.3 0.0 copy-done.3
  3.3 0.0 copy-done.7
  3.3 0.0 copy-done.8
  3.3 0.0 copy-done.6
  3.3 0.8 multiply_bitcast_fusion
  4.2 0.5 copy.20
  4.6 1.9 %copy.26 = f32[128,4,8,128]{3,1,2,0:T(4,128)} copy(f32[128,4,8,128]{3,2,1,0:T(8,128)S(1)} %bitcast.27) | data formatting | bytes 4194304 | tf_op jit(solution)/shard_map/reshape | solution.py:133
  6.5 0.0 copy-start.4
  6.5 11.5 %all-to-all-start = ((f32[128,8,4,128]{3,2,1,0:T(4,128)}), f32[128,8,4,128]{3,2,1,0:T(4,128)S(1)}, u32[]{:S(2)}, u32[]{:S(2)}) async-start(f32[128,8,4,128]{3,2,1,0:T(4,128)} %bitcast.26), calls=%async_computation | async-start | bytes 4194304 | tf_op jit(solution)/shard_map/all_to_all | solution.py:132
  18.0 0.0 copy-start.1
  18.0 0.0 copy-start.5
  18.0 0.0 copy-done.4
  18.1 1.1 copy.27
  19.2 0.0 copy-done
  19.2 1.2 gather_fusion.1
  20.5 0.0 copy-done.1
  20.5 0.6 gather_fusion
  21.1 0.0 copy-done.5
  21.1 0.2 slice_reduce_fusion
  21.3 1.1 select_reduce_fusion.inv_ref
  22.4 0.6 fusion.6.var_ref
  23.1 0.6 fusion.10
  23.7 24.1 %all-to-all-done.recv_ref = f32[128,8,4,128]{3,2,1,0:T(4,128)S(1)} async-done(((f32[128,8,4,128]{3,2,1,0:T(4,128)}), f32[128,8,4,128]{3,2,1,0:T(4,128)S(1)}, u32[]{:S(2)}, u32[]{:S(2)}) %all-to-all-start) | async-done | bytes 2097184 | tf_op jit(solution)/shard_map/all_to_all | solution.py:132
  47.8 0.0 copy-start.2
  47.8 1.3 copy-done.2
  49.1 64.8 %shard_map.104 = f32[128,8,4,128]{3,2,1,0:T(4,128)} custom-call(s32[1024]{0:T(1024)} %select_reduce_fusion.inv_ref, f32[4]{0:T(128)} %get-tuple-element.3.ax_ref, f32[4]{0:T(128)} %get-tuple-element.2.ay_ref, s32[4]{0:T(128)} %fusion.6.var_ref, s32[4]{0:T(128)} %gather_fusion.1, f32[128,8,4,128]{3,2,1,0:T(4,128)} %copy-done.2, f32[32,8,512]{2,1,0:T(8,128)} %bitcast.29), custom_call_target="tpu_custom_call" | custom-call | tf_op jit(solution)/shard_map/pallas_call | solution.py:110
  113.9 35.4 %all_to_all.10 = f32[128,8,4,128]{3,2,1,0:T(4,128)S(1)} all-to-all(f32[128,8,4,128]{3,2,1,0:T(4,128)} %shard_map.104), channel_id=1, replica_groups=mesh['pt'=8,'comp'=16] {'pt','comp'}, dimensions={0} | all-to-all | bytes 4194304 | tf_op jit(solution)/shard_map/all_to_all | solution.py:153
  149.3 0.3 bitcast_reduce_fusion
  149.6 0.6 multiply_bitcast_fusion.1
  150.2 0.2 copy.19
  150.3 1.8 %copy.25 = f32[64,8,8,128]{3,1,2,0:T(8,128)} copy(f32[64,8,8,128]{3,2,1,0:T(8,128)S(1)} %bitcast.28) | data formatting | bytes 4194304
  (6 shorter events, 0.1 us)
Async XLA Ops:
  0.6 18.6 %copy-start = (s32[512]{0:T(512)S(1)}, s32[512]{0:T(512)}, u32[]{:S(2)}) copy-start(s32[512]{0:T(512)} %param.14) | copy-start | bytes 6148
  0.6 2.6 %copy-start.3 = (f32[512,1024]{1,0:T(8,128)S(1)}, f32[512,1024]{1,0:T(8,128)}, u32[]{:S(2)}) copy-start(f32[512,1024]{1,0:T(8,128)} %param.9) | copy-start | bytes 6291460
  0.7 2.6 %copy-start.7 = (f32[512]{0:T(512)S(1)}, f32[512]{0:T(512)}, u32[]{:S(2)}) copy-start(f32[512]{0:T(512)} %param.12) | copy-start | bytes 6148
  0.7 2.6 %copy-start.8 = (f32[512]{0:T(512)S(1)}, f32[512]{0:T(512)}, u32[]{:S(2)}) copy-start(f32[512]{0:T(512)} %param.11) | copy-start | bytes 6148
  0.7 2.6 %copy-start.6 = (f32[1024]{0:T(1024)S(1)}, f32[1024]{0:T(1024)}, u32[]{:S(2)}) copy-start(f32[1024]{0:T(1024)} %param.10) | copy-start | bytes 12292
  6.5 11.5 %copy-start.4 = (s32[256,512]{1,0:T(8,128)S(1)}, s32[256,512]{1,0:T(8,128)}, u32[]{:S(2)}) copy-start(s32[256,512]{1,0:T(8,128)} %param.17) | copy-start | bytes 1572868
  6.5 41.3 %all-to-all-start = ((f32[128,8,4,128]{3,2,1,0:T(4,128)}), f32[128,8,4,128]{3,2,1,0:T(4,128)S(1)}, u32[]{:S(2)}, u32[]{:S(2)}) async-start(f32[128,8,4,128]{3,2,1,0:T(4,128)} %bitcast.26), calls=%async_computation | async-start | bytes 4194304 | tf_op jit(solution)/shard_map/all_to_all | solution.py:132
  18.0 2.5 %copy-start.1 = (f32[16]{0:T(128)S(1)}, f32[16]{0:T(128)}, u32[]{:S(2)}) copy-start(f32[16]{0:T(128)} %param.13) | copy-start | bytes 196
  18.0 3.1 %copy-start.5 = (s32[131072]{0:T(1024)S(1)}, s32[131072]{0:T(1024)}, u32[]{:S(2)}) copy-start(s32[131072]{0:T(1024)} %param.16) | copy-start | bytes 1572868
  47.8 1.3 copy-start.2

commit v6 on v4

v6 whole, which is shorter than its diff:
```python
import functools
import math

import jax
import jax.numpy as jnp
from jax import lax
from jax.experimental import pallas as pl
from jax.experimental.pallas import tpu as pltpu
from jax.sharding import PartitionSpec as P

DIRS = 32
MAXSUB = 8
RUN = 128
SUB = 8


rate_limit = 0.5
time_step = 0.5


def sources(spectrum, wind, growth, whitecap, limiter):
    mean_energy = jnp.mean(spectrum, axis=0)
    rate = (
        wind[None, :] * growth[:, None]
        - whitecap[:, None] * (mean_energy / (1.0 + mean_energy))[None, :]
    )
    rate = jnp.where(limiter[None, :] == 1, rate_limit * jnp.tanh(rate / rate_limit), rate)
    return spectrum * jnp.exp(time_step * rate)


def propagate_kernel(inv_ref, coef_ref, recv_ref, wet_ref, out_ref, buf_ref):
    comps = recv_ref.shape[2]
    runs_per_dev = recv_ref.shape[1]
    half = wet_ref.shape[0]
    cols = wet_ref.shape[2]
    quarters = cols // RUN
    halves = SUB // comps

    def copy_runs(to_grid, slot):
        def body(i, carry):
            for h in range(halves):
                for q in range(quarters):
                    s = inv_ref[(h * half + i) * quarters + q]
                    src = s // runs_per_dev
                    m = s % runs_per_dev
                    lanes = slice(q * RUN, (q + 1) * RUN)
                    rows = slice(h * comps, (h + 1) * comps)
                    if to_grid:
                        buf_ref[slot, i, rows, lanes] = recv_ref[src, m]
                    else:
                        out_ref[src, m] = buf_ref[slot, i, rows, lanes]
            return carry

        lax.fori_loop(0, half, body, 0)

    copy_runs(True, 0)
    ax = coef_ref[0]
    ay = coef_ref[1]
    south = coef_ref[2] > 0
    east = coef_ref[3] > 0
    cnt = coef_ref[4]
    sub_id = lax.broadcasted_iota(jnp.int32, (SUB, cols), 0)
    low = sub_id < comps
    for n in range(MAXSUB):
        src, dst = n % 2, (n + 1) % 2
        active = cnt > n
        sea = {}

        def sea_of(i):
            if i not in sea:
                sea[i] = buf_ref[src, i] * wet_ref[i]
            return sea[i]

        for i in range(half):
            if i == 0:
                prev = jnp.where(low, 0.0, pltpu.roll(sea_of(half - 1), comps, 0))
            else:
                prev = sea_of(i - 1)
            if i == half - 1:
                nxt = jnp.where(low, pltpu.roll(sea_of(0), comps, 0), 0.0)
            else:
                nxt = sea_of(i + 1)
            f = buf_ref[src, i]
            w = wet_ref[i]
            here = sea_of(i)
            up_row = jnp.where(south, prev, nxt)
            up_col = jnp.where(east, pltpu.roll(here, 1, 1), pltpu.roll(here, cols - 1, 1))
            moved = f - ax * (f - up_row) - ay * (f - up_col)
            buf_ref[dst, i] = jnp.where(active & (w > 0), moved, f)
            sea.pop(i - 1, None)
    copy_runs(False, MAXSUB % 2)


def propagate(inv, coef, recv, wet_h):
    half, _, cols = wet_h.shape
    smem = pl.BlockSpec(memory_space=pltpu.SMEM)
    vmem = pl.BlockSpec(memory_space=pltpu.VMEM)
    return pl.pallas_call(
        propagate_kernel,
        out_shape=jax.ShapeDtypeStruct(recv.shape, recv.dtype),
        in_specs=[smem] + [vmem] * 3,
        out_specs=vmem,
        scratch_shapes=[pltpu.VMEM((2, half, SUB, cols), jnp.float32)],
    )(inv, coef, recv, wet_h)


def on_device(spectrum, wind, growth, whitecap, courant, substeps, limiter, deck, wet):
    forced = sources(spectrum, wind, growth, whitecap, limiter)
    pt_count = lax.axis_size("pt")
    comp_count = lax.axis_size("comp")
    group_size = pt_count * comp_count
    total_comps = forced.shape[0]
    point_count = forced.shape[1]
    per_device = total_comps // group_size
    all_points = deck.shape[0]
    rows_grid = wet.shape[0]
    cols_grid = wet.shape[1]
    run_count = all_points // RUN
    runs_per_dev = point_count // RUN
    fields = lax.all_to_all(
        forced.reshape(group_size, per_device, runs_per_dev, RUN).transpose(0, 2, 1, 3),
        ("pt", "comp"),
        split_axis=0,
        concat_axis=0,
        tiled=True,
    )
    own_rank = lax.axis_index("pt") * comp_count + lax.axis_index("comp")
    comps = own_rank * per_device + jnp.arange(per_device, dtype=jnp.int32)
    angle = 2.0 * math.pi / DIRS * ((comps % DIRS).astype(jnp.float32) + 0.5)
    speed = courant[comps // DIRS]
    cross = speed * jnp.sin(angle)
    along = speed * jnp.cos(angle)
    counts = substeps[comps]
    halves = SUB // per_device
    half = rows_grid // halves
    lane_rows = jnp.stack([jnp.abs(cross), jnp.abs(along), (cross > 0).astype(jnp.float32),
                           (along > 0).astype(jnp.float32), counts.astype(jnp.float32)])
    coef = jnp.broadcast_to(jnp.tile(lane_rows, (1, halves))[:, :, None], (5, SUB, cols_grid))
    wet_h = jnp.broadcast_to(
        wet.astype(jnp.float32).reshape(halves, 1, half, cols_grid), (halves, per_device, half, cols_grid)
    ).reshape(SUB, half, cols_grid).transpose(1, 0, 2)
    slot_runs = deck.reshape(run_count, RUN)[:, 0] // RUN
    run_ids = jnp.arange(run_count, dtype=jnp.int32)
    inv = jnp.sum(jnp.where(slot_runs[None, :] == run_ids[:, None], run_ids[None, :], 0), axis=1)
    slots = propagate(inv, coef, fields, wet_h)
    back = lax.all_to_all(slots, ("pt", "comp"), split_axis=0, concat_axis=0, tiled=True)
    arrived = back.transpose(0, 2, 1, 3).reshape(total_comps, point_count)
    height = 4.0 * jnp.sqrt(jnp.mean(arrived, axis=0) + 1e-06)
    return (arrived, height)


def solution(mesh):
    in_specs = (
        P(None, ("pt", "comp")),
        P(("pt", "comp")),
        P(),
        P(),
        P(),
        P(),
        P(("pt", "comp")),
        P(),
        P(),
    )
    out_specs = (P(None, ("pt", "comp")), P(("pt", "comp")))
    return jax.shard_map(
        on_device, mesh=mesh, in_specs=in_specs, out_specs=out_specs, check_vma=False
    )
```

time: 153 us -> 113 us (0.74)
  Pallas kernels: 66 us -> 27.1 us
  other arithmetic: 6.76 us -> 4.91 us
    pallas_call x1, Pallas kernels: 66 us -> 27.1 us  [propagate(): pl.pallas_call(propagate_kernel, out_shape=jax.ShapeDtypeStruct(recv.shap...]
    broadcast_in_dim x0 -> x3, local copies, waits for them, and re-layouts: none -> 1.71 us  [the longest x2 1.02 us: on_device(): jnp.broadcast_to(wet.astype(jnp.float32).reshape(halves, 1, half, cols_gr...]
  transfers between devices with their start and end apart: 1 -> 1, of which waited for: 1 -> 1; matrix products, arithmetic and copies ran while one was open for 4% -> 5% of each run, Pallas kernels for 0% -> 0%
where the time goes in v6:
time: 113 us
  blocking collectives  34.6 us (31%)
  Pallas kernels  27.1 us (24%)
  waiting for transfers between devices  23.6 us (21%)
  starting transfers between devices  12 us (11%)
  local copies, waits for them, and re-layouts  9.73 us (9%)
  other arithmetic  4.91 us (4%)
    all_to_all x1, blocking collectives, on_device(): lax.all_to_all(slots, ('pt', 'comp'), split_axis=0, concat_axis=0, tiled=...  34.6 us
    pallas_call x1, Pallas kernels, propagate(): pl.pallas_call(propagate_kernel, out_shape=jax.ShapeDtypeStruct(recv.shap...  27.1 us
    all_to_all x1, waiting for transfers between devices, on_device(): lax.all_to_all(forced.reshape(group_size, per_device, runs_per_dev, RUN)....  23.6 us
    all_to_all x1, starting transfers between devices, on_device(): lax.all_to_all(forced.reshape(group_size, per_device, runs_per_dev, RUN)....  12 us
    unnamed x20, local copies, waits for them, and re-layouts  2.57 us
  transfers between devices with their start and end apart: 1, of which 1 were waited for; matrix products, arithmetic and copies ran while one was open for 5% of the time, Pallas kernels for 0%

profile of v6, /device:TPU:1, one launch (start us, length us, event | category | flops | bytes accessed | tf_op | source)
XLA Modules:
  0.0 112.6 jit_solution(13441134973850544070)
XLA Ops:
  0.6 0.0 copy-start
  0.6 0.0 copy-start.2
  0.7 0.0 copy-start.5
  0.7 0.0 copy-start.6
  0.7 0.0 copy-start.8
  0.7 0.0 copy-start.7
  0.7 1.9 %reduce_sum.28 = f32[1024]{0:T(1024)S(1)} reduce(f32[512,1024]{1,0:T(8,128)} %param.9, f32[]{:T(128)} %constant.73.clone.1), dimensions={0}, to_apply=%region_1.2 | reduce | flops 523264 | bytes 2101252 | tf_op jit(solution)/shard_map/reduce_sum | solution.py:22
  2.6 0.0 copy-done.5
  2.6 0.3 copy-done.2
  2.9 0.0 copy-done.6
  2.9 0.0 copy-done.8
  2.9 0.0 copy-done.7
  2.9 0.8 multiply_bitcast_fusion
  3.7 0.5 copy.29
  4.2 1.9 %copy.34 = f32[128,4,8,128]{3,1,2,0:T(4,128)} copy(f32[128,4,8,128]{3,2,1,0:T(8,128)S(1)} %bitcast.40) | data formatting | bytes 4194304 | tf_op jit(solution)/shard_map/reshape | solution.py:121
  6.1 0.0 copy-start.1
  6.1 0.0 copy-start.3
  6.1 12.0 %all-to-all-start = ((f32[128,8,4,128]{3,2,1,0:T(4,128)}), f32[128,8,4,128]{3,2,1,0:T(4,128)}, u32[]{:S(2)}, u32[]{:S(2)}) async-start(f32[128,8,4,128]{3,2,1,0:T(4,128)} %bitcast.38), calls=%async_computation | async-start | bytes 4194304 | tf_op jit(solution)/shard_map/all_to_all | solution.py:120
  18.1 0.0 copy-done.1
  18.1 0.6 gather_fusion
  18.8 0.0 copy-done
  18.8 0.6 gather_fusion.1
  19.4 0.1 compare_convert_fusion
  19.5 0.1 fusion.9
  19.5 0.1 copy.24
  19.7 0.1 copy.25
  19.7 0.0 copy-done.3
  19.8 0.4 copy.27
  20.2 0.6 broadcast_in_dim.47
  20.8 0.0 copy-start.4
  20.8 1.7 %reshape.246 = f32[8,128,512]{2,0,1:T(8,128)} reshape(f32[2,4,128,512]{3,1,0,2:T(4,128)S(1)} %broadcast_in_dim.47) | data formatting | bytes 4194304 | tf_op jit(solution)/shard_map/reshape | solution.py:141
  22.6 0.0 copy-done.4
  22.6 0.2 slice_reduce_fusion
  22.8 1.1 select_reduce_fusion.inv_ref
  23.9 23.6 %all-to-all-done.recv_ref = f32[128,8,4,128]{3,2,1,0:T(4,128)} async-done(((f32[128,8,4,128]{3,2,1,0:T(4,128)}), f32[128,8,4,128]{3,2,1,0:T(4,128)}, u32[]{:S(2)}, u32[]{:S(2)}) %all-to-all-start) | async-done | bytes 2097184 | tf_op jit(solution)/shard_map/all_to_all | solution.py:120
  47.5 0.7 broadcast_in_dim.24.coef_ref
  48.1 27.1 %shard_map.104 = f32[128,8,4,128]{3,2,1,0:T(4,128)} custom-call(s32[1024]{0:T(1024)} %select_reduce_fusion.inv_ref, f32[5,8,512]{2,1,0:T(8,128)} %broadcast_in_dim.24.coef_ref, f32[128,8,4,128]{3,2,1,0:T(4,128)} %all-to-all-done.recv_ref, f32[128,8,512]{2,1,0:T(8,128)} %bitcast.42), custom_call_target="tpu_custom_call" | custom-call | tf_op jit(solution)/shard_map/pallas_call | solution.py:98
  75.2 34.6 %all_to_all.10 = f32[128,8,4,128]{3,2,1,0:T(4,128)S(1)} all-to-all(f32[128,8,4,128]{3,2,1,0:T(4,128)} %shard_map.104), channel_id=1, replica_groups=mesh['pt'=8,'comp'=16] {'pt','comp'}, dimensions={0} | all-to-all | bytes 4194304 | tf_op jit(solution)/shard_map/all_to_all | solution.py:146
  109.8 0.2 copy.28
  110.0 1.8 %copy.33 = f32[64,8,8,128]{3,1,2,0:T(8,128)} copy(f32[64,8,8,128]{3,2,1,0:T(8,128)S(1)} %bitcast.41) | data formatting | bytes 4194304
  111.7 0.3 bitcast_reduce_fusion
  112.0 0.6 multiply_bitcast_fusion.1
  (10 shorter events, 0.1 us)
Async XLA Ops:
  0.6 18.1 %copy-start = (s32[512]{0:T(512)S(1)}, s32[512]{0:T(512)}, u32[]{:S(2)}) copy-start(s32[512]{0:T(512)} %param.14) | copy-start | bytes 6148
  0.6 2.2 %copy-start.2 = (f32[512,1024]{1,0:T(8,128)S(1)}, f32[512,1024]{1,0:T(8,128)}, u32[]{:S(2)}) copy-start(f32[512,1024]{1,0:T(8,128)} %param.9) | copy-start | bytes 6291460
  0.7 1.9 %copy-start.5 = (s32[1024]{0:T(1024)S(1)}, s32[1024]{0:T(1024)}, u32[]{:S(2)}) copy-start(s32[1024]{0:T(1024)} %param.15) | copy-start | bytes 12292
  0.7 2.2 %copy-start.6 = (f32[1024]{0:T(1024)S(1)}, f32[1024]{0:T(1024)}, u32[]{:S(2)}) copy-start(f32[1024]{0:T(1024)} %param.10) | copy-start | bytes 12292
  0.7 2.2 %copy-start.8 = (f32[512]{0:T(512)S(1)}, f32[512]{0:T(512)}, u32[]{:S(2)}) copy-start(f32[512]{0:T(512)} %param.11) | copy-start | bytes 6148
  0.7 2.2 %copy-start.7 = (f32[512]{0:T(512)S(1)}, f32[512]{0:T(512)}, u32[]{:S(2)}) copy-start(f32[512]{0:T(512)} %param.12) | copy-start | bytes 6148
  6.1 12.0 %copy-start.1 = (f32[16]{0:T(128)S(1)}, f32[16]{0:T(128)}, u32[]{:S(2)}) copy-start(f32[16]{0:T(128)} %param.13) | copy-start | bytes 196
  6.1 13.7 %copy-start.3 = (s32[256,512]{1,0:T(8,128)S(1)}, s32[256,512]{1,0:T(8,128)}, u32[]{:S(2)}) copy-start(s32[256,512]{1,0:T(8,128)} %param.17) | copy-start | bytes 1572868
  6.1 41.4 %all-to-all-start = ((f32[128,8,4,128]{3,2,1,0:T(4,128)}), f32[128,8,4,128]{3,2,1,0:T(4,128)}, u32[]{:S(2)}, u32[]{:S(2)}) async-start(f32[128,8,4,128]{3,2,1,0:T(4,128)} %bitcast.38), calls=%async_computation | async-start | bytes 4194304 | tf_op jit(solution)/shard_map/all_to_all | solution.py:120
  20.8 1.7 %copy-start.4 = (s32[131072]{0:T(1024)S(1)}, s32[131072]{0:T(1024)}, u32[]{:S(2)}) copy-start(s32[131072]{0:T(1024)} %param.16) | copy-start | bytes 1572868

commit v7 on v6

--- a/solution.py
+++ b/solution.py
@@ -29,8 +29,7 @@
 
 
 def propagate_kernel(inv_ref, coef_ref, recv_ref, wet_ref, out_ref, buf_ref):
-    comps = recv_ref.shape[2]
-    runs_per_dev = recv_ref.shape[1]
+    comps = recv_ref.shape[1]
     half = wet_ref.shape[0]
     cols = wet_ref.shape[2]
     quarters = cols // RUN
@@ -41,14 +40,12 @@
             for h in range(halves):
                 for q in range(quarters):
                     s = inv_ref[(h * half + i) * quarters + q]
-                    src = s // runs_per_dev
-                    m = s % runs_per_dev
                     lanes = slice(q * RUN, (q + 1) * RUN)
                     rows = slice(h * comps, (h + 1) * comps)
                     if to_grid:
-                        buf_ref[slot, i, rows, lanes] = recv_ref[src, m]
+                        buf_ref[slot, i, rows, lanes] = recv_ref[s]
                     else:
-                        out_ref[src, m] = buf_ref[slot, i, rows, lanes]
+                        out_ref[s] = buf_ref[slot, i, rows, lanes]
             return carry
 
         lax.fori_loop(0, half, body, 0)
@@ -142,7 +139,8 @@
     slot_runs = deck.reshape(run_count, RUN)[:, 0] // RUN
     run_ids = jnp.arange(run_count, dtype=jnp.int32)
     inv = jnp.sum(jnp.where(slot_runs[None, :] == run_ids[:, None], run_ids[None, :], 0), axis=1)
-    slots = propagate(inv, coef, fields, wet_h)
+    slots = propagate(inv, coef, fields.reshape(run_count, per_device, RUN), wet_h)
+    slots = slots.reshape(fields.shape)
     back = lax.all_to_all(slots, ("pt", "comp"), split_axis=0, concat_axis=0, tiled=True)
     arrived = back.transpose(0, 2, 1, 3).reshape(total_comps, point_count)
     height = 4.0 * jnp.sqrt(jnp.mean(arrived, axis=0) + 1e-06)

time: 113 us -> 102 us (0.903)
  Pallas kernels: 27.1 us -> 16.1 us
    pallas_call x1, Pallas kernels: 27.1 us -> 16.1 us  [propagate(): pl.pallas_call(propagate_kernel, out_shape=jax.ShapeDtypeStruct(recv.shap...]
  transfers between devices with their start and end apart: 1 -> 1, of which waited for: 1 -> 1; matrix products, arithmetic and copies ran while one was open for 5% -> 6% of each run, Pallas kernels for 0% -> 0%
where the time goes in v7:
time: 102 us
  blocking collectives  34.6 us (34%)
  waiting for transfers between devices  23.6 us (23%)
  Pallas kernels  16.1 us (16%)
  starting transfers between devices  12 us (12%)
  local copies, waits for them, and re-layouts  9.73 us (10%)
  other arithmetic  4.91 us (5%)
    all_to_all x1, blocking collectives, on_device(): lax.all_to_all(slots, ('pt', 'comp'), split_axis=0, concat_axis=0, tiled=...  34.6 us
    all_to_all x1, waiting for transfers between devices, on_device(): lax.all_to_all(forced.reshape(group_size, per_device, runs_per_dev, RUN)....  23.6 us
    pallas_call x1, Pallas kernels, propagate(): pl.pallas_call(propagate_kernel, out_shape=jax.ShapeDtypeStruct(recv.shap...  16.1 us
    all_to_all x1, starting transfers between devices, on_device(): lax.all_to_all(forced.reshape(group_size, per_device, runs_per_dev, RUN)....  12 us
    unnamed x20, local copies, waits for them, and re-layouts  2.57 us
  transfers between devices with their start and end apart: 1, of which 1 were waited for; matrix products, arithmetic and copies ran while one was open for 6% of the time, Pallas kernels for 0%

profile of v7, /device:TPU:1, one launch (start us, length us, event | category | flops | bytes accessed | tf_op | source)
XLA Modules:
  0.0 101.6 jit_solution(2504857663893175804)
XLA Ops:
  0.6 0.0 copy-start
  0.6 0.0 copy-start.2
  0.7 0.0 copy-start.5
  0.7 0.0 copy-start.6
  0.7 0.0 copy-start.8
  0.7 0.0 copy-start.7
  0.7 1.9 %reduce_sum.28 = f32[1024]{0:T(1024)S(1)} reduce(f32[512,1024]{1,0:T(8,128)} %param.9, f32[]{:T(128)} %constant.73.clone.1), dimensions={0}, to_apply=%region_1.2 | reduce | flops 523264 | bytes 2101252 | tf_op jit(solution)/shard_map/reduce_sum | solution.py:22
  2.6 0.0 copy-done.5
  2.6 0.3 copy-done.2
  2.9 0.0 copy-done.6
  2.9 0.0 copy-done.8
  2.9 0.0 copy-done.7
  2.9 0.8 multiply_bitcast_fusion
  3.7 0.5 copy.31
  4.2 1.9 %copy.36 = f32[128,4,8,128]{3,1,2,0:T(4,128)} copy(f32[128,4,8,128]{3,2,1,0:T(8,128)S(1)} %bitcast.42) | data formatting | bytes 4194304 | tf_op jit(solution)/shard_map/reshape | solution.py:118
  6.1 0.0 copy-start.1
  6.1 0.0 copy-start.3
  6.1 12.0 %all-to-all-start = ((f32[128,8,4,128]{3,2,1,0:T(4,128)}), f32[128,8,4,128]{3,2,1,0:T(4,128)}, u32[]{:S(2)}, u32[]{:S(2)}) async-start(f32[128,8,4,128]{3,2,1,0:T(4,128)} %bitcast.40), calls=%async_computation | async-start | bytes 4194304 | tf_op jit(solution)/shard_map/all_to_all | solution.py:117
  18.1 0.0 copy-done.1
  18.1 0.6 gather_fusion
  18.8 0.0 copy-done
  18.8 0.6 gather_fusion.1
  19.4 0.1 compare_convert_fusion
  19.5 0.1 fusion.9
  19.5 0.1 copy.26
  19.7 0.1 copy.27
  19.7 0.0 copy-done.3
  19.8 0.4 copy.29
  20.2 0.6 broadcast_in_dim.47
  20.8 0.0 copy-start.4
  20.8 1.7 %reshape.253 = f32[8,128,512]{2,0,1:T(8,128)} reshape(f32[2,4,128,512]{3,1,0,2:T(4,128)S(1)} %broadcast_in_dim.47) | data formatting | bytes 4194304 | tf_op jit(solution)/shard_map/reshape | solution.py:138
  22.6 0.0 copy-done.4
  22.6 0.2 slice_reduce_fusion
  22.8 1.1 %select_reduce_fusion.inv_ref = s32[1024]{0:T(1024)} fusion(s32[1024]{0:T(1024)S(1)} %add_select_fusion), kind=kLoop, calls=%fused_computation.2 | loop fusion | flops 3144704 | bytes 8192 | tf_op jit(solution)/shard_map/reduce_sum | solution.py:141
  23.9 23.6 %all-to-all-done = f32[128,8,4,128]{3,2,1,0:T(4,128)} async-done(((f32[128,8,4,128]{3,2,1,0:T(4,128)}), f32[128,8,4,128]{3,2,1,0:T(4,128)}, u32[]{:S(2)}, u32[]{:S(2)}) %all-to-all-start) | async-done | bytes 2097184 | tf_op jit(solution)/shard_map/all_to_all | solution.py:117
  47.5 0.7 broadcast_in_dim.24.coef_ref
  48.1 16.1 %shard_map.104 = f32[1024,4,128]{2,1,0:T(4,128)} custom-call(s32[1024]{0:T(1024)} %select_reduce_fusion.inv_ref, f32[5,8,512]{2,1,0:T(8,128)} %broadcast_in_dim.24.coef_ref, f32[1024,4,128]{2,1,0:T(4,128)} %bitcast.7.recv_ref, f32[128,8,512]{2,1,0:T(8,128)} %bitcast.44), custom_call_target="tpu_custom_call" | custom-call | tf_op jit(solution)/shard_map/pallas_call | solution.py:95
  64.2 34.6 %all_to_all.10 = f32[128,8,4,128]{3,2,1,0:T(4,128)S(1)} all-to-all(f32[128,8,4,128]{3,2,1,0:T(4,128)} %bitcast.45), channel_id=1, replica_groups=mesh['pt'=8,'comp'=16] {'pt','comp'}, dimensions={0} | all-to-all | bytes 4194304 | tf_op jit(solution)/shard_map/all_to_all | solution.py:144
  98.8 0.2 copy.30
  99.0 1.8 %copy.35 = f32[64,8,8,128]{3,1,2,0:T(8,128)} copy(f32[64,8,8,128]{3,2,1,0:T(8,128)S(1)} %bitcast.43) | data formatting | bytes 4194304
  100.8 0.3 bitcast_reduce_fusion
  101.0 0.6 multiply_bitcast_fusion.1
  (10 shorter events, 0.1 us)
Async XLA Ops:
  0.6 18.1 %copy-start = (s32[512]{0:T(512)S(1)}, s32[512]{0:T(512)}, u32[]{:S(2)}) copy-start(s32[512]{0:T(512)} %param.14) | copy-start | bytes 6148
  0.6 2.2 %copy-start.2 = (f32[512,1024]{1,0:T(8,128)S(1)}, f32[512,1024]{1,0:T(8,128)}, u32[]{:S(2)}) copy-start(f32[512,1024]{1,0:T(8,128)} %param.9) | copy-start | bytes 6291460
  0.7 1.9 %copy-start.5 = (s32[1024]{0:T(1024)S(1)}, s32[1024]{0:T(1024)}, u32[]{:S(2)}) copy-start(s32[1024]{0:T(1024)} %param.15) | copy-start | bytes 12292
  0.7 2.2 %copy-start.6 = (f32[1024]{0:T(1024)S(1)}, f32[1024]{0:T(1024)}, u32[]{:S(2)}) copy-start(f32[1024]{0:T(1024)} %param.10) | copy-start | bytes 12292
  0.7 2.2 %copy-start.8 = (f32[512]{0:T(512)S(1)}, f32[512]{0:T(512)}, u32[]{:S(2)}) copy-start(f32[512]{0:T(512)} %param.11) | copy-start | bytes 6148
  0.7 2.2 %copy-start.7 = (f32[512]{0:T(512)S(1)}, f32[512]{0:T(512)}, u32[]{:S(2)}) copy-start(f32[512]{0:T(512)} %param.12) | copy-start | bytes 6148
  6.1 12.0 %copy-start.1 = (f32[16]{0:T(128)S(1)}, f32[16]{0:T(128)}, u32[]{:S(2)}) copy-start(f32[16]{0:T(128)} %param.13) | copy-start | bytes 196
  6.1 13.7 %copy-start.3 = (s32[256,512]{1,0:T(8,128)S(1)}, s32[256,512]{1,0:T(8,128)}, u32[]{:S(2)}) copy-start(s32[256,512]{1,0:T(8,128)} %param.17) | copy-start | bytes 1572868
  6.1 41.4 %all-to-all-start = ((f32[128,8,4,128]{3,2,1,0:T(4,128)}), f32[128,8,4,128]{3,2,1,0:T(4,128)}, u32[]{:S(2)}, u32[]{:S(2)}) async-start(f32[128,8,4,128]{3,2,1,0:T(4,128)} %bitcast.40), calls=%async_computation | async-start | bytes 4194304 | tf_op jit(solution)/shard_map/all_to_all | solution.py:117
  20.8 1.7 %copy-start.4 = (s32[131072]{0:T(1024)S(1)}, s32[131072]{0:T(1024)}, u32[]{:S(2)}) copy-start(s32[131072]{0:T(1024)} %param.16) | copy-start | bytes 1572868

commit v8 on v7

--- a/solution.py
+++ b/solution.py
@@ -10,8 +10,10 @@
 
 DIRS = 32
 MAXSUB = 8
+CHUNKS = 2
 RUN = 128
 SUB = 8
+CHUNKS = 2
 
 
 rate_limit = 0.5
@@ -58,6 +60,7 @@
     cnt = coef_ref[4]
     sub_id = lax.broadcasted_iota(jnp.int32, (SUB, cols), 0)
     low = sub_id < comps
+    high = sub_id >= SUB - comps
     for n in range(MAXSUB):
         src, dst = n % 2, (n + 1) % 2
         active = cnt > n
@@ -74,7 +77,7 @@
             else:
                 prev = sea_of(i - 1)
             if i == half - 1:
-                nxt = jnp.where(low, pltpu.roll(sea_of(0), comps, 0), 0.0)
+                nxt = jnp.where(high, 0.0, pltpu.roll(sea_of(0), SUB - comps, 0))
             else:
                 nxt = sea_of(i + 1)
             f = buf_ref[src, i]
@@ -114,34 +117,38 @@
     cols_grid = wet.shape[1]
     run_count = all_points // RUN
     runs_per_dev = point_count // RUN
-    fields = lax.all_to_all(
-        forced.reshape(group_size, per_device, runs_per_dev, RUN).transpose(0, 2, 1, 3),
-        ("pt", "comp"),
-        split_axis=0,
-        concat_axis=0,
-        tiled=True,
-    )
+    chunk = per_device // CHUNKS
     own_rank = lax.axis_index("pt") * comp_count + lax.axis_index("comp")
-    comps = own_rank * per_device + jnp.arange(per_device, dtype=jnp.int32)
-    angle = 2.0 * math.pi / DIRS * ((comps % DIRS).astype(jnp.float32) + 0.5)
-    speed = courant[comps // DIRS]
-    cross = speed * jnp.sin(angle)
-    along = speed * jnp.cos(angle)
-    counts = substeps[comps]
-    halves = SUB // per_device
+    halves = SUB // chunk
     half = rows_grid // halves
-    lane_rows = jnp.stack([jnp.abs(cross), jnp.abs(along), (cross > 0).astype(jnp.float32),
-                           (along > 0).astype(jnp.float32), counts.astype(jnp.float32)])
-    coef = jnp.broadcast_to(jnp.tile(lane_rows, (1, halves))[:, :, None], (5, SUB, cols_grid))
     wet_h = jnp.broadcast_to(
-        wet.astype(jnp.float32).reshape(halves, 1, half, cols_grid), (halves, per_device, half, cols_grid)
+        wet.astype(jnp.float32).reshape(halves, 1, half, cols_grid), (halves, chunk, half, cols_grid)
     ).reshape(SUB, half, cols_grid).transpose(1, 0, 2)
     slot_runs = deck.reshape(run_count, RUN)[:, 0] // RUN
     run_ids = jnp.arange(run_count, dtype=jnp.int32)
     inv = jnp.sum(jnp.where(slot_runs[None, :] == run_ids[:, None], run_ids[None, :], 0), axis=1)
-    slots = propagate(inv, coef, fields.reshape(run_count, per_device, RUN), wet_h)
-    slots = slots.reshape(fields.shape)
-    back = lax.all_to_all(slots, ("pt", "comp"), split_axis=0, concat_axis=0, tiled=True)
+    per_point = forced.reshape(group_size, per_device, runs_per_dev, RUN)
+    results = []
+    for part in range(CHUNKS):
+        fields = lax.all_to_all(
+            per_point[:, part * chunk:(part + 1) * chunk].transpose(0, 2, 1, 3),
+            ("pt", "comp"),
+            split_axis=0,
+            concat_axis=0,
+            tiled=True,
+        )
+        comps = own_rank * per_device + part * chunk + jnp.arange(chunk, dtype=jnp.int32)
+        angle = 2.0 * math.pi / DIRS * ((comps % DIRS).astype(jnp.float32) + 0.5)
+        speed = courant[comps // DIRS]
+        cross = speed * jnp.sin(angle)
+        along = speed * jnp.cos(angle)
+        counts = substeps[comps]
+        lane_rows = jnp.stack([jnp.abs(cross), jnp.abs(along), (cross > 0).astype(jnp.float32),
+                               (along > 0).astype(jnp.float32), counts.astype(jnp.float32)])
+        coef = jnp.broadcast_to(jnp.tile(lane_rows, (1, halves))[:, :, None], (5, SUB, cols_grid))
+        slots = propagate(inv, coef, fields.reshape(run_count, chunk, RUN), wet_h)
+        results.append(lax.all_to_all(slots.reshape(fields.shape), ("pt", "comp"), split_axis=0, concat_axis=0, tiled=True))
+    back = jnp.concatenate(results, axis=2)
     arrived = back.transpose(0, 2, 1, 3).reshape(total_comps, point_count)
     height = 4.0 * jnp.sqrt(jnp.mean(arrived, axis=0) + 1e-06)
     return (arrived, height)

time: 102 us -> 114 us (1.12)
  starting transfers between devices: 12 us -> 23.5 us
  blocking collectives: 34.6 us -> 23.9 us
  local copies, waits for them, and re-layouts: 9.73 us -> 14 us
  Pallas kernels: 16.1 us -> 20 us
  other arithmetic: 4.91 us -> 6.79 us
  waiting for transfers between devices: 23.6 us -> 24.8 us
    all_to_all x1 -> x3, starting transfers between devices: 12 us -> 23.5 us  [the longest x2 16.4 us: on_device(): lax.all_to_all(per_point[:, part * chunk:(part + 1) * chunk].transpose(0,...]
    all_to_all x1, blocking collectives: 34.6 us -> 23.9 us  [on_device(): lax.all_to_all(slots.reshape(fields.shape), ('pt', 'comp'), split_axis=0,...]
    pallas_call x1 -> x2, Pallas kernels: 16.1 us -> 20 us  [propagate(): pl.pallas_call(propagate_kernel, out_shape=jax.ShapeDtypeStruct(recv.shap...]
    unnamed x20 -> x26, local copies, waits for them, and re-layouts: 2.57 us -> 5.61 us
    reshape x1 -> x0, local copies, waits for them, and re-layouts: 1.86 us -> none  [on_device(): forced.reshape(group_size, per_device, runs_per_dev, RUN)]
    all_to_all x1 -> x3, waiting for transfers between devices: 23.6 us -> 24.8 us  [the longest x2 19 us: on_device(): lax.all_to_all(per_point[:, part * chunk:(part + 1) * chunk].transpose(0,...]
  transfers between devices with their start and end apart: 1 -> 3, of which waited for: 1 -> 3; matrix products, arithmetic and copies ran while one was open for 6% -> 10% of each run, Pallas kernels for 0% -> 18%
where the time goes in v8:
time: 114 us
  waiting for transfers between devices  24.8 us (22%)
  blocking collectives  23.9 us (21%)
  starting transfers between devices  23.5 us (21%)
  Pallas kernels  20 us (18%)
  local copies, waits for them, and re-layouts  14 us (12%)
  other arithmetic  6.79 us (6%)
    all_to_all x1, blocking collectives, on_device(): lax.all_to_all(slots.reshape(fields.shape), ('pt', 'comp'), split_axis=0,...  23.9 us
    pallas_call x2, Pallas kernels, propagate(): pl.pallas_call(propagate_kernel, out_shape=jax.ShapeDtypeStruct(recv.shap...  20 us
    all_to_all x2, waiting for transfers between devices, on_device(): lax.all_to_all(per_point[:, part * chunk:(part + 1) * chunk].transpose(0,...  19 us
    all_to_all x2, starting transfers between devices, on_device(): lax.all_to_all(per_point[:, part * chunk:(part + 1) * chunk].transpose(0,...  16.4 us
    all_to_all x1, starting transfers between devices, on_device(): lax.all_to_all(slots.reshape(fields.shape), ('pt', 'comp'), split_axis=0,...  7.1 us
    all_to_all x1, waiting for transfers between devices, on_device(): lax.all_to_all(slots.reshape(fields.shape), ('pt', 'comp'), split_axis=0,...  5.8 us
    unnamed x26, local copies, waits for them, and re-layouts  5.61 us
  transfers between devices with their start and end apart: 3, of which 3 were waited for; matrix products, arithmetic and copies ran while one was open for 10% of the time, Pallas kernels for 18%

profile of v8, /device:TPU:1, one launch (start us, length us, event | category | flops | bytes accessed | tf_op | source)
XLA Modules:
  0.0 113.9 jit_solution(14052920973301755247)
XLA Ops:
  0.6 0.0 copy-start
  0.6 0.0 copy-start.2
  0.7 0.0 copy-start.7
  0.7 0.0 copy-start.8
  0.7 0.0 copy-start.10
  0.7 0.0 copy-start.9
  0.7 1.9 %reduce_sum.28 = f32[1024]{0:T(1024)S(1)} reduce(f32[512,1024]{1,0:T(8,128)} %param.9, f32[]{:T(128)} %constant.86.clone.1), dimensions={0}, to_apply=%region_1.2 | reduce | flops 523264 | bytes 2101252 | tf_op jit(solution)/shard_map/reduce_sum | solution.py:24
  2.6 0.0 copy-done.7
  2.6 0.3 copy-done.2
  2.9 0.0 copy-done.8
  2.9 0.0 copy-done.10
  2.9 0.0 copy-done.9
  2.9 0.8 multiply_bitcast_fusion
  3.7 0.5 copy.69
  4.2 0.1 fusion.19
  4.4 0.0 copy-start.1
  4.4 1.5 %copy.75 = f32[128,2,8,128]{3,1,2,0:T(2,128)} copy(f32[128,2,8,128]{3,2,1,0:T(8,128)S(1)} %get-tuple-element.3) | data formatting | bytes 2097152
  5.9 11.5 %all-to-all-start.2 = ((f32[128,8,2,128]{3,2,1,0:T(2,128)}), f32[128,8,2,128]{3,2,1,0:T(2,128)S(1)}, u32[]{:S(2)}, u32[]{:S(2)}) async-start(f32[128,8,2,128]{3,2,1,0:T(2,128)} %bitcast.64), calls=%async_computation.2 | async-start | bytes 2097152 | tf_op jit(solution)/shard_map/all_to_all | solution.py:133
  17.4 0.0 copy-done.1
  17.4 0.6 gather_fusion.2
  18.1 0.1 fusion.17
  18.1 0.1 copy.59
  18.2 0.1 copy.60
  18.3 1.5 %copy.76 = f32[128,2,8,128]{3,1,2,0:T(2,128)} copy(f32[128,2,8,128]{3,2,1,0:T(8,128)S(1)} %get-tuple-element.2) | data formatting | bytes 2097152
  19.8 16.1 %all-to-all-done.2 = f32[128,8,2,128]{3,2,1,0:T(2,128)S(1)} async-done(((f32[128,8,2,128]{3,2,1,0:T(2,128)}), f32[128,8,2,128]{3,2,1,0:T(2,128)S(1)}, u32[]{:S(2)}, u32[]{:S(2)}) %all-to-all-start.2) | async-done | bytes 1048608 | tf_op jit(solution)/shard_map/all_to_all | solution.py:133
  36.0 4.9 %all-to-all-start = ((f32[128,8,2,128]{3,2,1,0:T(2,128)}), f32[128,8,2,128]{3,2,1,0:T(2,128)S(1)}, u32[]{:S(2)}, u32[]{:S(2)}) async-start(f32[128,8,2,128]{3,2,1,0:T(2,128)} %bitcast.65), calls=%async_computation | async-start | bytes 2097152 | tf_op jit(solution)/shard_map/all_to_all | solution.py:133
  40.9 0.1 compare_convert_fusion
  41.0 0.1 copy.61
  41.1 0.1 copy.62
  41.2 0.6 gather_fusion.3
  41.8 0.1 copy.63
  41.9 0.1 stack.5
  42.0 0.1 copy.64
  42.1 0.0 copy-done.5
  42.2 0.3 copy.58
  42.5 0.6 broadcast_in_dim.33
  43.1 0.0 copy-start.6
  43.1 1.7 %reshape.439 = f32[8,64,512]{2,0,1:T(8,128)} reshape(f32[4,2,64,512]{3,1,0,2:T(2,128)S(1)} %broadcast_in_dim.33) | data formatting | bytes 2097152 | tf_op jit(solution)/shard_map/reshape | solution.py:126
  44.8 0.2 slice_reduce_fusion
  45.1 1.1 select_reduce_fusion.inv_ref
  46.2 0.7 broadcast_in_dim.34.coef_ref
  46.9 10.0 %shard_map.105 = f32[1024,2,128]{2,1,0:T(2,128)} custom-call(s32[1024]{0:T(1024)} %select_reduce_fusion.inv_ref, f32[5,8,512]{2,1,0:T(8,128)} %broadcast_in_dim.34.coef_ref, f32[1024,2,128]{2,1,0:T(2,128)} %bitcast.71, f32[64,8,512]{2,1,0:T(8,128)} %bitcast.66), custom_call_target="tpu_custom_call" | custom-call | tf_op jit(solution)/shard_map/pallas_call | solution.py:98
  56.9 2.8 %all-to-all-done = f32[128,8,2,128]{3,2,1,0:T(2,128)S(1)} async-done(((f32[128,8,2,128]{3,2,1,0:T(2,128)}), f32[128,8,2,128]{3,2,1,0:T(2,128)S(1)}, u32[]{:S(2)}, u32[]{:S(2)}) %all-to-all-start) | async-done | bytes 1048608 | tf_op jit(solution)/shard_map/all_to_all | solution.py:133
  59.7 7.1 %all-to-all-start.3 = ((f32[128,8,2,128]{3,2,1,0:T(2,128)}), f32[128,8,2,128]{3,2,1,0:T(2,128)S(1)}, u32[]{:S(2)}, u32[]{:S(2)}) async-start(f32[128,8,2,128]{3,2,1,0:T(2,128)} %bitcast.72), calls=%async_computation.3 | async-start | bytes 2097152 | tf_op jit(solution)/shard_map/all_to_all | solution.py:150
  66.8 0.6 gather_fusion
  67.5 0.1 fusion.15
  67.5 0.1 copy.51
  67.6 0.1 copy.52
  67.7 0.1 compare_convert_fusion.2
  67.8 0.1 copy.53
  67.9 0.1 copy.54
  68.0 0.6 gather_fusion.1
  68.6 0.1 copy.55
  68.7 0.1 stack.4
  68.8 0.1 copy.56
  68.9 0.7 broadcast_in_dim.30.coef_ref
  69.6 10.0 %shard_map.104 = f32[1024,2,128]{2,1,0:T(2,128)} custom-call(s32[1024]{0:T(1024)} %select_reduce_fusion.inv_ref, f32[5,8,512]{2,1,0:T(8,128)} %broadcast_in_dim.30.coef_ref, f32[1024,2,128]{2,1,0:T(2,128)} %bitcast.70, f32[64,8,512]{2,1,0:T(8,128)} %bitcast.67), custom_call_target="tpu_custom_call" | custom-call | tf_op jit(solution)/shard_map/pallas_call | solution.py:98
  79.6 5.8 %all-to-all-done.3 = f32[128,8,2,128]{3,2,1,0:T(2,128)S(1)} async-done(((f32[128,8,2,128]{3,2,1,0:T(2,128)}), f32[128,8,2,128]{3,2,1,0:T(2,128)S(1)}, u32[]{:S(2)}, u32[]{:S(2)}) %all-to-all-start.3) | async-done | bytes 1048608 | tf_op jit(solution)/shard_map/all_to_all | solution.py:150
  85.4 23.9 %all_to_all.20 = f32[128,8,2,128]{3,2,1,0:T(2,128)S(1)} all-to-all(f32[128,8,2,128]{3,2,1,0:T(2,128)} %bitcast.73), channel_id=1, replica_groups=mesh['pt'=8,'comp'=16] {'pt','comp'}, dimensions={0} | all-to-all | bytes 2097152 | tf_op jit(solution)/shard_map/all_to_all | solution.py:150
  109.3 1.1 fusion.18
  110.4 0.6 multiply_bitcast_fusion.1
  111.0 1.0 maximum_bitcast_fusion
  111.9 0.2 copy.66
  112.1 1.8 %copy.74 = f32[64,8,8,128]{3,1,2,0:T(8,128)} copy(f32[64,8,8,128]{3,2,1,0:T(8,128)S(1)} %bitcast.69) | data formatting | bytes 4194304
  (21 shorter events, 0.1 us)
Async XLA Ops:
  0.6 40.6 %copy-start = (s32[512]{0:T(512)S(1)}, s32[512]{0:T(512)}, u32[]{:S(2)}) copy-start(s32[512]{0:T(512)} %param.14) | copy-start | bytes 6148
  0.6 2.2 %copy-start.2 = (f32[512,1024]{1,0:T(8,128)S(1)}, f32[512,1024]{1,0:T(8,128)}, u32[]{:S(2)}) copy-start(f32[512,1024]{1,0:T(8,128)} %param.9) | copy-start | bytes 6291460
  0.7 1.9 %copy-start.7 = (s32[1024]{0:T(1024)S(1)}, s32[1024]{0:T(1024)}, u32[]{:S(2)}) copy-start(s32[1024]{0:T(1024)} %param.15) | copy-start | bytes 12292
  0.7 2.2 %copy-start.8 = (f32[1024]{0:T(1024)S(1)}, f32[1024]{0:T(1024)}, u32[]{:S(2)}) copy-start(f32[1024]{0:T(1024)} %param.10) | copy-start | bytes 12292
  0.7 2.2 %copy-start.10 = (f32[512]{0:T(512)S(1)}, f32[512]{0:T(512)}, u32[]{:S(2)}) copy-start(f32[512]{0:T(512)} %param.11) | copy-start | bytes 6148
  0.7 2.2 %copy-start.9 = (f32[512]{0:T(512)S(1)}, f32[512]{0:T(512)}, u32[]{:S(2)}) copy-start(f32[512]{0:T(512)} %param.12) | copy-start | bytes 6148
  4.4 13.1 %copy-start.1 = (f32[16]{0:T(128)S(1)}, f32[16]{0:T(128)}, u32[]{:S(2)}) copy-start(f32[16]{0:T(128)} %param.13) | copy-start | bytes 196
  5.9 30.1 %all-to-all-start.2 = ((f32[128,8,2,128]{3,2,1,0:T(2,128)}), f32[128,8,2,128]{3,2,1,0:T(2,128)S(1)}, u32[]{:S(2)}, u32[]{:S(2)}) async-start(f32[128,8,2,128]{3,2,1,0:T(2,128)} %bitcast.64), calls=%async_computation.2 | async-start | bytes 2097152 | tf_op jit(solution)/shard_map/all_to_all | solution.py:133
  18.3 23.8 %copy-start.5 = (s32[256,512]{1,0:T(8,128)S(1)}, s32[256,512]{1,0:T(8,128)}, u32[]{:S(2)}) copy-start(s32[256,512]{1,0:T(8,128)} %param.17) | copy-start | bytes 1572868
  36.0 6.5 %copy-start.4 = (f32[128,8,2,128]{3,2,1,0:T(2,128)}, f32[128,8,2,128]{3,2,1,0:T(2,128)S(1)}, u32[]{:S(2)}) copy-start(f32[128,8,2,128]{3,2,1,0:T(2,128)S(1)} %all-to-all-done.2) | copy-start | bytes 3145732
  36.0 23.7 %all-to-all-start = ((f32[128,8,2,128]{3,2,1,0:T(2,128)}), f32[128,8,2,128]{3,2,1,0:T(2,128)S(1)}, u32[]{:S(2)}, u32[]{:S(2)}) async-start(f32[128,8,2,128]{3,2,1,0:T(2,128)} %bitcast.65), calls=%async_computation | async-start | bytes 2097152 | tf_op jit(solution)/shard_map/all_to_all | solution.py:133
  43.1 1.7 %copy-start.6 = (s32[131072]{0:T(1024)S(1)}, s32[131072]{0:T(1024)}, u32[]{:S(2)}) copy-start(s32[131072]{0:T(1024)} %param.16) | copy-start | bytes 1572868
  59.7 9.9 %copy-start.3 = (f32[128,8,2,128]{3,2,1,0:T(2,128)}, f32[128,8,2,128]{3,2,1,0:T(2,128)S(1)}, u32[]{:S(2)}) copy-start(f32[128,8,2,128]{3,2,1,0:T(2,128)S(1)} %all-to-all-done) | copy-start | bytes 3145732
  59.7 25.7 %all-to-all-start.3 = ((f32[128,8,2,128]{3,2,1,0:T(2,128)}), f32[128,8,2,128]{3,2,1,0:T(2,128)S(1)}, u32[]{:S(2)}, u32[]{:S(2)}) async-start(f32[128,8,2,128]{3,2,1,0:T(2,128)} %bitcast.72), calls=%async_computation.3 | async-start | bytes 2097152 | tf_op jit(solution)/shard_map/all_to_all | solution.py:150

commit v9 on v7

--- a/solution.py
+++ b/solution.py
@@ -51,8 +51,8 @@
         lax.fori_loop(0, half, body, 0)
 
     copy_runs(True, 0)
-    ax = coef_ref[0]
-    ay = coef_ref[1]
+    ax_all = coef_ref[0]
+    ay_all = coef_ref[1]
     south = coef_ref[2] > 0
     east = coef_ref[3] > 0
     cnt = coef_ref[4]
@@ -61,6 +61,9 @@
     for n in range(MAXSUB):
         src, dst = n % 2, (n + 1) % 2
         active = cnt > n
+        ax = jnp.where(active, ax_all, 0.0)
+        ay = jnp.where(active, ay_all, 0.0)
+        keep = 1.0 - ax - ay
         sea = {}
 
         def sea_of(i):
@@ -82,8 +85,8 @@
             here = sea_of(i)
             up_row = jnp.where(south, prev, nxt)
             up_col = jnp.where(east, pltpu.roll(here, 1, 1), pltpu.roll(here, cols - 1, 1))
-            moved = f - ax * (f - up_row) - ay * (f - up_col)
-            buf_ref[dst, i] = jnp.where(active & (w > 0), moved, f)
+            moved = keep * f + ax * up_row + ay * up_col
+            buf_ref[dst, i] = jnp.where(w > 0, moved, f)
             sea.pop(i - 1, None)
     copy_runs(False, MAXSUB % 2)
 
@@ -102,20 +105,27 @@
 
 
 def on_device(spectrum, wind, growth, whitecap, courant, substeps, limiter, deck, wet):
-    forced = sources(spectrum, wind, growth, whitecap, limiter)
     pt_count = lax.axis_size("pt")
     comp_count = lax.axis_size("comp")
     group_size = pt_count * comp_count
-    total_comps = forced.shape[0]
-    point_count = forced.shape[1]
+    total_comps = spectrum.shape[0]
+    point_count = spectrum.shape[1]
     per_device = total_comps // group_size
     all_points = deck.shape[0]
     rows_grid = wet.shape[0]
     cols_grid = wet.shape[1]
     run_count = all_points // RUN
     runs_per_dev = point_count // RUN
+    mean_energy = jnp.mean(spectrum, axis=0).reshape(runs_per_dev, 1, RUN)
+    ordered = spectrum.reshape(group_size, per_device, runs_per_dev, RUN).transpose(0, 2, 1, 3)
+    rate = (
+        wind.reshape(runs_per_dev, 1, RUN) * growth.reshape(group_size, 1, per_device, 1)
+        - whitecap.reshape(group_size, 1, per_device, 1) * (mean_energy / (1.0 + mean_energy))
+    )
+    rate = jnp.where(limiter.reshape(runs_per_dev, 1, RUN) == 1, rate_limit * jnp.tanh(rate / rate_limit), rate)
+    forced = ordered * jnp.exp(time_step * rate)
     fields = lax.all_to_all(
-        forced.reshape(group_size, per_device, runs_per_dev, RUN).transpose(0, 2, 1, 3),
+        forced,
         ("pt", "comp"),
         split_axis=0,
         concat_axis=0,

time: 102 us -> 103 us (level)
  other arithmetic: 4.91 us -> 6.62 us
    mul x0 -> x1, other arithmetic: none -> 2.68 us  [on_device(): forced = ordered * jnp.exp(time_step * rate)]
    reshape x1 -> x0, local copies, waits for them, and re-layouts: 1.86 us -> none  [on_device(): forced.reshape(group_size, per_device, runs_per_dev, RUN)]
    unnamed x20 -> x18, local copies, waits for them, and re-layouts: 2.57 us -> 3.9 us
where the time goes in v9:
time: 103 us
  blocking collectives  34.6 us (34%)
  waiting for transfers between devices  23.6 us (23%)
  Pallas kernels  16 us (16%)
  starting transfers between devices  12 us (12%)
  local copies, waits for them, and re-layouts  9.42 us (9%)
  other arithmetic  6.62 us (6%)
    all_to_all x1, blocking collectives, on_device(): lax.all_to_all(slots, ('pt', 'comp'), split_axis=0, concat_axis=0, tiled=...  34.6 us
    all_to_all x1, waiting for transfers between devices, on_device(): lax.all_to_all(forced, ('pt', 'comp'), split_axis=0, concat_axis=0, tiled...  23.6 us
    pallas_call x1, Pallas kernels, propagate(): pl.pallas_call(propagate_kernel, out_shape=jax.ShapeDtypeStruct(recv.shap...  16 us
    all_to_all x1, starting transfers between devices, on_device(): lax.all_to_all(forced, ('pt', 'comp'), split_axis=0, concat_axis=0, tiled...  12 us
    unnamed x18, local copies, waits for them, and re-layouts  3.9 us
    mul x1, other arithmetic, on_device(): forced = ordered * jnp.exp(time_step * rate)  2.68 us
  transfers between devices with their start and end apart: 1, of which 1 were waited for; matrix products, arithmetic and copies ran while one was open for 6% of the time, Pallas kernels for 0%

profile of v9, /device:TPU:1, one launch (start us, length us, event | category | flops | bytes accessed | tf_op | source)
XLA Modules:
  0.0 103.0 jit_solution(17751038617452723311)
XLA Ops:
  0.6 0.0 copy-start
  0.6 2.1 %copy.31 = f32[64,8,8,128]{3,2,1,0:T(8,128)S(1)} copy(f32[64,8,8,128]{3,1,2,0:T(8,128)} %bitcast.46) | data formatting | bytes 4194304
  2.7 0.0 copy-start.6
  2.7 0.0 copy-start.7
  2.7 0.0 copy-start.5
  2.7 0.0 copy-start.4
  2.8 1.8 %reduce_sum.28 = f32[1024]{0:T(1024)S(1)} reduce(f32[512,1024]{1,0:T(8,128)} %param.9, f32[]{:T(128)} %constant.73.clone.1), dimensions={0}, to_apply=%region_1.2 | reduce | flops 523264 | bytes 2101252 | tf_op jit(solution)/shard_map/reduce_sum | solution.py:119
  4.5 0.0 copy-done.6
  4.5 0.1 mul.116
  4.6 0.0 copy-done.7
  4.7 0.1 mul.113
  4.8 0.0 copy-done.5
  4.8 0.0 copy-done.4
  4.8 2.7 %bitcast_multiply_fusion = f32[128,8,4,128]{3,2,1,0:T(4,128)} fusion(f32[128,4,8,128]{3,2,1,0:T(8,128)S(1)} %bitcast.45, f32[8,128]{1,0:T(8,128)S(1)} %add_divide_fusion, f32[128,4]{1,0:T(8,128)S(1)} %mul.116, f32[128,4]{1,0:T(8,128)S(1)} %mul.113, f32[8,128]{1,0:T(8,128)S(1)} %bitcast.54, pred[8,128]{1,0:T(8,128)(4,1)S(1)} %compare_bitcast_fusion), kind=kLoop, calls=%fused_computation.5 | loop fusion | flops 4194304 | bytes 4207616 | tf_op jit(solution)/shard_map/mul | solution.py:126
  7.5 0.0 copy-start.1
  7.5 0.0 copy-start.2
  7.5 12.0 %all-to-all-start = ((f32[128,8,4,128]{3,2,1,0:T(4,128)}), f32[128,8,4,128]{3,2,1,0:T(4,128)}, u32[]{:S(2)}, u32[]{:S(2)}) async-start(f32[128,8,4,128]{3,2,1,0:T(4,128)} %bitcast_multiply_fusion), calls=%async_computation | async-start | bytes 4194304 | tf_op jit(solution)/shard_map/all_to_all | solution.py:127
  19.5 0.0 copy-done.1
  19.5 0.6 gather_fusion
  20.2 0.0 copy-done
  20.2 0.6 gather_fusion.1
  20.8 0.1 fusion.9
  20.9 0.1 compare_convert_fusion
  20.9 0.1 copy.26
  21.1 0.1 copy.27
  21.1 0.0 copy-done.2
  21.2 0.4 copy.29
  21.6 0.6 broadcast_in_dim.43
  22.2 0.0 copy-start.3
  22.2 1.7 %reshape.275 = f32[8,128,512]{2,0,1:T(8,128)} reshape(f32[2,4,128,512]{3,1,0,2:T(4,128)S(1)} %broadcast_in_dim.43) | data formatting | bytes 4194304 | tf_op jit(solution)/shard_map/reshape | solution.py:148
  24.0 0.0 copy-done.3
  24.0 0.2 slice_reduce_fusion
  24.2 1.1 %select_reduce_fusion.inv_ref = s32[1024]{0:T(1024)} fusion(s32[1024]{0:T(1024)S(1)} %add_select_fusion), kind=kLoop, calls=%fused_computation.2 | loop fusion | flops 3144704 | bytes 8192 | tf_op jit(solution)/shard_map/reduce_sum | solution.py:151
  25.3 23.6 %all-to-all-done = f32[128,8,4,128]{3,2,1,0:T(4,128)} async-done(((f32[128,8,4,128]{3,2,1,0:T(4,128)}), f32[128,8,4,128]{3,2,1,0:T(4,128)}, u32[]{:S(2)}, u32[]{:S(2)}) %all-to-all-start) | async-done | bytes 2097184 | tf_op jit(solution)/shard_map/all_to_all | solution.py:127
  48.9 0.7 broadcast_in_dim.40.coef_ref
  49.6 16.0 %shard_map.104 = f32[1024,4,128]{2,1,0:T(4,128)} custom-call(s32[1024]{0:T(1024)} %select_reduce_fusion.inv_ref, f32[5,8,512]{2,1,0:T(8,128)} %broadcast_in_dim.40.coef_ref, f32[1024,4,128]{2,1,0:T(4,128)} %bitcast.10.recv_ref, f32[128,8,512]{2,1,0:T(8,128)} %bitcast.48), custom_call_target="tpu_custom_call" | custom-call | tf_op jit(solution)/shard_map/pallas_call | solution.py:98
  65.5 34.6 %all_to_all.10 = f32[128,8,4,128]{3,2,1,0:T(4,128)S(1)} all-to-all(f32[128,8,4,128]{3,2,1,0:T(4,128)} %bitcast.49), channel_id=1, replica_groups=mesh['pt'=8,'comp'=16] {'pt','comp'}, dimensions={0} | all-to-all | bytes 4194304 | tf_op jit(solution)/shard_map/all_to_all | solution.py:154
  100.1 0.2 copy.30
  100.3 1.8 %copy.35 = f32[64,8,8,128]{3,1,2,0:T(8,128)} copy(f32[64,8,8,128]{3,2,1,0:T(8,128)S(1)} %bitcast.47) | data formatting | bytes 4194304
  102.1 0.3 bitcast_reduce_fusion
  102.4 0.6 multiply_bitcast_fusion
  (10 shorter events, 0.1 us)
Async XLA Ops:
  0.6 19.5 %copy-start = (s32[512]{0:T(512)S(1)}, s32[512]{0:T(512)}, u32[]{:S(2)}) copy-start(s32[512]{0:T(512)} %param.14) | copy-start | bytes 6148
  2.7 1.8 %copy-start.6 = (f32[512]{0:T(512)S(1)}, f32[512]{0:T(512)}, u32[]{:S(2)}) copy-start(f32[512]{0:T(512)} %param.12) | copy-start | bytes 6148
  2.7 1.9 %copy-start.7 = (f32[512]{0:T(512)S(1)}, f32[512]{0:T(512)}, u32[]{:S(2)}) copy-start(f32[512]{0:T(512)} %param.11) | copy-start | bytes 6148
  2.7 2.0 %copy-start.5 = (s32[1024]{0:T(1024)S(1)}, s32[1024]{0:T(1024)}, u32[]{:S(2)}) copy-start(s32[1024]{0:T(1024)} %param.15) | copy-start | bytes 12292
  2.7 2.0 %copy-start.4 = (f32[1024]{0:T(1024)S(1)}, f32[1024]{0:T(1024)}, u32[]{:S(2)}) copy-start(f32[1024]{0:T(1024)} %param.10) | copy-start | bytes 12292
  7.5 12.0 %copy-start.1 = (f32[16]{0:T(128)S(1)}, f32[16]{0:T(128)}, u32[]{:S(2)}) copy-start(f32[16]{0:T(128)} %param.13) | copy-start | bytes 196
  7.5 13.7 %copy-start.2 = (s32[256,512]{1,0:T(8,128)S(1)}, s32[256,512]{1,0:T(8,128)}, u32[]{:S(2)}) copy-start(s32[256,512]{1,0:T(8,128)} %param.17) | copy-start | bytes 1572868
  7.5 41.4 %all-to-all-start = ((f32[128,8,4,128]{3,2,1,0:T(4,128)}), f32[128,8,4,128]{3,2,1,0:T(4,128)}, u32[]{:S(2)}, u32[]{:S(2)}) async-start(f32[128,8,4,128]{3,2,1,0:T(4,128)} %bitcast_multiply_fusion), calls=%async_computation | async-start | bytes 4194304 | tf_op jit(solution)/shard_map/all_to_all | solution.py:127
  22.2 1.7 %copy-start.3 = (s32[131072]{0:T(1024)S(1)}, s32[131072]{0:T(1024)}, u32[]{:S(2)}) copy-start(s32[131072]{0:T(1024)} %param.16) | copy-start | bytes 1572868

commit v10 on v7

--- a/solution.py
+++ b/solution.py
@@ -28,7 +28,7 @@
     return spectrum * jnp.exp(time_step * rate)
 
 
-def propagate_kernel(inv_ref, coef_ref, recv_ref, wet_ref, out_ref, buf_ref):
+def propagate_kernel(inv_ref, shift_ref, coef_ref, recv_ref, wet_ref, out_ref, buf_ref):
     comps = recv_ref.shape[1]
     half = wet_ref.shape[0]
     cols = wet_ref.shape[2]
@@ -48,13 +48,13 @@
                         out_ref[s] = buf_ref[slot, i, rows, lanes]
             return carry
 
-        lax.fori_loop(0, half, body, 0)
+        lax.fori_loop(0, half, body, 0, unroll=8)
 
     copy_runs(True, 0)
     ax = coef_ref[0]
     ay = coef_ref[1]
     south = coef_ref[2] > 0
-    east = coef_ref[3] > 0
+    shift = shift_ref[0]
     cnt = coef_ref[4]
     sub_id = lax.broadcasted_iota(jnp.int32, (SUB, cols), 0)
     low = sub_id < comps
@@ -62,10 +62,12 @@
         src, dst = n % 2, (n + 1) % 2
         active = cnt > n
         sea = {}
+        vals = {}
 
         def sea_of(i):
             if i not in sea:
-                sea[i] = buf_ref[src, i] * wet_ref[i]
+                vals[i] = (buf_ref[src, i], wet_ref[i])
+                sea[i] = vals[i][0] * vals[i][1]
             return sea[i]
 
         for i in range(half):
@@ -77,28 +79,28 @@
                 nxt = jnp.where(low, pltpu.roll(sea_of(0), comps, 0), 0.0)
             else:
                 nxt = sea_of(i + 1)
-            f = buf_ref[src, i]
-            w = wet_ref[i]
             here = sea_of(i)
+            f, w = vals[i]
             up_row = jnp.where(south, prev, nxt)
-            up_col = jnp.where(east, pltpu.roll(here, 1, 1), pltpu.roll(here, cols - 1, 1))
+            up_col = pltpu.roll(here, shift, 1)
             moved = f - ax * (f - up_row) - ay * (f - up_col)
             buf_ref[dst, i] = jnp.where(active & (w > 0), moved, f)
             sea.pop(i - 1, None)
+            vals.pop(i - 1, None)
     copy_runs(False, MAXSUB % 2)
 
 
-def propagate(inv, coef, recv, wet_h):
+def propagate(inv, shift, coef, recv, wet_h):
     half, _, cols = wet_h.shape
     smem = pl.BlockSpec(memory_space=pltpu.SMEM)
     vmem = pl.BlockSpec(memory_space=pltpu.VMEM)
     return pl.pallas_call(
         propagate_kernel,
         out_shape=jax.ShapeDtypeStruct(recv.shape, recv.dtype),
-        in_specs=[smem] + [vmem] * 3,
+        in_specs=[smem] * 2 + [vmem] * 3,
         out_specs=vmem,
         scratch_shapes=[pltpu.VMEM((2, half, SUB, cols), jnp.float32)],
-    )(inv, coef, recv, wet_h)
+    )(inv, shift, coef, recv, wet_h)
 
 
 def on_device(spectrum, wind, growth, whitecap, courant, substeps, limiter, deck, wet):
@@ -139,7 +141,8 @@
     slot_runs = deck.reshape(run_count, RUN)[:, 0] // RUN
     run_ids = jnp.arange(run_count, dtype=jnp.int32)
     inv = jnp.sum(jnp.where(slot_runs[None, :] == run_ids[:, None], run_ids[None, :], 0), axis=1)
-    slots = propagate(inv, coef, fields.reshape(run_count, per_device, RUN), wet_h)
+    shift = jnp.where(along[:1] > 0, 1, cols_grid - 1).astype(jnp.int32)
+    slots = propagate(inv, shift, coef, fields.reshape(run_count, per_device, RUN), wet_h)
     slots = slots.reshape(fields.shape)
     back = lax.all_to_all(slots, ("pt", "comp"), split_axis=0, concat_axis=0, tiled=True)
     arrived = back.transpose(0, 2, 1, 3).reshape(total_comps, point_count)

time: 102 us -> 101 us (level)
  local copies, waits for them, and re-layouts: 9.73 us -> 13 us
  waiting for transfers between devices: 23.6 us -> 21.2 us
  Pallas kernels: 16.1 us -> 14.2 us
    all_to_all x1, waiting for transfers between devices: 23.6 us -> 21.2 us  [on_device(): lax.all_to_all(forced.reshape(group_size, per_device, runs_per_dev, RUN)....]
    pallas_call x1, Pallas kernels: 16.1 us -> 14.2 us  [propagate(): pl.pallas_call(propagate_kernel, out_shape=jax.ShapeDtypeStruct(recv.shap...]
    broadcast_in_dim x2, local copies, waits for them, and re-layouts: 1.02 us -> 2.34 us  [on_device(): jnp.broadcast_to(wet.astype(jnp.float32).reshape(halves, 1, half, cols_gr...]
    reshape x1, local copies, waits for them, and re-layouts: 1.73 us -> 3.03 us  [on_device(): wet_h = jnp.broadcast_to(wet.astype(jnp.float32).reshape(halves, 1, half,...]
    unnamed x20 -> x22, local copies, waits for them, and re-layouts: 2.57 us -> 3.1 us
  transfers between devices with their start and end apart: 1 -> 1, of which waited for: 1 -> 1; matrix products, arithmetic and copies ran while one was open for 6% -> 8% of each run, Pallas kernels for 0% -> 0%
where the time goes in v10:
time: 101 us; the launch traced here: 100 us
  blocking collectives  34.6 us (34%)
  waiting for transfers between devices  21.2 us (21%)
  Pallas kernels  14.2 us (14%)
  local copies, waits for them, and re-layouts  13 us (13%)
  starting transfers between devices  11.5 us (11%)
  other arithmetic  4.96 us (5%)
    all_to_all x1, blocking collectives, on_device(): lax.all_to_all(slots, ('pt', 'comp'), split_axis=0, concat_axis=0, tiled=...  34.6 us
    all_to_all x1, waiting for transfers between devices, on_device(): lax.all_to_all(forced.reshape(group_size, per_device, runs_per_dev, RUN)....  21.2 us
    pallas_call x1, Pallas kernels, propagate(): pl.pallas_call(propagate_kernel, out_shape=jax.ShapeDtypeStruct(recv.shap...  14.2 us
    all_to_all x1, starting transfers between devices, on_device(): lax.all_to_all(forced.reshape(group_size, per_device, runs_per_dev, RUN)....  11.5 us
    unnamed x22, local copies, waits for them, and re-layouts  3.1 us
    reshape x1, local copies, waits for them, and re-layouts, on_device(): wet_h = jnp.broadcast_to(wet.astype(jnp.float32).reshape(halves, 1, half,...  3.03 us
    broadcast_in_dim x2, local copies, waits for them, and re-layouts, on_device(): jnp.broadcast_to(wet.astype(jnp.float32).reshape(halves, 1, half, cols_gr...  2.34 us
  transfers between devices with their start and end apart: 1, of which 1 were waited for; matrix products, arithmetic and copies ran while one was open for 8% of the time, Pallas kernels for 0%

profile of v10, /device:TPU:1, one launch (start us, length us, event | category | flops | bytes accessed | tf_op | source)
XLA Modules:
  0.0 100.3 jit_solution(926586097069669777)
XLA Ops:
  0.6 0.0 copy-start
  0.6 0.0 copy-start.3
  0.7 0.0 copy-start.6
  0.7 0.0 copy-start.7
  0.7 0.0 copy-start.9
  0.7 0.0 copy-start.8
  0.7 1.9 %reduce_sum.28 = f32[1024]{0:T(1024)S(1)} reduce(f32[512,1024]{1,0:T(8,128)} %param.9, f32[]{:T(128)} %constant.83.clone.1), dimensions={0}, to_apply=%region_1.2 | reduce | flops 523264 | bytes 2101252 | tf_op jit(solution)/shard_map/reduce_sum | solution.py:22
  2.6 0.0 copy-done.6
  2.6 0.3 copy-done.3
  2.9 0.0 copy-done.7
  2.9 0.0 copy-done.9
  2.9 0.0 copy-done.8
  2.9 0.8 multiply_bitcast_fusion
  3.7 0.5 copy.31
  4.2 1.9 %copy.36 = f32[128,4,8,128]{3,1,2,0:T(4,128)} copy(f32[128,4,8,128]{3,2,1,0:T(8,128)S(1)} %bitcast.47) | data formatting | bytes 4194304 | tf_op jit(solution)/shard_map/reshape | solution.py:120
  6.1 0.0 copy-start.1
  6.1 0.0 copy-start.4
  6.1 11.5 %all-to-all-start = ((f32[128,8,4,128]{3,2,1,0:T(4,128)}), f32[128,8,4,128]{3,2,1,0:T(4,128)S(1)}, u32[]{:S(2)}, u32[]{:S(2)}) async-start(f32[128,8,4,128]{3,2,1,0:T(4,128)} %bitcast.46), calls=%async_computation | async-start | bytes 4194304 | tf_op jit(solution)/shard_map/all_to_all | solution.py:119
  17.6 0.0 copy-done.1
  17.6 0.6 gather_fusion
  18.3 0.0 copy-done
  18.3 0.6 gather_fusion.1
  18.9 0.1 compare_convert_fusion
  19.0 0.1 fusion.15
  19.1 0.1 copy.26
  19.2 0.1 copy.27
  19.3 0.0 copy-done.4
  19.3 0.4 copy.29
  19.7 1.9 %broadcast_in_dim.51 = f32[2,4,128,512]{3,1,0,2:T(4,128)} broadcast(f32[2,128,512]{2,0,1:T(2,128)S(1)} %copy.29), dimensions={0,2,3} | broadcast | bytes 2621440 | tf_op jit(solution)/shard_map/broadcast_in_dim | solution.py:138
  21.7 0.0 copy-start.5
  21.7 3.0 %reshape.253 = f32[8,128,512]{2,0,1:T(8,128)} reshape(f32[2,4,128,512]{3,1,0,2:T(4,128)} %broadcast_in_dim.51) | data formatting | bytes 4194304 | tf_op jit(solution)/shard_map/reshape | solution.py:140
  24.7 0.1 fusion.7
  24.8 0.0 copy-done.5
  24.8 0.2 slice_reduce_fusion
  25.0 1.1 %select_reduce_fusion.inv_ref = s32[1024]{0:T(1024)} fusion(s32[1024]{0:T(1024)S(1)} %add_select_fusion), kind=kLoop, calls=%fused_computation.2 | loop fusion | flops 3144704 | bytes 8192 | tf_op jit(solution)/shard_map/reduce_sum | solution.py:143
  26.1 21.2 %all-to-all-done = f32[128,8,4,128]{3,2,1,0:T(4,128)S(1)} async-done(((f32[128,8,4,128]{3,2,1,0:T(4,128)}), f32[128,8,4,128]{3,2,1,0:T(4,128)S(1)}, u32[]{:S(2)}, u32[]{:S(2)}) %all-to-all-start) | async-done | bytes 2097184 | tf_op jit(solution)/shard_map/all_to_all | solution.py:119
  47.4 0.0 copy-start.2
  47.4 0.8 broadcast_in_dim.30.coef_ref
  48.2 0.5 copy-done.2
  48.7 14.2 %shard_map.104 = f32[1024,4,128]{2,1,0:T(4,128)} custom-call(s32[1024]{0:T(1024)} %select_reduce_fusion.inv_ref, s32[1]{0:T(128)S(6)} %select_n.86.shift_ref, f32[5,8,512]{2,1,0:T(8,128)} %broadcast_in_dim.30.coef_ref, f32[1024,4,128]{2,1,0:T(4,128)} %bitcast.43, f32[128,8,512]{2,1,0:T(8,128)} %bitcast.44), custom_call_target="tpu_custom_call" | custom-call | tf_op jit(solution)/shard_map/pallas_call | solution.py:97
  62.9 34.6 %all_to_all.10 = f32[128,8,4,128]{3,2,1,0:T(4,128)S(1)} all-to-all(f32[128,8,4,128]{3,2,1,0:T(4,128)} %bitcast.45), channel_id=1, replica_groups=mesh['pt'=8,'comp'=16] {'pt','comp'}, dimensions={0} | all-to-all | bytes 4194304 | tf_op jit(solution)/shard_map/all_to_all | solution.py:147
  97.5 0.2 copy.30
  97.7 1.8 %copy.35 = f32[64,8,8,128]{3,1,2,0:T(8,128)} copy(f32[64,8,8,128]{3,2,1,0:T(8,128)S(1)} %bitcast.48) | data formatting | bytes 4194304
  99.5 0.3 bitcast_reduce_fusion
  99.7 0.6 multiply_bitcast_fusion.1
  (10 shorter events, 0.1 us)
Async XLA Ops:
  0.6 17.7 %copy-start = (s32[512]{0:T(512)S(1)}, s32[512]{0:T(512)}, u32[]{:S(2)}) copy-start(s32[512]{0:T(512)} %param.14) | copy-start | bytes 6148
  0.6 2.2 %copy-start.3 = (f32[512,1024]{1,0:T(8,128)S(1)}, f32[512,1024]{1,0:T(8,128)}, u32[]{:S(2)}) copy-start(f32[512,1024]{1,0:T(8,128)} %param.9) | copy-start | bytes 6291460
  0.7 1.9 %copy-start.6 = (s32[1024]{0:T(1024)S(1)}, s32[1024]{0:T(1024)}, u32[]{:S(2)}) copy-start(s32[1024]{0:T(1024)} %param.15) | copy-start | bytes 12292
  0.7 2.2 %copy-start.7 = (f32[1024]{0:T(1024)S(1)}, f32[1024]{0:T(1024)}, u32[]{:S(2)}) copy-start(f32[1024]{0:T(1024)} %param.10) | copy-start | bytes 12292
  0.7 2.2 %copy-start.9 = (f32[512]{0:T(512)S(1)}, f32[512]{0:T(512)}, u32[]{:S(2)}) copy-start(f32[512]{0:T(512)} %param.11) | copy-start | bytes 6148
  0.7 2.2 %copy-start.8 = (f32[512]{0:T(512)S(1)}, f32[512]{0:T(512)}, u32[]{:S(2)}) copy-start(f32[512]{0:T(512)} %param.12) | copy-start | bytes 6148
  6.1 11.6 %copy-start.1 = (f32[16]{0:T(128)S(1)}, f32[16]{0:T(128)}, u32[]{:S(2)}) copy-start(f32[16]{0:T(128)} %param.13) | copy-start | bytes 196
  6.1 13.2 %copy-start.4 = (s32[256,512]{1,0:T(8,128)S(1)}, s32[256,512]{1,0:T(8,128)}, u32[]{:S(2)}) copy-start(s32[256,512]{1,0:T(8,128)} %param.17) | copy-start | bytes 1572868
  6.1 41.3 %all-to-all-start = ((f32[128,8,4,128]{3,2,1,0:T(4,128)}), f32[128,8,4,128]{3,2,1,0:T(4,128)S(1)}, u32[]{:S(2)}, u32[]{:S(2)}) async-start(f32[128,8,4,128]{3,2,1,0:T(4,128)} %bitcast.46), calls=%async_computation | async-start | bytes 4194304 | tf_op jit(solution)/shard_map/all_to_all | solution.py:119
  21.7 3.1 %copy-start.5 = (s32[131072]{0:T(1024)S(1)}, s32[131072]{0:T(1024)}, u32[]{:S(2)}) copy-start(s32[131072]{0:T(1024)} %param.16) | copy-start | bytes 1572868
  47.4 1.3 %copy-start.2 = (f32[128,8,4,128]{3,2,1,0:T(4,128)}, f32[128,8,4,128]{3,2,1,0:T(4,128)S(1)}, u32[]{:S(2)}) copy-start(f32[128,8,4,128]{3,2,1,0:T(4,128)S(1)} %all-to-all-done) | copy-start | bytes 6291460

commit v11 on v10

--- a/solution.py
+++ b/solution.py
@@ -84,10 +84,17 @@
             up_row = jnp.where(south, prev, nxt)
             up_col = pltpu.roll(here, shift, 1)
             moved = f - ax * (f - up_row) - ay * (f - up_col)
-            buf_ref[dst, i] = jnp.where(active & (w > 0), moved, f)
+            result = jnp.where(active & (w > 0), moved, f)
+            if n < MAXSUB - 1:
+                buf_ref[dst, i] = result
+            else:
+                for h in range(halves):
+                    for q in range(quarters):
+                        out_ref[inv_ref[(h * half + i) * quarters + q]] = result[
+                            h * comps:(h + 1) * comps, q * RUN:(q + 1) * RUN
+                        ]
             sea.pop(i - 1, None)
             vals.pop(i - 1, None)
-    copy_runs(False, MAXSUB % 2)
 
 
 def propagate(inv, shift, coef, recv, wet_h):

time: 101 us -> 99.3 us (0.983)
  Pallas kernels: 14.2 us -> 12.9 us
    pallas_call x1, Pallas kernels: 14.2 us -> 12.9 us  [propagate(): pl.pallas_call(propagate_kernel, out_shape=jax.ShapeDtypeStruct(recv.shap...]
where the time goes in v11:
time: 99.3 us; the launch traced here: 99 us
  blocking collectives  34.6 us (35%)
  waiting for transfers between devices  21.2 us (21%)
  local copies, waits for them, and re-layouts  13 us (13%)
  Pallas kernels  12.9 us (13%)
  starting transfers between devices  11.5 us (12%)
  other arithmetic  4.96 us (5%)
    all_to_all x1, blocking collectives, on_device(): lax.all_to_all(slots, ('pt', 'comp'), split_axis=0, concat_axis=0, tiled=...  34.6 us
    all_to_all x1, waiting for transfers between devices, on_device(): lax.all_to_all(forced.reshape(group_size, per_device, runs_per_dev, RUN)....  21.2 us
    pallas_call x1, Pallas kernels, propagate(): pl.pallas_call(propagate_kernel, out_shape=jax.ShapeDtypeStruct(recv.shap...  12.9 us
    all_to_all x1, starting transfers between devices, on_device(): lax.all_to_all(forced.reshape(group_size, per_device, runs_per_dev, RUN)....  11.5 us
    unnamed x22, local copies, waits for them, and re-layouts  3.1 us
    reshape x1, local copies, waits for them, and re-layouts, on_device(): wet_h = jnp.broadcast_to(wet.astype(jnp.float32).reshape(halves, 1, half,...  3.03 us
    broadcast_in_dim x2, local copies, waits for them, and re-layouts, on_device(): jnp.broadcast_to(wet.astype(jnp.float32).reshape(halves, 1, half, cols_gr...  2.34 us
  transfers between devices with their start and end apart: 1, of which 1 were waited for; matrix products, arithmetic and copies ran while one was open for 8% of the time, Pallas kernels for 0%

profile of v11, /device:TPU:1, one launch (start us, length us, event | category | flops | bytes accessed | tf_op | source)
XLA Modules:
  0.0 99.0 jit_solution(3863724494476937)
XLA Ops:
  0.6 0.0 copy-start
  0.6 0.0 copy-start.3
  0.7 0.0 copy-start.6
  0.7 0.0 copy-start.7
  0.7 0.0 copy-start.9
  0.7 0.0 copy-start.8
  0.7 1.9 %reduce_sum.28 = f32[1024]{0:T(1024)S(1)} reduce(f32[512,1024]{1,0:T(8,128)} %param.9, f32[]{:T(128)} %constant.83.clone.1), dimensions={0}, to_apply=%region_1.2 | reduce | flops 523264 | bytes 2101252 | tf_op jit(solution)/shard_map/reduce_sum | solution.py:22
  2.6 0.0 copy-done.6
  2.6 0.3 copy-done.3
  2.9 0.0 copy-done.7
  2.9 0.0 copy-done.9
  2.9 0.0 copy-done.8
  2.9 0.8 multiply_bitcast_fusion
  3.7 0.5 copy.31
  4.2 1.9 %copy.36 = f32[128,4,8,128]{3,1,2,0:T(4,128)} copy(f32[128,4,8,128]{3,2,1,0:T(8,128)S(1)} %bitcast.47) | data formatting | bytes 4194304 | tf_op jit(solution)/shard_map/reshape | solution.py:127
  6.1 0.0 copy-start.1
  6.1 0.0 copy-start.4
  6.1 11.5 %all-to-all-start = ((f32[128,8,4,128]{3,2,1,0:T(4,128)}), f32[128,8,4,128]{3,2,1,0:T(4,128)S(1)}, u32[]{:S(2)}, u32[]{:S(2)}) async-start(f32[128,8,4,128]{3,2,1,0:T(4,128)} %bitcast.46), calls=%async_computation | async-start | bytes 4194304 | tf_op jit(solution)/shard_map/all_to_all | solution.py:126
  17.6 0.0 copy-done.1
  17.6 0.6 gather_fusion
  18.3 0.0 copy-done
  18.3 0.6 gather_fusion.1
  18.9 0.1 compare_convert_fusion
  19.0 0.1 fusion.15
  19.1 0.1 copy.26
  19.2 0.1 copy.27
  19.3 0.0 copy-done.4
  19.3 0.4 copy.29
  19.7 1.9 %broadcast_in_dim.51 = f32[2,4,128,512]{3,1,0,2:T(4,128)} broadcast(f32[2,128,512]{2,0,1:T(2,128)S(1)} %copy.29), dimensions={0,2,3} | broadcast | bytes 2621440 | tf_op jit(solution)/shard_map/broadcast_in_dim | solution.py:145
  21.7 0.0 copy-start.5
  21.7 3.0 %reshape.253 = f32[8,128,512]{2,0,1:T(8,128)} reshape(f32[2,4,128,512]{3,1,0,2:T(4,128)} %broadcast_in_dim.51) | data formatting | bytes 4194304 | tf_op jit(solution)/shard_map/reshape | solution.py:147
  24.7 0.1 fusion.7
  24.8 0.0 copy-done.5
  24.8 0.2 slice_reduce_fusion
  25.0 1.1 %select_reduce_fusion.inv_ref = s32[1024]{0:T(1024)} fusion(s32[1024]{0:T(1024)S(1)} %add_select_fusion), kind=kLoop, calls=%fused_computation.2 | loop fusion | flops 3144704 | bytes 8192 | tf_op jit(solution)/shard_map/reduce_sum | solution.py:150
  26.1 21.2 %all-to-all-done = f32[128,8,4,128]{3,2,1,0:T(4,128)S(1)} async-done(((f32[128,8,4,128]{3,2,1,0:T(4,128)}), f32[128,8,4,128]{3,2,1,0:T(4,128)S(1)}, u32[]{:S(2)}, u32[]{:S(2)}) %all-to-all-start) | async-done | bytes 2097184 | tf_op jit(solution)/shard_map/all_to_all | solution.py:126
  47.4 0.0 copy-start.2
  47.4 0.8 broadcast_in_dim.30.coef_ref
  48.2 0.5 copy-done.2
  48.7 12.9 %shard_map.104 = f32[1024,4,128]{2,1,0:T(4,128)} custom-call(s32[1024]{0:T(1024)} %select_reduce_fusion.inv_ref, s32[1]{0:T(128)S(6)} %select_n.86.shift_ref, f32[5,8,512]{2,1,0:T(8,128)} %broadcast_in_dim.30.coef_ref, f32[1024,4,128]{2,1,0:T(4,128)} %bitcast.43, f32[128,8,512]{2,1,0:T(8,128)} %bitcast.44), custom_call_target="tpu_custom_call" | custom-call | tf_op jit(solution)/shard_map/pallas_call | solution.py:104
  61.6 34.6 %all_to_all.10 = f32[128,8,4,128]{3,2,1,0:T(4,128)S(1)} all-to-all(f32[128,8,4,128]{3,2,1,0:T(4,128)} %bitcast.45), channel_id=1, replica_groups=mesh['pt'=8,'comp'=16] {'pt','comp'}, dimensions={0} | all-to-all | bytes 4194304 | tf_op jit(solution)/shard_map/all_to_all | solution.py:154
  96.2 0.2 copy.30
  96.3 1.8 %copy.35 = f32[64,8,8,128]{3,1,2,0:T(8,128)} copy(f32[64,8,8,128]{3,2,1,0:T(8,128)S(1)} %bitcast.48) | data formatting | bytes 4194304
  98.1 0.3 bitcast_reduce_fusion
  98.4 0.6 multiply_bitcast_fusion.1
  (10 shorter events, 0.1 us)
Async XLA Ops:
  0.6 17.7 %copy-start = (s32[512]{0:T(512)S(1)}, s32[512]{0:T(512)}, u32[]{:S(2)}) copy-start(s32[512]{0:T(512)} %param.14) | copy-start | bytes 6148
  0.6 2.2 %copy-start.3 = (f32[512,1024]{1,0:T(8,128)S(1)}, f32[512,1024]{1,0:T(8,128)}, u32[]{:S(2)}) copy-start(f32[512,1024]{1,0:T(8,128)} %param.9) | copy-start | bytes 6291460
  0.7 1.9 %copy-start.6 = (s32[1024]{0:T(1024)S(1)}, s32[1024]{0:T(1024)}, u32[]{:S(2)}) copy-start(s32[1024]{0:T(1024)} %param.15) | copy-start | bytes 12292
  0.7 2.2 %copy-start.7 = (f32[1024]{0:T(1024)S(1)}, f32[1024]{0:T(1024)}, u32[]{:S(2)}) copy-start(f32[1024]{0:T(1024)} %param.10) | copy-start | bytes 12292
  0.7 2.2 %copy-start.9 = (f32[512]{0:T(512)S(1)}, f32[512]{0:T(512)}, u32[]{:S(2)}) copy-start(f32[512]{0:T(512)} %param.11) | copy-start | bytes 6148
  0.7 2.2 %copy-start.8 = (f32[512]{0:T(512)S(1)}, f32[512]{0:T(512)}, u32[]{:S(2)}) copy-start(f32[512]{0:T(512)} %param.12) | copy-start | bytes 6148
  6.1 11.6 %copy-start.1 = (f32[16]{0:T(128)S(1)}, f32[16]{0:T(128)}, u32[]{:S(2)}) copy-start(f32[16]{0:T(128)} %param.13) | copy-start | bytes 196
  6.1 13.2 %copy-start.4 = (s32[256,512]{1,0:T(8,128)S(1)}, s32[256,512]{1,0:T(8,128)}, u32[]{:S(2)}) copy-start(s32[256,512]{1,0:T(8,128)} %param.17) | copy-start | bytes 1572868
  6.1 41.3 %all-to-all-start = ((f32[128,8,4,128]{3,2,1,0:T(4,128)}), f32[128,8,4,128]{3,2,1,0:T(4,128)S(1)}, u32[]{:S(2)}, u32[]{:S(2)}) async-start(f32[128,8,4,128]{3,2,1,0:T(4,128)} %bitcast.46), calls=%async_computation | async-start | bytes 4194304 | tf_op jit(solution)/shard_map/all_to_all | solution.py:126
  21.7 3.1 %copy-start.5 = (s32[131072]{0:T(1024)S(1)}, s32[131072]{0:T(1024)}, u32[]{:S(2)}) copy-start(s32[131072]{0:T(1024)} %param.16) | copy-start | bytes 1572868
  47.4 1.3 %copy-start.2 = (f32[128,8,4,128]{3,2,1,0:T(4,128)}, f32[128,8,4,128]{3,2,1,0:T(4,128)S(1)}, u32[]{:S(2)}) copy-start(f32[128,8,4,128]{3,2,1,0:T(4,128)S(1)} %all-to-all-done) | copy-start | bytes 6291460

commit v12 on v11

--- a/solution.py
+++ b/solution.py
@@ -51,13 +51,21 @@
         lax.fori_loop(0, half, body, 0, unroll=8)
 
     copy_runs(True, 0)
-    ax = coef_ref[0]
-    ay = coef_ref[1]
-    south = coef_ref[2] > 0
     shift = shift_ref[0]
-    cnt = coef_ref[4]
+    south = shift_ref[1] > 0
     sub_id = lax.broadcasted_iota(jnp.int32, (SUB, cols), 0)
     low = sub_id < comps
+    sub_comp = jnp.where(low, sub_id, sub_id - comps)
+
+    def per_sublane(row):
+        v = jnp.full((SUB, cols), coef_ref[row * comps], jnp.float32)
+        for c in range(1, comps):
+            v = jnp.where(sub_comp == c, coef_ref[row * comps + c], v)
+        return v
+
+    ax = per_sublane(0)
+    ay = per_sublane(1)
+    cnt = per_sublane(2)
     for n in range(MAXSUB):
         src, dst = n % 2, (n + 1) % 2
         active = cnt > n
@@ -104,7 +112,7 @@
     return pl.pallas_call(
         propagate_kernel,
         out_shape=jax.ShapeDtypeStruct(recv.shape, recv.dtype),
-        in_specs=[smem] * 2 + [vmem] * 3,
+        in_specs=[smem] * 3 + [vmem] * 2,
         out_specs=vmem,
         scratch_shapes=[pltpu.VMEM((2, half, SUB, cols), jnp.float32)],
     )(inv, shift, coef, recv, wet_h)
@@ -139,16 +147,14 @@
     counts = substeps[comps]
     halves = SUB // per_device
     half = rows_grid // halves
-    lane_rows = jnp.stack([jnp.abs(cross), jnp.abs(along), (cross > 0).astype(jnp.float32),
-                           (along > 0).astype(jnp.float32), counts.astype(jnp.float32)])
-    coef = jnp.broadcast_to(jnp.tile(lane_rows, (1, halves))[:, :, None], (5, SUB, cols_grid))
+    coef = jnp.concatenate([jnp.abs(cross), jnp.abs(along), counts.astype(jnp.float32)])
     wet_h = jnp.broadcast_to(
         wet.astype(jnp.float32).reshape(halves, 1, half, cols_grid), (halves, per_device, half, cols_grid)
     ).reshape(SUB, half, cols_grid).transpose(1, 0, 2)
     slot_runs = deck.reshape(run_count, RUN)[:, 0] // RUN
     run_ids = jnp.arange(run_count, dtype=jnp.int32)
     inv = jnp.sum(jnp.where(slot_runs[None, :] == run_ids[:, None], run_ids[None, :], 0), axis=1)
-    shift = jnp.where(along[:1] > 0, 1, cols_grid - 1).astype(jnp.int32)
+    shift = jnp.stack([jnp.where(along[0] > 0, 1, cols_grid - 1), (cross[0] > 0).astype(jnp.int32)]).astype(jnp.int32)
     slots = propagate(inv, shift, coef, fields.reshape(run_count, per_device, RUN), wet_h)
     slots = slots.reshape(fields.shape)
     back = lax.all_to_all(slots, ("pt", "comp"), split_axis=0, concat_axis=0, tiled=True)

time: 99.3 us -> 99.2 us (level)
  other arithmetic: 4.96 us -> 6.01 us
  transfers between devices with their start and end apart: 1 -> 1, of which waited for: 1 -> 1; matrix products, arithmetic and copies ran while one was open for 8% -> 9% of each run, Pallas kernels for 0% -> 0%
where the time goes in v12:
time: 99.2 us; the launch traced here: 98.9 us
  blocking collectives  34.6 us (35%)
  waiting for transfers between devices  20.3 us (20%)
  local copies, waits for them, and re-layouts  12.8 us (13%)
  Pallas kernels  12.8 us (13%)
  starting transfers between devices  11.5 us (12%)
  other arithmetic  6.01 us (6%)
    all_to_all x1, blocking collectives, on_device(): lax.all_to_all(slots, ('pt', 'comp'), split_axis=0, concat_axis=0, tiled=...  34.6 us
    all_to_all x1, waiting for transfers between devices, on_device(): lax.all_to_all(forced.reshape(group_size, per_device, runs_per_dev, RUN)....  20.3 us
    pallas_call x1, Pallas kernels, propagate(): pl.pallas_call(propagate_kernel, out_shape=jax.ShapeDtypeStruct(recv.shap...  12.8 us
    all_to_all x1, starting transfers between devices, on_device(): lax.all_to_all(forced.reshape(group_size, per_device, runs_per_dev, RUN)....  11.5 us
    unnamed x22, local copies, waits for them, and re-layouts  3.89 us
    reshape x1, local copies, waits for them, and re-layouts, on_device(): wet_h = jnp.broadcast_to(wet.astype(jnp.float32).reshape(halves, 1, half,...  3.04 us
    broadcast_in_dim x2, local copies, waits for them, and re-layouts, on_device(): jnp.broadcast_to(wet.astype(jnp.float32).reshape(halves, 1, half, cols_gr...  2.34 us
  transfers between devices with their start and end apart: 1, of which 1 were waited for; matrix products, arithmetic and copies ran while one was open for 9% of the time, Pallas kernels for 0%

profile of v12, /device:TPU:1, one launch (start us, length us, event | category | flops | bytes accessed | tf_op | source)
XLA Modules:
  0.0 98.9 jit_solution(11820991111160806604)
XLA Ops:
  0.6 0.0 copy-start
  0.6 0.0 copy-start.3
  0.7 0.0 copy-start.6
  0.7 0.0 copy-start.7
  0.7 0.0 copy-start.9
  0.7 0.0 copy-start.8
  0.7 1.9 %reduce_sum.28 = f32[1024]{0:T(1024)S(1)} reduce(f32[512,1024]{1,0:T(8,128)} %param.9, f32[]{:T(128)} %constant.82.clone.1), dimensions={0}, to_apply=%region_1.2 | reduce | flops 523264 | bytes 2101252 | tf_op jit(solution)/shard_map/reduce_sum | solution.py:22
  2.6 0.0 copy-done.6
  2.6 0.3 copy-done.3
  2.9 0.0 copy-done.7
  2.9 0.0 copy-done.9
  2.9 0.0 copy-done.8
  2.9 0.8 multiply_bitcast_fusion
  3.7 0.5 copy.23
  4.2 1.9 %copy.28 = f32[128,4,8,128]{3,1,2,0:T(4,128)} copy(f32[128,4,8,128]{3,2,1,0:T(8,128)S(1)} %bitcast.34) | data formatting | bytes 4194304 | tf_op jit(solution)/shard_map/reshape | solution.py:135
  6.1 0.0 copy-start.1
  6.1 0.0 copy-start.4
  6.1 11.5 %all-to-all-start = ((f32[128,8,4,128]{3,2,1,0:T(4,128)}), f32[128,8,4,128]{3,2,1,0:T(4,128)S(1)}, u32[]{:S(2)}, u32[]{:S(2)}) async-start(f32[128,8,4,128]{3,2,1,0:T(4,128)} %bitcast.33), calls=%async_computation | async-start | bytes 4194304 | tf_op jit(solution)/shard_map/all_to_all | solution.py:134
  17.6 0.0 copy-done
  17.6 0.6 gather_fusion.1
  18.3 0.0 copy-done.1
  18.3 0.6 gather_fusion
  18.9 0.1 fusion.9
  19.1 0.0 copy-done.4
  19.1 0.4 copy.21
  19.6 1.9 %broadcast_in_dim.41 = f32[2,4,128,512]{3,1,0,2:T(4,128)} broadcast(f32[2,128,512]{2,0,1:T(2,128)S(1)} %copy.21), dimensions={0,2,3} | broadcast | bytes 2621440 | tf_op jit(solution)/shard_map/broadcast_in_dim | solution.py:151
  21.5 0.0 copy-start.5
  21.5 3.0 %reshape.151 = f32[8,128,512]{2,0,1:T(8,128)} reshape(f32[2,4,128,512]{3,1,0,2:T(4,128)} %broadcast_in_dim.41) | data formatting | bytes 4194304 | tf_op jit(solution)/shard_map/reshape | solution.py:153
  24.5 0.6 pad_add_fusion.shift_ref
  25.1 0.6 pad_maximum_fusion.coef_ref
  25.7 0.0 copy-done.5
  25.7 0.2 slice_reduce_fusion
  25.9 1.1 %select_reduce_fusion.inv_ref = s32[1024]{0:T(1024)} fusion(s32[1024]{0:T(1024)S(1)} %add_select_fusion), kind=kLoop, calls=%fused_computation.2 | loop fusion | flops 3144704 | bytes 8192 | tf_op jit(solution)/shard_map/reduce_sum | solution.py:156
  27.0 20.3 %all-to-all-done = f32[128,8,4,128]{3,2,1,0:T(4,128)S(1)} async-done(((f32[128,8,4,128]{3,2,1,0:T(4,128)}), f32[128,8,4,128]{3,2,1,0:T(4,128)S(1)}, u32[]{:S(2)}, u32[]{:S(2)}) %all-to-all-start) | async-done | bytes 2097184 | tf_op jit(solution)/shard_map/all_to_all | solution.py:134
  47.4 0.0 copy-start.2
  47.4 1.3 %copy-done.2 = f32[128,8,4,128]{3,2,1,0:T(4,128)} copy-done((f32[128,8,4,128]{3,2,1,0:T(4,128)}, f32[128,8,4,128]{3,2,1,0:T(4,128)S(1)}, u32[]{:S(2)}) %copy-start.2) | copy-done | bytes 2097176
  48.7 12.8 %shard_map.104 = f32[1024,4,128]{2,1,0:T(4,128)} custom-call(s32[1024]{0:T(1024)} %select_reduce_fusion.inv_ref, s32[2]{0:T(128)} %pad_add_fusion.shift_ref, f32[12]{0:T(128)} %pad_maximum_fusion.coef_ref, f32[1024,4,128]{2,1,0:T(4,128)} %bitcast.30, f32[128,8,512]{2,1,0:T(8,128)} %bitcast.31), custom_call_target="tpu_custom_call" | custom-call | tf_op jit(solution)/shard_map/pallas_call | solution.py:112
  61.5 34.6 %all_to_all.10 = f32[128,8,4,128]{3,2,1,0:T(4,128)S(1)} all-to-all(f32[128,8,4,128]{3,2,1,0:T(4,128)} %bitcast.32), channel_id=1, replica_groups=mesh['pt'=8,'comp'=16] {'pt','comp'}, dimensions={0} | all-to-all | bytes 4194304 | tf_op jit(solution)/shard_map/all_to_all | solution.py:160
  96.1 0.2 copy.22
  96.2 1.8 %copy.27 = f32[64,8,8,128]{3,1,2,0:T(8,128)} copy(f32[64,8,8,128]{3,2,1,0:T(8,128)S(1)} %bitcast.35) | data formatting | bytes 4194304
  98.0 0.3 bitcast_reduce_fusion
  98.3 0.6 multiply_bitcast_fusion.1
  (8 shorter events, 0.1 us)
Async XLA Ops:
  0.6 17.0 %copy-start = (s32[512]{0:T(512)S(1)}, s32[512]{0:T(512)}, u32[]{:S(2)}) copy-start(s32[512]{0:T(512)} %param.14) | copy-start | bytes 6148
  0.6 2.2 %copy-start.3 = (f32[512,1024]{1,0:T(8,128)S(1)}, f32[512,1024]{1,0:T(8,128)}, u32[]{:S(2)}) copy-start(f32[512,1024]{1,0:T(8,128)} %param.9) | copy-start | bytes 6291460
  0.7 1.9 %copy-start.6 = (s32[1024]{0:T(1024)S(1)}, s32[1024]{0:T(1024)}, u32[]{:S(2)}) copy-start(s32[1024]{0:T(1024)} %param.15) | copy-start | bytes 12292
  0.7 2.2 %copy-start.7 = (f32[1024]{0:T(1024)S(1)}, f32[1024]{0:T(1024)}, u32[]{:S(2)}) copy-start(f32[1024]{0:T(1024)} %param.10) | copy-start | bytes 12292
  0.7 2.2 %copy-start.9 = (f32[512]{0:T(512)S(1)}, f32[512]{0:T(512)}, u32[]{:S(2)}) copy-start(f32[512]{0:T(512)} %param.11) | copy-start | bytes 6148
  0.7 2.2 %copy-start.8 = (f32[512]{0:T(512)S(1)}, f32[512]{0:T(512)}, u32[]{:S(2)}) copy-start(f32[512]{0:T(512)} %param.12) | copy-start | bytes 6148
  6.1 12.2 %copy-start.1 = (f32[16]{0:T(128)S(1)}, f32[16]{0:T(128)}, u32[]{:S(2)}) copy-start(f32[16]{0:T(128)} %param.13) | copy-start | bytes 196
  6.1 13.0 %copy-start.4 = (s32[256,512]{1,0:T(8,128)S(1)}, s32[256,512]{1,0:T(8,128)}, u32[]{:S(2)}) copy-start(s32[256,512]{1,0:T(8,128)} %param.17) | copy-start | bytes 1572868
  6.1 41.3 %all-to-all-start = ((f32[128,8,4,128]{3,2,1,0:T(4,128)}), f32[128,8,4,128]{3,2,1,0:T(4,128)S(1)}, u32[]{:S(2)}, u32[]{:S(2)}) async-start(f32[128,8,4,128]{3,2,1,0:T(4,128)} %bitcast.33), calls=%async_computation | async-start | bytes 4194304 | tf_op jit(solution)/shard_map/all_to_all | solution.py:134
  21.5 4.2 %copy-start.5 = (s32[131072]{0:T(1024)S(1)}, s32[131072]{0:T(1024)}, u32[]{:S(2)}) copy-start(s32[131072]{0:T(1024)} %param.16) | copy-start | bytes 1572868
  47.4 1.3 %copy-start.2 = (f32[128,8,4,128]{3,2,1,0:T(4,128)}, f32[128,8,4,128]{3,2,1,0:T(4,128)S(1)}, u32[]{:S(2)}) copy-start(f32[128,8,4,128]{3,2,1,0:T(4,128)S(1)} %all-to-all-done) | copy-start | bytes 6291460

commit v13 on v12

--- a/solution.py
+++ b/solution.py
@@ -52,7 +52,6 @@
 
     copy_runs(True, 0)
     shift = shift_ref[0]
-    south = shift_ref[1] > 0
     sub_id = lax.broadcasted_iota(jnp.int32, (SUB, cols), 0)
     low = sub_id < comps
     sub_comp = jnp.where(low, sub_id, sub_id - comps)
@@ -66,43 +65,52 @@
     ax = per_sublane(0)
     ay = per_sublane(1)
     cnt = per_sublane(2)
-    for n in range(MAXSUB):
-        src, dst = n % 2, (n + 1) % 2
-        active = cnt > n
-        sea = {}
-        vals = {}
+    def run_substeps(south):
+        for n in range(MAXSUB):
+            src, dst = n % 2, (n + 1) % 2
+            active = cnt > n
+            sea = {}
+            vals = {}
 
-        def sea_of(i):
-            if i not in sea:
-                vals[i] = (buf_ref[src, i], wet_ref[i])
-                sea[i] = vals[i][0] * vals[i][1]
-            return sea[i]
+            def sea_of(i):
+                if i not in sea:
+                    vals[i] = (buf_ref[src, i], wet_ref[i])
+                    sea[i] = vals[i][0] * vals[i][1]
+                return sea[i]
 
-        for i in range(half):
-            if i == 0:
-                prev = jnp.where(low, 0.0, pltpu.roll(sea_of(half - 1), comps, 0))
-            else:
-                prev = sea_of(i - 1)
-            if i == half - 1:
-                nxt = jnp.where(low, pltpu.roll(sea_of(0), comps, 0), 0.0)
-            else:
-                nxt = sea_of(i + 1)
-            here = sea_of(i)
-            f, w = vals[i]
-            up_row = jnp.where(south, prev, nxt)
-            up_col = pltpu.roll(here, shift, 1)
-            moved = f - ax * (f - up_row) - ay * (f - up_col)
-            result = jnp.where(active & (w > 0), moved, f)
-            if n < MAXSUB - 1:
-                buf_ref[dst, i] = result
-            else:
-                for h in range(halves):
-                    for q in range(quarters):
-                        out_ref[inv_ref[(h * half + i) * quarters + q]] = result[
-                            h * comps:(h + 1) * comps, q * RUN:(q + 1) * RUN
-                        ]
-            sea.pop(i - 1, None)
-            vals.pop(i - 1, None)
+            for i in range(half):
+                if i == 0:
+                    prev = jnp.where(low, 0.0, pltpu.roll(sea_of(half - 1), comps, 0))
+                else:
+                    prev = sea_of(i - 1)
+                if i == half - 1:
+                    nxt = jnp.where(low, pltpu.roll(sea_of(0), comps, 0), 0.0)
+                else:
+                    nxt = sea_of(i + 1)
+                here = sea_of(i)
+                f, w = vals[i]
+                up_row = prev if south else nxt
+                up_col = pltpu.roll(here, shift, 1)
+                moved = f - ax * (f - up_row) - ay * (f - up_col)
+                result = jnp.where(active & (w > 0), moved, f)
+                if n < MAXSUB - 1:
+                    buf_ref[dst, i] = result
+                else:
+                    for h in range(halves):
+                        for q in range(quarters):
+                            out_ref[inv_ref[(h * half + i) * quarters + q]] = result[
+                                h * comps:(h + 1) * comps, q * RUN:(q + 1) * RUN
+                            ]
+                sea.pop(i - 1, None)
+                vals.pop(i - 1, None)
+
+    @pl.when(shift_ref[1] > 0)
+    def _():
+        run_substeps(True)
+
+    @pl.when(shift_ref[1] <= 0)
+    def _():
+        run_substeps(False)
 
 
 def propagate(inv, shift, coef, recv, wet_h):

time: 99.2 us -> 99.3 us (level)
  no operation moved by 1% of the time
where the time goes in v13:
time: 99.3 us; the launch traced here: 98.9 us
  blocking collectives  34.6 us (35%)
  waiting for transfers between devices  20.3 us (20%)
  local copies, waits for them, and re-layouts  12.8 us (13%)
  Pallas kernels  12.8 us (13%)
  starting transfers between devices  11.5 us (12%)
  other arithmetic  6.01 us (6%)
    all_to_all x1, blocking collectives, on_device(): lax.all_to_all(slots, ('pt', 'comp'), split_axis=0, concat_axis=0, tiled=...  34.6 us
    all_to_all x1, waiting for transfers between devices, on_device(): lax.all_to_all(forced.reshape(group_size, per_device, runs_per_dev, RUN)....  20.3 us
    pallas_call x1, Pallas kernels, propagate(): pl.pallas_call(propagate_kernel, out_shape=jax.ShapeDtypeStruct(recv.shap...  12.8 us
    all_to_all x1, starting transfers between devices, on_device(): lax.all_to_all(forced.reshape(group_size, per_device, runs_per_dev, RUN)....  11.5 us
    unnamed x22, local copies, waits for them, and re-layouts  3.89 us
    reshape x1, local copies, waits for them, and re-layouts, on_device(): wet_h = jnp.broadcast_to(wet.astype(jnp.float32).reshape(halves, 1, half,...  3.04 us
    broadcast_in_dim x2, local copies, waits for them, and re-layouts, on_device(): jnp.broadcast_to(wet.astype(jnp.float32).reshape(halves, 1, half, cols_gr...  2.34 us
  transfers between devices with their start and end apart: 1, of which 1 were waited for; matrix products, arithmetic and copies ran while one was open for 9% of the time, Pallas kernels for 0%

profile of v13, /device:TPU:1, one launch (start us, length us, event | category | flops | bytes accessed | tf_op | source)
XLA Modules:
  0.0 98.9 jit_solution(16826973474997415551)
XLA Ops:
  0.6 0.0 copy-start
  0.6 0.0 copy-start.3
  0.7 0.0 copy-start.6
  0.7 0.0 copy-start.7
  0.7 0.0 copy-start.9
  0.7 0.0 copy-start.8
  0.7 1.9 %reduce_sum.28 = f32[1024]{0:T(1024)S(1)} reduce(f32[512,1024]{1,0:T(8,128)} %param.9, f32[]{:T(128)} %constant.82.clone.1), dimensions={0}, to_apply=%region_1.2 | reduce | flops 523264 | bytes 2101252 | tf_op jit(solution)/shard_map/reduce_sum | solution.py:22
  2.6 0.0 copy-done.6
  2.6 0.3 copy-done.3
  2.9 0.0 copy-done.7
  2.9 0.0 copy-done.9
  2.9 0.0 copy-done.8
  2.9 0.8 multiply_bitcast_fusion
  3.7 0.5 copy.23
  4.2 1.9 %copy.28 = f32[128,4,8,128]{3,1,2,0:T(4,128)} copy(f32[128,4,8,128]{3,2,1,0:T(8,128)S(1)} %bitcast.34) | data formatting | bytes 4194304 | tf_op jit(solution)/shard_map/reshape | solution.py:143
  6.1 0.0 copy-start.1
  6.1 0.0 copy-start.4
  6.1 11.5 %all-to-all-start = ((f32[128,8,4,128]{3,2,1,0:T(4,128)}), f32[128,8,4,128]{3,2,1,0:T(4,128)S(1)}, u32[]{:S(2)}, u32[]{:S(2)}) async-start(f32[128,8,4,128]{3,2,1,0:T(4,128)} %bitcast.33), calls=%async_computation | async-start | bytes 4194304 | tf_op jit(solution)/shard_map/all_to_all | solution.py:142
  17.6 0.0 copy-done
  17.6 0.6 gather_fusion.1
  18.3 0.0 copy-done.1
  18.3 0.6 gather_fusion
  18.9 0.1 fusion.9
  19.1 0.0 copy-done.4
  19.1 0.4 copy.21
  19.6 1.9 %broadcast_in_dim.41 = f32[2,4,128,512]{3,1,0,2:T(4,128)} broadcast(f32[2,128,512]{2,0,1:T(2,128)S(1)} %copy.21), dimensions={0,2,3} | broadcast | bytes 2621440 | tf_op jit(solution)/shard_map/broadcast_in_dim | solution.py:159
  21.5 0.0 copy-start.5
  21.5 3.0 %reshape.151 = f32[8,128,512]{2,0,1:T(8,128)} reshape(f32[2,4,128,512]{3,1,0,2:T(4,128)} %broadcast_in_dim.41) | data formatting | bytes 4194304 | tf_op jit(solution)/shard_map/reshape | solution.py:161
  24.5 0.6 pad_add_fusion.shift_ref
  25.1 0.6 pad_maximum_fusion.coef_ref
  25.7 0.0 copy-done.5
  25.7 0.2 slice_reduce_fusion
  25.9 1.1 %select_reduce_fusion.inv_ref = s32[1024]{0:T(1024)} fusion(s32[1024]{0:T(1024)S(1)} %add_select_fusion), kind=kLoop, calls=%fused_computation.2 | loop fusion | flops 3144704 | bytes 8192 | tf_op jit(solution)/shard_map/reduce_sum | solution.py:164
  27.0 20.3 %all-to-all-done = f32[128,8,4,128]{3,2,1,0:T(4,128)S(1)} async-done(((f32[128,8,4,128]{3,2,1,0:T(4,128)}), f32[128,8,4,128]{3,2,1,0:T(4,128)S(1)}, u32[]{:S(2)}, u32[]{:S(2)}) %all-to-all-start) | async-done | bytes 2097184 | tf_op jit(solution)/shard_map/all_to_all | solution.py:142
  47.4 0.0 copy-start.2
  47.4 1.3 %copy-done.2 = f32[128,8,4,128]{3,2,1,0:T(4,128)} copy-done((f32[128,8,4,128]{3,2,1,0:T(4,128)}, f32[128,8,4,128]{3,2,1,0:T(4,128)S(1)}, u32[]{:S(2)}) %copy-start.2) | copy-done | bytes 2097176
  48.7 12.8 %shard_map.104 = f32[1024,4,128]{2,1,0:T(4,128)} custom-call(s32[1024]{0:T(1024)} %select_reduce_fusion.inv_ref, s32[2]{0:T(128)} %pad_add_fusion.shift_ref, f32[12]{0:T(128)} %pad_maximum_fusion.coef_ref, f32[1024,4,128]{2,1,0:T(4,128)} %bitcast.30, f32[128,8,512]{2,1,0:T(8,128)} %bitcast.31), custom_call_target="tpu_custom_call" | custom-call | tf_op jit(solution)/shard_map/pallas_call | solution.py:120
  61.5 34.6 %all_to_all.10 = f32[128,8,4,128]{3,2,1,0:T(4,128)S(1)} all-to-all(f32[128,8,4,128]{3,2,1,0:T(4,128)} %bitcast.32), channel_id=1, replica_groups=mesh['pt'=8,'comp'=16] {'pt','comp'}, dimensions={0} | all-to-all | bytes 4194304 | tf_op jit(solution)/shard_map/all_to_all | solution.py:168
  96.1 0.2 copy.22
  96.3 1.8 %copy.27 = f32[64,8,8,128]{3,1,2,0:T(8,128)} copy(f32[64,8,8,128]{3,2,1,0:T(8,128)S(1)} %bitcast.35) | data formatting | bytes 4194304
  98.1 0.3 bitcast_reduce_fusion
  98.3 0.6 multiply_bitcast_fusion.1
  (8 shorter events, 0.1 us)
Async XLA Ops:
  0.6 17.0 %copy-start = (s32[512]{0:T(512)S(1)}, s32[512]{0:T(512)}, u32[]{:S(2)}) copy-start(s32[512]{0:T(512)} %param.14) | copy-start | bytes 6148
  0.6 2.2 %copy-start.3 = (f32[512,1024]{1,0:T(8,128)S(1)}, f32[512,1024]{1,0:T(8,128)}, u32[]{:S(2)}) copy-start(f32[512,1024]{1,0:T(8,128)} %param.9) | copy-start | bytes 6291460
  0.7 1.9 %copy-start.6 = (s32[1024]{0:T(1024)S(1)}, s32[1024]{0:T(1024)}, u32[]{:S(2)}) copy-start(s32[1024]{0:T(1024)} %param.15) | copy-start | bytes 12292
  0.7 2.2 %copy-start.7 = (f32[1024]{0:T(1024)S(1)}, f32[1024]{0:T(1024)}, u32[]{:S(2)}) copy-start(f32[1024]{0:T(1024)} %param.10) | copy-start | bytes 12292
  0.7 2.2 %copy-start.9 = (f32[512]{0:T(512)S(1)}, f32[512]{0:T(512)}, u32[]{:S(2)}) copy-start(f32[512]{0:T(512)} %param.11) | copy-start | bytes 6148
  0.7 2.2 %copy-start.8 = (f32[512]{0:T(512)S(1)}, f32[512]{0:T(512)}, u32[]{:S(2)}) copy-start(f32[512]{0:T(512)} %param.12) | copy-start | bytes 6148
  6.1 12.2 %copy-start.1 = (f32[16]{0:T(128)S(1)}, f32[16]{0:T(128)}, u32[]{:S(2)}) copy-start(f32[16]{0:T(128)} %param.13) | copy-start | bytes 196
  6.1 13.0 %copy-start.4 = (s32[256,512]{1,0:T(8,128)S(1)}, s32[256,512]{1,0:T(8,128)}, u32[]{:S(2)}) copy-start(s32[256,512]{1,0:T(8,128)} %param.17) | copy-start | bytes 1572868
  6.1 41.3 %all-to-all-start = ((f32[128,8,4,128]{3,2,1,0:T(4,128)}), f32[128,8,4,128]{3,2,1,0:T(4,128)S(1)}, u32[]{:S(2)}, u32[]{:S(2)}) async-start(f32[128,8,4,128]{3,2,1,0:T(4,128)} %bitcast.33), calls=%async_computation | async-start | bytes 4194304 | tf_op jit(solution)/shard_map/all_to_all | solution.py:142
  21.5 4.2 %copy-start.5 = (s32[131072]{0:T(1024)S(1)}, s32[131072]{0:T(1024)}, u32[]{:S(2)}) copy-start(s32[131072]{0:T(1024)} %param.16) | copy-start | bytes 1572868
  47.4 1.3 %copy-start.2 = (f32[128,8,4,128]{3,2,1,0:T(4,128)}, f32[128,8,4,128]{3,2,1,0:T(4,128)S(1)}, u32[]{:S(2)}) copy-start(f32[128,8,4,128]{3,2,1,0:T(4,128)S(1)} %all-to-all-done) | copy-start | bytes 6291460

commit v14 on v12

--- a/solution.py
+++ b/solution.py
@@ -48,7 +48,7 @@
                         out_ref[s] = buf_ref[slot, i, rows, lanes]
             return carry
 
-        lax.fori_loop(0, half, body, 0, unroll=8)
+        lax.fori_loop(0, half, body, 0, unroll=True)
 
     copy_runs(True, 0)
     shift = shift_ref[0]

time: 99.2 us -> 98.5 us (level)
  no operation moved by 1% of the time
where the time goes in v14:
time: 98.5 us; the launch traced here: 98.2 us
  blocking collectives  34.6 us (35%)
  waiting for transfers between devices  20.3 us (21%)
  local copies, waits for them, and re-layouts  12.8 us (13%)
  Pallas kernels  12.1 us (12%)
  starting transfers between devices  11.5 us (12%)
  other arithmetic  6.01 us (6%)
    all_to_all x1, blocking collectives, on_device(): lax.all_to_all(slots, ('pt', 'comp'), split_axis=0, concat_axis=0, tiled=...  34.6 us
    all_to_all x1, waiting for transfers between devices, on_device(): lax.all_to_all(forced.reshape(group_size, per_device, runs_per_dev, RUN)....  20.3 us
    pallas_call x1, Pallas kernels, propagate(): pl.pallas_call(propagate_kernel, out_shape=jax.ShapeDtypeStruct(recv.shap...  12.1 us
    all_to_all x1, starting transfers between devices, on_device(): lax.all_to_all(forced.reshape(group_size, per_device, runs_per_dev, RUN)....  11.5 us
    unnamed x22, local copies, waits for them, and re-layouts  3.89 us
    reshape x1, local copies, waits for them, and re-layouts, on_device(): wet_h = jnp.broadcast_to(wet.astype(jnp.float32).reshape(halves, 1, half,...  3.04 us
    broadcast_in_dim x2, local copies, waits for them, and re-layouts, on_device(): jnp.broadcast_to(wet.astype(jnp.float32).reshape(halves, 1, half, cols_gr...  2.34 us
  transfers between devices with their start and end apart: 1, of which 1 were waited for; matrix products, arithmetic and copies ran while one was open for 9% of the time, Pallas kernels for 0%

profile of v14, /device:TPU:1, one launch (start us, length us, event | category | flops | bytes accessed | tf_op | source)
XLA Modules:
  0.0 98.2 jit_solution(15320573449351523494)
XLA Ops:
  0.6 0.0 copy-start
  0.6 0.0 copy-start.3
  0.7 0.0 copy-start.6
  0.7 0.0 copy-start.7
  0.7 0.0 copy-start.9
  0.7 0.0 copy-start.8
  0.7 1.9 %reduce_sum.28 = f32[1024]{0:T(1024)S(1)} reduce(f32[512,1024]{1,0:T(8,128)} %param.9, f32[]{:T(128)} %constant.82.clone.1), dimensions={0}, to_apply=%region_1.2 | reduce | flops 523264 | bytes 2101252 | tf_op jit(solution)/shard_map/reduce_sum | solution.py:22
  2.6 0.0 copy-done.6
  2.6 0.3 copy-done.3
  2.9 0.0 copy-done.7
  2.9 0.0 copy-done.9
  2.9 0.0 copy-done.8
  2.9 0.8 multiply_bitcast_fusion
  3.7 0.5 copy.23
  4.2 1.9 %copy.28 = f32[128,4,8,128]{3,1,2,0:T(4,128)} copy(f32[128,4,8,128]{3,2,1,0:T(8,128)S(1)} %bitcast.34) | data formatting | bytes 4194304 | tf_op jit(solution)/shard_map/reshape | solution.py:135
  6.1 0.0 copy-start.1
  6.1 0.0 copy-start.4
  6.1 11.5 %all-to-all-start = ((f32[128,8,4,128]{3,2,1,0:T(4,128)}), f32[128,8,4,128]{3,2,1,0:T(4,128)S(1)}, u32[]{:S(2)}, u32[]{:S(2)}) async-start(f32[128,8,4,128]{3,2,1,0:T(4,128)} %bitcast.33), calls=%async_computation | async-start | bytes 4194304 | tf_op jit(solution)/shard_map/all_to_all | solution.py:134
  17.6 0.0 copy-done
  17.6 0.6 gather_fusion.1
  18.3 0.0 copy-done.1
  18.3 0.6 gather_fusion
  18.9 0.1 fusion.9
  19.1 0.0 copy-done.4
  19.1 0.4 copy.21
  19.6 1.9 %broadcast_in_dim.41 = f32[2,4,128,512]{3,1,0,2:T(4,128)} broadcast(f32[2,128,512]{2,0,1:T(2,128)S(1)} %copy.21), dimensions={0,2,3} | broadcast | bytes 2621440 | tf_op jit(solution)/shard_map/broadcast_in_dim | solution.py:151
  21.5 0.0 copy-start.5
  21.5 3.0 %reshape.151 = f32[8,128,512]{2,0,1:T(8,128)} reshape(f32[2,4,128,512]{3,1,0,2:T(4,128)} %broadcast_in_dim.41) | data formatting | bytes 4194304 | tf_op jit(solution)/shard_map/reshape | solution.py:153
  24.5 0.6 pad_add_fusion.shift_ref
  25.1 0.6 pad_maximum_fusion.coef_ref
  25.7 0.0 copy-done.5
  25.7 0.2 slice_reduce_fusion
  25.9 1.1 %select_reduce_fusion.inv_ref = s32[1024]{0:T(1024)} fusion(s32[1024]{0:T(1024)S(1)} %add_select_fusion), kind=kLoop, calls=%fused_computation.2 | loop fusion | flops 3144704 | bytes 8192 | tf_op jit(solution)/shard_map/reduce_sum | solution.py:156
  27.0 20.3 %all-to-all-done = f32[128,8,4,128]{3,2,1,0:T(4,128)S(1)} async-done(((f32[128,8,4,128]{3,2,1,0:T(4,128)}), f32[128,8,4,128]{3,2,1,0:T(4,128)S(1)}, u32[]{:S(2)}, u32[]{:S(2)}) %all-to-all-start) | async-done | bytes 2097184 | tf_op jit(solution)/shard_map/all_to_all | solution.py:134
  47.4 0.0 copy-start.2
  47.4 1.3 %copy-done.2 = f32[128,8,4,128]{3,2,1,0:T(4,128)} copy-done((f32[128,8,4,128]{3,2,1,0:T(4,128)}, f32[128,8,4,128]{3,2,1,0:T(4,128)S(1)}, u32[]{:S(2)}) %copy-start.2) | copy-done | bytes 2097176
  48.7 12.1 %shard_map.104 = f32[1024,4,128]{2,1,0:T(4,128)} custom-call(s32[1024]{0:T(1024)} %select_reduce_fusion.inv_ref, s32[2]{0:T(128)} %pad_add_fusion.shift_ref, f32[12]{0:T(128)} %pad_maximum_fusion.coef_ref, f32[1024,4,128]{2,1,0:T(4,128)} %bitcast.30, f32[128,8,512]{2,1,0:T(8,128)} %bitcast.31), custom_call_target="tpu_custom_call" | custom-call | tf_op jit(solution)/shard_map/pallas_call | solution.py:112
  60.8 34.6 %all_to_all.10 = f32[128,8,4,128]{3,2,1,0:T(4,128)S(1)} all-to-all(f32[128,8,4,128]{3,2,1,0:T(4,128)} %bitcast.32), channel_id=1, replica_groups=mesh['pt'=8,'comp'=16] {'pt','comp'}, dimensions={0} | all-to-all | bytes 4194304 | tf_op jit(solution)/shard_map/all_to_all | solution.py:160
  95.4 0.2 copy.22
  95.6 1.8 %copy.27 = f32[64,8,8,128]{3,1,2,0:T(8,128)} copy(f32[64,8,8,128]{3,2,1,0:T(8,128)S(1)} %bitcast.35) | data formatting | bytes 4194304
  97.3 0.3 bitcast_reduce_fusion
  97.6 0.6 multiply_bitcast_fusion.1
  (8 shorter events, 0.1 us)
Async XLA Ops:
  0.6 17.0 %copy-start = (s32[512]{0:T(512)S(1)}, s32[512]{0:T(512)}, u32[]{:S(2)}) copy-start(s32[512]{0:T(512)} %param.14) | copy-start | bytes 6148
  0.6 2.2 %copy-start.3 = (f32[512,1024]{1,0:T(8,128)S(1)}, f32[512,1024]{1,0:T(8,128)}, u32[]{:S(2)}) copy-start(f32[512,1024]{1,0:T(8,128)} %param.9) | copy-start | bytes 6291460
  0.7 1.9 %copy-start.6 = (s32[1024]{0:T(1024)S(1)}, s32[1024]{0:T(1024)}, u32[]{:S(2)}) copy-start(s32[1024]{0:T(1024)} %param.15) | copy-start | bytes 12292
  0.7 2.2 %copy-start.7 = (f32[1024]{0:T(1024)S(1)}, f32[1024]{0:T(1024)}, u32[]{:S(2)}) copy-start(f32[1024]{0:T(1024)} %param.10) | copy-start | bytes 12292
  0.7 2.2 %copy-start.9 = (f32[512]{0:T(512)S(1)}, f32[512]{0:T(512)}, u32[]{:S(2)}) copy-start(f32[512]{0:T(512)} %param.11) | copy-start | bytes 6148
  0.7 2.2 %copy-start.8 = (f32[512]{0:T(512)S(1)}, f32[512]{0:T(512)}, u32[]{:S(2)}) copy-start(f32[512]{0:T(512)} %param.12) | copy-start | bytes 6148
  6.1 12.2 %copy-start.1 = (f32[16]{0:T(128)S(1)}, f32[16]{0:T(128)}, u32[]{:S(2)}) copy-start(f32[16]{0:T(128)} %param.13) | copy-start | bytes 196
  6.1 13.0 %copy-start.4 = (s32[256,512]{1,0:T(8,128)S(1)}, s32[256,512]{1,0:T(8,128)}, u32[]{:S(2)}) copy-start(s32[256,512]{1,0:T(8,128)} %param.17) | copy-start | bytes 1572868
  6.1 41.3 %all-to-all-start = ((f32[128,8,4,128]{3,2,1,0:T(4,128)}), f32[128,8,4,128]{3,2,1,0:T(4,128)S(1)}, u32[]{:S(2)}, u32[]{:S(2)}) async-start(f32[128,8,4,128]{3,2,1,0:T(4,128)} %bitcast.33), calls=%async_computation | async-start | bytes 4194304 | tf_op jit(solution)/shard_map/all_to_all | solution.py:134
  21.5 4.2 %copy-start.5 = (s32[131072]{0:T(1024)S(1)}, s32[131072]{0:T(1024)}, u32[]{:S(2)}) copy-start(s32[131072]{0:T(1024)} %param.16) | copy-start | bytes 1572868
  47.4 1.3 %copy-start.2 = (f32[128,8,4,128]{3,2,1,0:T(4,128)}, f32[128,8,4,128]{3,2,1,0:T(4,128)S(1)}, u32[]{:S(2)}) copy-start(f32[128,8,4,128]{3,2,1,0:T(4,128)S(1)} %all-to-all-done) | copy-start | bytes 6291460

commit v15 on v14

--- a/solution.py
+++ b/solution.py
@@ -159,7 +159,7 @@
     slots = slots.reshape(fields.shape)
     back = lax.all_to_all(slots, ("pt", "comp"), split_axis=0, concat_axis=0, tiled=True)
     arrived = back.transpose(0, 2, 1, 3).reshape(total_comps, point_count)
-    height = 4.0 * jnp.sqrt(jnp.mean(arrived, axis=0) + 1e-06)
+    height = 4.0 * jnp.sqrt(jnp.sum(back, axis=(0, 2)).reshape(point_count) / total_comps + 1e-06)
     return (arrived, height)
 
 

time: 98.5 us -> 98.6 us (level)
  no operation moved by 1% of the time
where the time goes in v15:
time: 98.6 us; the launch traced here: 98.3 us
  blocking collectives  34.6 us (35%)
  waiting for transfers between devices  20.3 us (21%)
  local copies, waits for them, and re-layouts  12.8 us (13%)
  Pallas kernels  12.1 us (12%)
  starting transfers between devices  11.5 us (12%)
  other arithmetic  6.09 us (6%)
    all_to_all x1, blocking collectives, on_device(): lax.all_to_all(slots, ('pt', 'comp'), split_axis=0, concat_axis=0, tiled=...  34.6 us
    all_to_all x1, waiting for transfers between devices, on_device(): lax.all_to_all(forced.reshape(group_size, per_device, runs_per_dev, RUN)....  20.3 us
    pallas_call x1, Pallas kernels, propagate(): pl.pallas_call(propagate_kernel, out_shape=jax.ShapeDtypeStruct(recv.shap...  12.1 us
    all_to_all x1, starting transfers between devices, on_device(): lax.all_to_all(forced.reshape(group_size, per_device, runs_per_dev, RUN)....  11.5 us
    unnamed x22, local copies, waits for them, and re-layouts  3.89 us
    reshape x1, local copies, waits for them, and re-layouts, on_device(): wet_h = jnp.broadcast_to(wet.astype(jnp.float32).reshape(halves, 1, half,...  3.04 us
    broadcast_in_dim x2, local copies, waits for them, and re-layouts, on_device(): jnp.broadcast_to(wet.astype(jnp.float32).reshape(halves, 1, half, cols_gr...  2.34 us
  transfers between devices with their start and end apart: 1, of which 1 were waited for; matrix products, arithmetic and copies ran while one was open for 9% of the time, Pallas kernels for 0%

profile of v15, /device:TPU:1, one launch (start us, length us, event | category | flops | bytes accessed | tf_op | source)
XLA Modules:
  0.0 98.3 jit_solution(17589332318339395470)
XLA Ops:
  0.6 0.0 copy-start
  0.6 0.0 copy-start.3
  0.7 0.0 copy-start.6
  0.7 0.0 copy-start.7
  0.7 0.0 copy-start.9
  0.7 0.0 copy-start.8
  0.7 1.9 %reduce_sum.28 = f32[1024]{0:T(1024)S(1)} reduce(f32[512,1024]{1,0:T(8,128)} %param.9, f32[]{:T(128)} %constant.82.clone.1), dimensions={0}, to_apply=%region_1.2 | reduce | flops 523264 | bytes 2101252 | tf_op jit(solution)/shard_map/reduce_sum | solution.py:22
  2.6 0.0 copy-done.6
  2.6 0.3 copy-done.3
  2.9 0.0 copy-done.7
  2.9 0.0 copy-done.9
  2.9 0.0 copy-done.8
  2.9 0.8 multiply_bitcast_fusion
  3.7 0.5 copy.23
  4.2 1.9 %copy.28 = f32[128,4,8,128]{3,1,2,0:T(4,128)} copy(f32[128,4,8,128]{3,2,1,0:T(8,128)S(1)} %bitcast.33) | data formatting | bytes 4194304 | tf_op jit(solution)/shard_map/reshape | solution.py:135
  6.1 0.0 copy-start.1
  6.1 0.0 copy-start.4
  6.1 11.5 %all-to-all-start = ((f32[128,8,4,128]{3,2,1,0:T(4,128)}), f32[128,8,4,128]{3,2,1,0:T(4,128)S(1)}, u32[]{:S(2)}, u32[]{:S(2)}) async-start(f32[128,8,4,128]{3,2,1,0:T(4,128)} %bitcast.32), calls=%async_computation | async-start | bytes 4194304 | tf_op jit(solution)/shard_map/all_to_all | solution.py:134
  17.6 0.0 copy-done
  17.6 0.6 gather_fusion.1
  18.3 0.0 copy-done.1
  18.3 0.6 gather_fusion
  18.9 0.1 fusion.9
  19.1 0.0 copy-done.4
  19.1 0.4 copy.21
  19.6 1.9 %broadcast_in_dim.41 = f32[2,4,128,512]{3,1,0,2:T(4,128)} broadcast(f32[2,128,512]{2,0,1:T(2,128)S(1)} %copy.21), dimensions={0,2,3} | broadcast | bytes 2621440 | tf_op jit(solution)/shard_map/broadcast_in_dim | solution.py:151
  21.5 0.0 copy-start.5
  21.5 3.0 %reshape.151 = f32[8,128,512]{2,0,1:T(8,128)} reshape(f32[2,4,128,512]{3,1,0,2:T(4,128)} %broadcast_in_dim.41) | data formatting | bytes 4194304 | tf_op jit(solution)/shard_map/reshape | solution.py:153
  24.5 0.6 pad_add_fusion.shift_ref
  25.1 0.6 pad_maximum_fusion.coef_ref
  25.7 0.0 copy-done.5
  25.7 0.2 slice_reduce_fusion
  25.9 1.1 %select_reduce_fusion.inv_ref = s32[1024]{0:T(1024)} fusion(s32[1024]{0:T(1024)S(1)} %add_select_fusion), kind=kLoop, calls=%fused_computation.2 | loop fusion | flops 3144704 | bytes 8192 | tf_op jit(solution)/shard_map/reduce_sum | solution.py:156
  27.0 20.3 %all-to-all-done = f32[128,8,4,128]{3,2,1,0:T(4,128)S(1)} async-done(((f32[128,8,4,128]{3,2,1,0:T(4,128)}), f32[128,8,4,128]{3,2,1,0:T(4,128)S(1)}, u32[]{:S(2)}, u32[]{:S(2)}) %all-to-all-start) | async-done | bytes 2097184 | tf_op jit(solution)/shard_map/all_to_all | solution.py:134
  47.4 0.0 copy-start.2
  47.4 1.3 %copy-done.2 = f32[128,8,4,128]{3,2,1,0:T(4,128)} copy-done((f32[128,8,4,128]{3,2,1,0:T(4,128)}, f32[128,8,4,128]{3,2,1,0:T(4,128)S(1)}, u32[]{:S(2)}) %copy-start.2) | copy-done | bytes 2097176
  48.7 12.1 %shard_map.104 = f32[1024,4,128]{2,1,0:T(4,128)} custom-call(s32[1024]{0:T(1024)} %select_reduce_fusion.inv_ref, s32[2]{0:T(128)} %pad_add_fusion.shift_ref, f32[12]{0:T(128)} %pad_maximum_fusion.coef_ref, f32[1024,4,128]{2,1,0:T(4,128)} %bitcast.29, f32[128,8,512]{2,1,0:T(8,128)} %bitcast.30), custom_call_target="tpu_custom_call" | custom-call | tf_op jit(solution)/shard_map/pallas_call | solution.py:112
  60.8 34.6 %all_to_all.10 = f32[128,8,4,128]{3,2,1,0:T(4,128)S(1)} all-to-all(f32[128,8,4,128]{3,2,1,0:T(4,128)} %bitcast.31), channel_id=1, replica_groups=mesh['pt'=8,'comp'=16] {'pt','comp'}, dimensions={0} | all-to-all | bytes 4194304 | tf_op jit(solution)/shard_map/all_to_all | solution.py:160
  95.4 0.2 copy.22
  95.6 1.8 %copy.27 = f32[64,8,8,128]{3,1,2,0:T(8,128)} copy(f32[64,8,8,128]{3,2,1,0:T(8,128)S(1)} %bitcast.34) | data formatting | bytes 4194304
  97.3 0.4 reduce_sum.29
  97.7 0.6 multiply_bitcast_fusion.1
  (8 shorter events, 0.1 us)
Async XLA Ops:
  0.6 17.0 %copy-start = (s32[512]{0:T(512)S(1)}, s32[512]{0:T(512)}, u32[]{:S(2)}) copy-start(s32[512]{0:T(512)} %param.14) | copy-start | bytes 6148
  0.6 2.2 %copy-start.3 = (f32[512,1024]{1,0:T(8,128)S(1)}, f32[512,1024]{1,0:T(8,128)}, u32[]{:S(2)}) copy-start(f32[512,1024]{1,0:T(8,128)} %param.9) | copy-start | bytes 6291460
  0.7 1.9 %copy-start.6 = (s32[1024]{0:T(1024)S(1)}, s32[1024]{0:T(1024)}, u32[]{:S(2)}) copy-start(s32[1024]{0:T(1024)} %param.15) | copy-start | bytes 12292
  0.7 2.2 %copy-start.7 = (f32[1024]{0:T(1024)S(1)}, f32[1024]{0:T(1024)}, u32[]{:S(2)}) copy-start(f32[1024]{0:T(1024)} %param.10) | copy-start | bytes 12292
  0.7 2.2 %copy-start.9 = (f32[512]{0:T(512)S(1)}, f32[512]{0:T(512)}, u32[]{:S(2)}) copy-start(f32[512]{0:T(512)} %param.11) | copy-start | bytes 6148
  0.7 2.2 %copy-start.8 = (f32[512]{0:T(512)S(1)}, f32[512]{0:T(512)}, u32[]{:S(2)}) copy-start(f32[512]{0:T(512)} %param.12) | copy-start | bytes 6148
  6.1 12.2 %copy-start.1 = (f32[16]{0:T(128)S(1)}, f32[16]{0:T(128)}, u32[]{:S(2)}) copy-start(f32[16]{0:T(128)} %param.13) | copy-start | bytes 196
  6.1 13.0 %copy-start.4 = (s32[256,512]{1,0:T(8,128)S(1)}, s32[256,512]{1,0:T(8,128)}, u32[]{:S(2)}) copy-start(s32[256,512]{1,0:T(8,128)} %param.17) | copy-start | bytes 1572868
  6.1 41.3 %all-to-all-start = ((f32[128,8,4,128]{3,2,1,0:T(4,128)}), f32[128,8,4,128]{3,2,1,0:T(4,128)S(1)}, u32[]{:S(2)}, u32[]{:S(2)}) async-start(f32[128,8,4,128]{3,2,1,0:T(4,128)} %bitcast.32), calls=%async_computation | async-start | bytes 4194304 | tf_op jit(solution)/shard_map/all_to_all | solution.py:134
  21.5 4.2 %copy-start.5 = (s32[131072]{0:T(1024)S(1)}, s32[131072]{0:T(1024)}, u32[]{:S(2)}) copy-start(s32[131072]{0:T(1024)} %param.16) | copy-start | bytes 1572868
  47.4 1.3 %copy-start.2 = (f32[128,8,4,128]{3,2,1,0:T(4,128)}, f32[128,8,4,128]{3,2,1,0:T(4,128)S(1)}, u32[]{:S(2)}) copy-start(f32[128,8,4,128]{3,2,1,0:T(4,128)S(1)} %all-to-all-done) | copy-start | bytes 6291460
